TPU v7x, 32 devices: a whole 2x2x4 slice. The times are simulated.
32 devices in a mesh: rep: 4 (over x, core), fsdp: 8 (over z, y).
Axes of the slice: x: 2, y: 2, z: 4, core: 2. Of those that a mesh axis runs over, the one named last changes fastest.
Arguments:
- tokens: bfloat16 [64, 512, 1024], P('rep', 'fsdp'), may hold values from -6 to 6
- cotangent: bfloat16 [64, 512, 1024], P('rep', 'fsdp'), may hold values from -6 to 6
- lengths: int32 [4, 16], P('rep'), may hold values from 1 to 512, as said below
- deal: int32 [4, 16], P('rep'), may hold values from 0 to 15, each once within a row
- norm_gain: bfloat16 [1024], P('fsdp'), may hold values from 0.099609375 to 1.8984375
- in_weight: bfloat16 [1024, 3072], P('fsdp'), may hold values from -0.1875 to 0.1875
- conv_weight: bfloat16 [1024, 3], P('fsdp'), may hold values from -3 to 3
- out_weight: bfloat16 [1024, 1024], P('fsdp'), may hold values from -0.1875 to 0.1875
- ffn_gain: bfloat16 [1024], P('fsdp'), may hold values from 0.099609375 to 1.8984375
- gate_weight: bfloat16 [1024, 4608], P('fsdp'), may hold values from -0.1875 to 0.1875
- up_weight: bfloat16 [1024, 4608], P('fsdp'), may hold values from -0.1875 to 0.1875
- down_weight: bfloat16 [4608, 1024], P('fsdp'), may hold values from -0.1875 to 0.1875
Outputs:
- block_out: bfloat16 [64, 512, 1024], P('rep', 'fsdp')
- block_grad: bfloat16 [64, 512, 1024], P('rep', 'fsdp')
- norm_gain_grad: float32 [1024], P('fsdp')
- in_grad: float32 [1024, 3072], P('fsdp')
- conv_grad: float32 [1024, 3], P('fsdp')
- out_grad: float32 [1024, 1024], P('fsdp')
- ffn_gain_grad: float32 [1024], P('fsdp')
- gate_grad: float32 [1024, 4608], P('fsdp')
- up_grad: float32 [1024, 4608], P('fsdp')
- down_grad: float32 [4608, 1024], P('fsdp')
Inputs may be any that keep to these rules, and one draw needn't show every extreme that they name: In each row, the 2 lengths of slots 2 i to 2 i + 1 sum to at most 768; in each row one such set sums to exactly 768 and holds a length of exactly 512. `deal`: each row is a permutation of the group's sequence numbers.
All inputs are finite; a program needn't handle non-finite values.
Results may differ from a plain program's by a relative error of at most 0.018.
Values may be sent and summed in bfloat16 or wider, within the bound.
A program may use at most 256 MiB of HBM per device.

v0:
```python
import jax
import jax.numpy as jnp
from jax import lax
from jax.sharding import PartitionSpec as P

SLOT = 512
CAP_DEV = 768


EPS = 1e-05


def row_scale(values):
    return lax.rsqrt(jnp.mean(values * values, axis=-1, keepdims=True) + EPS)


def norm_back(grad_unit, unit_rows, scale_rows):
    return scale_rows * (
        grad_unit - unit_rows * jnp.mean(grad_unit * unit_rows, axis=-1, keepdims=True)
    )


def lag_rows(values, amount):
    return jnp.pad(values, ((amount, 0), (0, 0)))[: values.shape[0]]


def lead_rows(values, amount):
    return jnp.pad(values, ((0, amount), (0, 0)))[amount:]


def over_rows(left_side, right_side):
    return lax.dot_general(
        left_side, right_side, (((0,), (0,)), ((), ())), preferred_element_type=jnp.float32
    )


def over_cols(left_side, right_side):
    return lax.dot_general(
        left_side, right_side, (((1,), (1,)), ((), ())), preferred_element_type=jnp.float32
    )


def pack_tables(lengths):
    group_len = lengths[0]
    seq_dev = group_len.shape[0] // lax.axis_size("fsdp")
    own_len = lax.dynamic_slice_in_dim(group_len, lax.axis_index("fsdp") * seq_dev, seq_dev)
    seq_ends = jnp.cumsum(own_len)
    starts = seq_ends - own_len
    total_len = seq_ends[seq_dev - 1]
    slot_ids = jnp.arange(seq_dev, dtype=jnp.int32)
    row_ids = jnp.arange(CAP_DEV, dtype=jnp.int32)
    which_seq = jnp.minimum(
        jnp.sum((row_ids[:, None] >= seq_ends[None, :]).astype(jnp.int32), axis=1), seq_dev - 1
    )
    row_start = jnp.sum(
        jnp.where(which_seq[:, None] == slot_ids[None, :], starts[None, :], 0), axis=1
    )
    row_live = row_ids < total_len
    position = jnp.where(row_live, row_ids - row_start, 0)
    source = jnp.where(row_live, which_seq * SLOT + position, 0)
    lag_masks = (
        (position >= 1).astype(jnp.float32)[:, None],
        (position >= 2).astype(jnp.float32)[:, None],
    )
    cell_ids = jnp.arange(seq_dev * SLOT, dtype=jnp.int32)
    cell_pick = (cell_ids // SLOT)[:, None] == slot_ids[None, :]
    cell_pos = cell_ids % SLOT
    cell_len = jnp.sum(jnp.where(cell_pick, own_len[None, :], 0), axis=1)
    cell_start = jnp.sum(jnp.where(cell_pick, starts[None, :], 0), axis=1)
    cell_live = cell_pos < cell_len
    back_index = jnp.where(cell_live, cell_start + cell_pos, 0)
    return (source, row_live, lag_masks, back_index, cell_live)


def to_rows(slot_values, source):
    width = slot_values.shape[2]
    return jnp.take(slot_values.reshape(-1, width), source, axis=0).astype(jnp.float32)


def to_slots(packed_rows, back_index, cell_live, seq_dev):
    cells = jnp.where(cell_live[:, None], jnp.take(packed_rows, back_index, axis=0), 0.0)
    return cells.astype(jnp.bfloat16).reshape(seq_dev, SLOT, packed_rows.shape[1])


def to_sources(received, deal_row):
    slot_ids = jnp.arange(deal_row.shape[0], dtype=jnp.int32)
    inverse = jnp.sum(
        jnp.where(deal_row[None, :] == slot_ids[:, None], slot_ids[None, :], 0), axis=1
    )
    return jnp.take(received, inverse, axis=0)


def forward_pass(token_rows, mix_set, ffn_set, lag_masks):
    norm_gain, in_weight, conv_weight, out_weight = mix_set
    ffn_gain, gate_weight, up_weight, down_weight = ffn_set
    width = in_weight.shape[0]
    scale_one = row_scale(token_rows)
    unit_one = token_rows * scale_one
    normed_one = (unit_one * norm_gain.astype(jnp.float32)).astype(jnp.bfloat16)
    projected = jnp.dot(normed_one, in_weight, preferred_element_type=jnp.float32)
    b_gate = projected[:, :width]
    c_gate = projected[:, width : 2 * width]
    x_value = projected[:, 2 * width :]
    product = b_gate * x_value
    lag_one = lag_rows(product, 1) * lag_masks[0]
    lag_two = lag_rows(product, 2) * lag_masks[1]
    taps = conv_weight.astype(jnp.float32)
    convolved = taps[:, 0] * lag_two + taps[:, 1] * lag_one + taps[:, 2] * product
    gated = (c_gate * convolved).astype(jnp.bfloat16)
    middle = token_rows + jnp.dot(gated, out_weight, preferred_element_type=jnp.float32)
    scale_two = row_scale(middle)
    unit_two = middle * scale_two
    normed_two = (unit_two * ffn_gain.astype(jnp.float32)).astype(jnp.bfloat16)
    gate_lin = jnp.dot(normed_two, gate_weight, preferred_element_type=jnp.float32)
    up_lin = jnp.dot(normed_two, up_weight, preferred_element_type=jnp.float32)
    hidden = (jax.nn.silu(gate_lin) * up_lin).astype(jnp.bfloat16)
    output = middle + jnp.dot(hidden, down_weight, preferred_element_type=jnp.float32)
    return (
        scale_one,
        unit_one,
        normed_one,
        b_gate,
        c_gate,
        x_value,
        product,
        lag_one,
        lag_two,
        convolved,
        gated,
        scale_two,
        unit_two,
        normed_two,
        gate_lin,
        up_lin,
        hidden,
        output,
    )


def backward_pass(saved, mix_set, ffn_set, lag_masks, grad_out):
    (
        scale_one,
        unit_one,
        normed_one,
        b_gate,
        c_gate,
        x_value,
        product,
        lag_one,
        lag_two,
        convolved,
        gated,
        scale_two,
        unit_two,
        normed_two,
        gate_lin,
        up_lin,
        hidden,
        output,
    ) = saved
    norm_gain, in_weight, conv_weight, out_weight = mix_set
    ffn_gain, gate_weight, up_weight, down_weight = ffn_set
    grad_ffn = grad_out.astype(jnp.bfloat16)
    down_grad = over_rows(hidden, grad_ffn)
    grad_hidden = over_cols(grad_ffn, down_weight)
    sigma = jax.nn.sigmoid(gate_lin)
    grad_gate = (grad_hidden * up_lin * sigma * (1.0 + gate_lin * (1.0 - sigma))).astype(
        jnp.bfloat16
    )
    grad_up = (grad_hidden * gate_lin * sigma).astype(jnp.bfloat16)
    gate_grad = over_rows(normed_two, grad_gate)
    up_grad = over_rows(normed_two, grad_up)
    grad_normed_two = over_cols(grad_gate, gate_weight) + over_cols(grad_up, up_weight)
    ffn_gain_grad = jnp.sum(grad_normed_two * unit_two, axis=0)
    grad_middle = grad_out + norm_back(
        grad_normed_two * ffn_gain.astype(jnp.float32), unit_two, scale_two
    )
    grad_mixed = grad_middle.astype(jnp.bfloat16)
    out_grad = over_rows(gated, grad_mixed)
    grad_gated = over_cols(grad_mixed, out_weight)
    grad_c = grad_gated * convolved
    grad_conv = grad_gated * c_gate
    conv_grad = jnp.stack(
        [
            jnp.sum(grad_conv * lag_two, axis=0),
            jnp.sum(grad_conv * lag_one, axis=0),
            jnp.sum(grad_conv * product, axis=0),
        ],
        axis=1,
    )
    taps = conv_weight.astype(jnp.float32)
    grad_product = (
        taps[:, 2] * grad_conv
        + taps[:, 1] * lead_rows(grad_conv * lag_masks[0], 1)
        + taps[:, 0] * lead_rows(grad_conv * lag_masks[1], 2)
    )
    grad_projected = jnp.concatenate(
        [grad_product * x_value, grad_c, grad_product * b_gate], axis=1
    ).astype(jnp.bfloat16)
    in_grad = over_rows(normed_one, grad_projected)
    grad_normed_one = over_cols(grad_projected, in_weight)
    norm_gain_grad = jnp.sum(grad_normed_one * unit_one, axis=0)
    grad_tokens = grad_middle + norm_back(
        grad_normed_one * norm_gain.astype(jnp.float32), unit_one, scale_one
    )
    return (
        grad_tokens,
        (
            norm_gain_grad,
            in_grad,
            conv_grad,
            out_grad,
            ffn_gain_grad,
            gate_grad,
            up_grad,
            down_grad,
        ),
    )


def body(
    tokens,
    cotangent,
    lengths,
    deal,
    norm_gain,
    in_weight,
    conv_weight,
    out_weight,
    ffn_gain,
    gate_weight,
    up_weight,
    down_weight,
):
    source, row_live, lag_masks, back_index, cell_live = pack_tables(lengths)
    seq_dev = deal.shape[1] // lax.axis_size("fsdp")
    deal_row = deal[0]
    sent_tokens = jnp.take(tokens, deal_row, axis=0)
    sent_cot = jnp.take(cotangent, deal_row, axis=0)
    slot_tokens, slot_cot = (
        lax.all_to_all(sent_tokens, "fsdp", split_axis=0, concat_axis=1, tiled=True),
        lax.all_to_all(sent_cot, "fsdp", split_axis=0, concat_axis=1, tiled=True),
    )
    token_rows = to_rows(slot_tokens, source)
    cot_rows = jnp.where(row_live[:, None], to_rows(slot_cot, source), 0.0)
    mix_set = (
        lax.all_gather(norm_gain, "fsdp", axis=0, tiled=True),
        lax.all_gather(in_weight, "fsdp", axis=0, tiled=True),
        lax.all_gather(conv_weight, "fsdp", axis=0, tiled=True),
        lax.all_gather(out_weight, "fsdp", axis=0, tiled=True),
    )
    ffn_set = (
        lax.all_gather(ffn_gain, "fsdp", axis=0, tiled=True),
        lax.all_gather(gate_weight, "fsdp", axis=0, tiled=True),
        lax.all_gather(up_weight, "fsdp", axis=0, tiled=True),
        lax.all_gather(down_weight, "fsdp", axis=0, tiled=True),
    )
    saved = forward_pass(token_rows, mix_set, ffn_set, lag_masks)
    out_slots = to_slots(saved[-1], back_index, cell_live, seq_dev)
    out_back = lax.all_to_all(out_slots, "fsdp", split_axis=1, concat_axis=0, tiled=True)
    block_out = to_sources(out_back, deal_row)
    again_slots = lax.all_to_all(sent_tokens, "fsdp", split_axis=0, concat_axis=1, tiled=True)
    again_rows = to_rows(again_slots, source)
    mix_back = (
        lax.all_gather(norm_gain, "fsdp", axis=0, tiled=True),
        lax.all_gather(in_weight, "fsdp", axis=0, tiled=True),
        lax.all_gather(conv_weight, "fsdp", axis=0, tiled=True),
        lax.all_gather(out_weight, "fsdp", axis=0, tiled=True),
    )
    ffn_back = (
        lax.all_gather(ffn_gain, "fsdp", axis=0, tiled=True),
        lax.all_gather(gate_weight, "fsdp", axis=0, tiled=True),
        lax.all_gather(up_weight, "fsdp", axis=0, tiled=True),
        lax.all_gather(down_weight, "fsdp", axis=0, tiled=True),
    )
    saved_back = forward_pass(again_rows, mix_back, ffn_back, lag_masks)
    grad_rows, weight_grads = backward_pass(saved_back, mix_back, ffn_back, lag_masks, cot_rows)
    grad_slots = to_slots(grad_rows, back_index, cell_live, seq_dev)
    grad_back = lax.all_to_all(grad_slots, "fsdp", split_axis=1, concat_axis=0, tiled=True)
    block_grad = to_sources(grad_back, deal_row)
    shares = (
        lax.psum_scatter(
            weight_grads[0].astype(jnp.bfloat16), "fsdp", scatter_dimension=0, tiled=True
        ).astype(jnp.float32),
        lax.psum_scatter(
            weight_grads[1].astype(jnp.bfloat16), "fsdp", scatter_dimension=0, tiled=True
        ).astype(jnp.float32),
        lax.psum_scatter(
            weight_grads[2].astype(jnp.bfloat16), "fsdp", scatter_dimension=0, tiled=True
        ).astype(jnp.float32),
        lax.psum_scatter(
            weight_grads[3].astype(jnp.bfloat16), "fsdp", scatter_dimension=0, tiled=True
        ).astype(jnp.float32),
        lax.psum_scatter(
            weight_grads[4].astype(jnp.bfloat16), "fsdp", scatter_dimension=0, tiled=True
        ).astype(jnp.float32),
        lax.psum_scatter(
            weight_grads[5].astype(jnp.bfloat16), "fsdp", scatter_dimension=0, tiled=True
        ).astype(jnp.float32),
        lax.psum_scatter(
            weight_grads[6].astype(jnp.bfloat16), "fsdp", scatter_dimension=0, tiled=True
        ).astype(jnp.float32),
        lax.psum_scatter(
            weight_grads[7].astype(jnp.bfloat16), "fsdp", scatter_dimension=0, tiled=True
        ).astype(jnp.float32),
    )
    summed = (
        lax.psum(shares[0].astype(jnp.bfloat16), "rep").astype(jnp.float32),
        lax.psum(shares[1].astype(jnp.bfloat16), "rep").astype(jnp.float32),
        lax.psum(shares[2].astype(jnp.bfloat16), "rep").astype(jnp.float32),
        lax.psum(shares[3].astype(jnp.bfloat16), "rep").astype(jnp.float32),
        lax.psum(shares[4].astype(jnp.bfloat16), "rep").astype(jnp.float32),
        lax.psum(shares[5].astype(jnp.bfloat16), "rep").astype(jnp.float32),
        lax.psum(shares[6].astype(jnp.bfloat16), "rep").astype(jnp.float32),
        lax.psum(shares[7].astype(jnp.bfloat16), "rep").astype(jnp.float32),
    )
    return (
        block_out,
        block_grad,
        summed[0],
        summed[1],
        summed[2],
        summed[3],
        summed[4],
        summed[5],
        summed[6],
        summed[7],
    )


def solution(mesh):
    placed = (
        P("rep", "fsdp", None),
        P("rep", "fsdp", None),
        P("rep", None),
        P("rep", None),
        P("fsdp"),
        P("fsdp", None),
        P("fsdp", None),
        P("fsdp", None),
        P("fsdp"),
        P("fsdp", None),
        P("fsdp", None),
        P("fsdp", None),
    )
    return jax.shard_map(
        body,
        mesh=mesh,
        in_specs=placed,
        out_specs=(
            P("rep", "fsdp", None),
            P("rep", "fsdp", None),
            P("fsdp"),
            P("fsdp", None),
            P("fsdp", None),
            P("fsdp", None),
            P("fsdp"),
            P("fsdp", None),
            P("fsdp", None),
            P("fsdp", None),
        ),
        check_vma=False,
    )
```

profile of v0, /device:TPU:0, one launch (start us, length us, event | category | flops | bytes accessed | tf_op | source)
XLA Modules:
  0.0 1630.6 jit_solution(14455915364186069048)
XLA Ops:
  19.7 92.7 %all_to_all.71 = bf16[16,64,1024]{2,1,0:T(8,128)(2,1)} all-to-all(bf16[16,64,1024]{2,1,0:T(8,128)(2,1)S(1)} %get-tuple-element.59), channel_id=1, replica_groups=mesh['rep'=4,'fsdp'=8] {'fsdp'}, dimensions={0} | all-to-all | bytes 4194304 | tf_op jit(solution)/shard_map/all_to_all | solution.py:241
  119.0 68.1 %all-gather = bf16[8,1,128]{2,1,0:T(2,128)(2,1)S(1)} all-gather(bf16[1,1,128]{2,1,0:T(2,128)(2,1)S(1)} %bitcast.88), channel_id=1, replica_groups=mesh['rep'=4,'fsdp'=8] {'fsdp'}, dimensions={0}, use_global_device_ids=true | all-gather | bytes 2304 | tf_op jit(solution)/shard_map/all_gather | solution.py:247
  187.1 30.4 %all-gather.1 = bf16[8,1,128]{2,1,0:T(2,128)(2,1)S(1)} all-gather(bf16[1,1,128]{2,1,0:T(2,128)(2,1)S(1)} %bitcast.89), channel_id=1, replica_groups=mesh['rep'=4,'fsdp'=8] {'fsdp'}, dimensions={0}, use_global_device_ids=true | all-gather | bytes 2304 | tf_op jit(solution)/shard_map/all_gather | solution.py:253
  217.5 16.5 %all_gather.34 = bf16[1024,3]{0,1:T(4,128)(2,1)S(1)} all-gather(bf16[128,3]{0,1:T(4,128)(2,1)S(1)} %copy-done.28), channel_id=1, replica_groups=mesh['rep'=4,'fsdp'=8] {'fsdp'}, dimensions={0}, use_global_device_ids=true | all-gather | bytes 6912 | tf_op jit(solution)/shard_map/all_gather | solution.py:249
  244.2 6.6 gather_fusion.5
  251.4 7.5 fusion.25
  273.8 100.0 %all-gather.12.cloned.1.call-done = bf16[1024,4608]{1,0:T(8,128)(2,1)} async-done(((bf16[128,4608]{1,0:T(8,128)(2,1)}), bf16[1024,4608]{1,0:T(8,128)(2,1)}) %all-gather.12.cloned.1.call-update) | async-done | bytes 9437200 | tf_op jit(solution)/shard_map/all_gather | solution.py:254
  373.8 13.4 fusion.46
  387.1 125.0 %all-gather.14.cloned.1.call-done = bf16[1024,4608]{1,0:T(8,128)(2,1)} async-done(((bf16[128,4608]{1,0:T(8,128)(2,1)}), bf16[1024,4608]{1,0:T(8,128)(2,1)}) %all-gather.14.cloned.1.call-update) | async-done | bytes 9437200 | tf_op jit(solution)/shard_map/all_gather | solution.py:255
  512.1 13.7 fusion.47
  525.7 124.7 %all-gather.16.cloned.1.call-done = bf16[4608,1024]{1,0:T(8,128)(2,1)} async-done(((bf16[576,1024]{1,0:T(8,128)(2,1)}), bf16[4608,1024]{1,0:T(8,128)(2,1)}) %all-gather.16.cloned.1.call-update) | async-done | bytes 9437200 | tf_op jit(solution)/shard_map/all_gather | solution.py:256
  650.4 28.2 %multiply_convert_fusion = (bf16[768,4608]{1,0:T(8,128)(2,1)}, bf16[768,4608]{1,0:T(8,128)(2,1)}, bf16[768,4608]{1,0:T(8,128)(2,1)}) fusion(f32[768,4608]{1,0:T(8,128)} %fusion.46, f32[768,4608]{1,0:T(8,128)} %fusion.47, bf16[4608,1024]{1,0:T(8,128)(2,1)} %all-gather.16.cloned.1.call-done, pred[768]{0:T(1024)(128)(4,1)S(1)} %iota_compare_fusion.2, ...), kind=kOutput, calls=%fused_computation.8 | convolution fusion | flops 7307526144 | bytes 60556800 | tf_op jit(solution)/shard_map/dot_general | solution.py:38
  678.6 13.5 fusion.48
  692.1 11.2 multiply_reduce_fusion
  710.1 10.1 multiply_reduce_fusion.3
  728.6 8.2 convolution_convert_fusion.3
  738.2 13.2 convolution_convert_fusion.2
  751.5 12.9 convolution_convert_fusion.1
  765.9 13.5 convolution_convert_fusion
  780.1 12.6 convolution_add_fusion.1
  792.7 5.3 gather_fusion.2
  798.1 10.0 fusion.17
  809.5 5.3 gather_fusion.6
  829.5 54.8 %all-to-all-done.1 = bf16[2,512,1024]{2,0,1:T(2,128)(2,1)} async-done(((bf16[2,512,1024]{2,0,1:T(2,128)(2,1)}), bf16[2,512,1024]{2,0,1:T(2,128)(2,1)}, u32[]{:S(2)}, u32[]{:S(2)}) %all-to-all-start.1) | async-done | bytes 2097184 | tf_op jit(solution)/shard_map/all_to_all | solution.py:260
  889.1 70.7 %reduce-scatter.9.cloned.1.call-done = bf16[128,3072]{1,0:T(8,128)(2,1)} async-done(((bf16[1024,3072]{1,0:T(8,128)(2,1)}), bf16[128,3072]{1,0:T(8,128)(2,1)}) %reduce-scatter.9.cloned.1.call-update) | async-done | bytes 786448 | tf_op jit(solution)/shard_map/reduce_scatter | solution.py:285
  959.8 164.2 %reduce-scatter.13.cloned.1.call-done = bf16[128,4608]{1,0:T(8,128)(2,1)} async-done(((bf16[1024,4608]{1,0:T(8,128)(2,1)}), bf16[128,4608]{1,0:T(8,128)(2,1)}) %reduce-scatter.13.cloned.1.call-update) | async-done | bytes 1179664 | tf_op jit(solution)/shard_map/reduce_scatter | solution.py:297
  1124.0 166.2 %reduce-scatter.15.cloned.1.call-done = bf16[128,4608]{1,0:T(8,128)(2,1)} async-done(((bf16[1024,4608]{1,0:T(8,128)(2,1)}), bf16[128,4608]{1,0:T(8,128)(2,1)}) %reduce-scatter.15.cloned.1.call-update) | async-done | bytes 1179664 | tf_op jit(solution)/shard_map/reduce_scatter | solution.py:300
  1290.2 166.0 %reduce-scatter.17.cloned.1.call-done = bf16[576,1024]{1,0:T(8,128)(2,1)} async-done(((bf16[4608,1024]{1,0:T(8,128)(2,1)}), bf16[576,1024]{1,0:T(8,128)(2,1)}) %reduce-scatter.17.cloned.1.call-update) | async-done | bytes 1179664 | tf_op jit(solution)/shard_map/reduce_scatter | solution.py:303
  1457.6 19.5 %all-reduce.6 = (bf16[1024]{0:T(1024)(128)(2,1)S(1)}, bf16[1024]{0:T(1024)(128)(2,1)S(1)}) all-reduce(bf16[1024]{0:T(1024)(128)(2,1)S(1)} %get-tuple-element.18, bf16[1024]{0:T(1024)(128)(2,1)S(1)} %get-tuple-element.13), channel_id=2, replica_groups=mesh['rep'=4,'fsdp'=8] {'fsdp'}, use_global_device_ids=true, to_apply=%region_11.15.clone | all-reduce | flops 2048 | bytes 8192
  1477.2 43.3 %reduce-scatter.19.cloned.1.call-done = bf16[128,3]{1,0:T(8,128)(2,1)} async-done(((bf16[1024,3]{1,0:T(8,128)(2,1)}), bf16[128,3]{1,0:T(8,128)(2,1)}) %reduce-scatter.19.cloned.1.call-update) | async-done | bytes 784
  1521.3 5.7 all-reduce.7
  1545.1 69.7 %all-reduce.11.cloned.1.call-done = (bf16[128,3072]{1,0:T(8,128)(2,1)}, bf16[128,1024]{1,0:T(8,128)(2,1)}, bf16[128,4608]{1,0:T(8,128)(2,1)}, bf16[128,4608]{1,0:T(8,128)(2,1)}, bf16[576,1024]{1,0:T(8,128)(2,1)}) async-done(((bf16[128,3072]{1,0:T(8,128)(2,1)}, bf16[128,1024]{1,0:T(8,128)(2,1)}, bf16[128,4608]{1,0:T(8,128)(2,1)}, bf16[128,4608]{1,0:T(8,128)(2,1)}, bf16[576,1024]{1,0:T(8,128)(2,1)}), ...) | async-done | bytes 4587536 | tf_op jit(solution)/shard_map/psum | solution.py:309
  (174 shorter events, 112.1 us)
Async XLA Ops:
  7.2 244.2 %all-gather.8.cloned.1.call-start = ((), (), s32[]{:S(2)}) async-start(), calls=%async_computation.10 | async-start | bytes 7077888 | tf_op jit(solution)/shard_map/all_gather | solution.py:248
  7.9 258.6 %all-gather.10.cloned.1.call-start = ((), (), s32[]{:S(2)}) async-start(), calls=%async_computation.11 | async-start | bytes 2359296 | tf_op jit(solution)/shard_map/all_gather | solution.py:250
  8.7 365.1 %all-gather.12.cloned.1.call-start = ((), (), s32[]{:S(2)}) async-start(), calls=%async_computation.12 | async-start | bytes 10616832 | tf_op jit(solution)/shard_map/all_gather | solution.py:254
  9.4 502.7 %all-gather.14.cloned.1.call-start = ((), (), s32[]{:S(2)}) async-start(), calls=%async_computation.13 | async-start | bytes 10616832 | tf_op jit(solution)/shard_map/all_gather | solution.py:255
  10.0 640.4 %all-gather.16.cloned.1.call-start = ((), (), s32[]{:S(2)}) async-start(), calls=%async_computation.14 | async-start | bytes 10616832 | tf_op jit(solution)/shard_map/all_gather | solution.py:256
  12.6 3.8 copy-start.12
  112.4 5.2 copy-start.26
  112.5 6.5 copy-start.29
  112.5 74.6 %copy-start.30 = (bf16[128]{0:T(256)(128)(2,1)S(1)}, bf16[128]{0:T(256)(128)(2,1)}, u32[]{:S(2)}) copy-start(bf16[128]{0:T(256)(128)(2,1)} %param.26) | copy-start | bytes 772
  112.5 105.1 %copy-start.28 = (bf16[128,3]{0,1:T(4,128)(2,1)S(1)}, bf16[128,3]{0,1:T(4,128)(2,1)}, u32[]{:S(2)}) copy-start(bf16[128,3]{0,1:T(4,128)(2,1)} %param.24) | copy-start | bytes 2308
  112.5 125.0 %all-to-all-start.2 = ((bf16[16,64,1024]{2,1,0:T(8,128)(2,1)}), bf16[16,64,1024]{2,1,0:T(8,128)(2,1)}, u32[]{:S(2)}, u32[]{:S(2)}) async-start(bf16[16,64,1024]{2,1,0:T(8,128)(2,1)} %get-tuple-element.58), calls=%async_computation.2 | async-start | bytes 4194304 | tf_op jit(solution)/shard_map/all_to_all | solution.py:242
  117.6 771.5 %reduce-scatter.11.cloned.1.call-start = ((), (), s32[]{:S(2)}) async-start(), calls=%async_computation.16 | async-start | bytes 2359296 | tf_op jit(solution)/shard_map/reduce_scatter | solution.py:291
  244.2 6.6 copy-start.6
  678.6 13.5 copy-start.9
  678.6 13.5 copy-start.34
  692.1 11.3 copy-start.13
  710.0 249.8 %reduce-scatter.9.cloned.1.call-start = ((), (), s32[]{:S(2)}) async-start(), calls=%async_computation.15 | async-start | bytes 7077888 | tf_op jit(solution)/shard_map/reduce_scatter | solution.py:285
  720.2 7.3 copy-start.19
  736.8 387.2 %reduce-scatter.13.cloned.1.call-start = ((), (), s32[]{:S(2)}) async-start(), calls=%async_computation.17 | async-start | bytes 10616832 | tf_op jit(solution)/shard_map/reduce_scatter | solution.py:297
  751.5 538.7 %reduce-scatter.15.cloned.1.call-start = ((), (), s32[]{:S(2)}) async-start(), calls=%async_computation.18 | async-start | bytes 10616832 | tf_op jit(solution)/shard_map/reduce_scatter | solution.py:300
  764.5 691.7 %reduce-scatter.17.cloned.1.call-start = ((), (), s32[]{:S(2)}) async-start(), calls=%async_computation.19 | async-start | bytes 10616832 | tf_op jit(solution)/shard_map/reduce_scatter | solution.py:303
  798.1 10.0 copy-start.4
  798.1 10.0 copy-start.7
  821.7 62.7 %all-to-all-start.1 = ((bf16[2,512,1024]{2,0,1:T(2,128)(2,1)}), bf16[2,512,1024]{2,0,1:T(2,128)(2,1)}, u32[]{:S(2)}, u32[]{:S(2)}) async-start(bf16[2,512,1024]{2,0,1:T(2,128)(2,1)} %copy.39), calls=%async_computation.1 | async-start | bytes 4194304 | tf_op jit(solution)/shard_map/all_to_all | solution.py:260
  884.4 647.9 %all-to-all-start.3 = ((bf16[2,512,1024]{2,0,1:T(2,128)(2,1)}), bf16[2,512,1024]{2,0,1:T(2,128)(2,1)S(1)}, u32[]{:S(2)}, u32[]{:S(2)}) async-start(bf16[2,512,1024]{2,0,1:T(2,128)(2,1)} %copy.43), calls=%async_computation.3 | async-start | bytes 4194304 | tf_op jit(solution)/shard_map/all_to_all | solution.py:279
  888.0 568.2 %copy-start.33 = (u32[32]{0:T(128)S(1)}, u32[32]{0:T(128)}, u32[]{:S(2)}) copy-start(u32[32]{0:T(128)} %constant.108) | copy-start | bytes 388
  888.0 569.4 %copy-start.32 = (s32[1,16]{1,0:T(1,128)S(1)}, s32[1,16]{1,0:T(1,128)}, u32[]{:S(2)}) copy-start(s32[1,16]{1,0:T(1,128)} %param.21) | copy-start | bytes 196
  888.0 632.5 %reduce-scatter.19.cloned.1.call-start = ((), (), s32[]{:S(2)}) async-start(), calls=%async_computation.20 | async-start | bytes 294912
  889.0 725.7 %all-reduce.11.cloned.1.call-start = ((), (), s32[]{:S(2)}) async-start(), calls=%async_computation.21 | async-start | bytes 9175040 | tf_op jit(solution)/shard_map/psum | solution.py:309
  1537.3 3.7 copy-start.11
  1614.8 4.7 copy-start.20
  1619.5 3.8 copy-start.1
  (18 other events, 41.9 us)
Sparse Core Ops, SparseCore 0:
  10.2 174.4 all-gather.7
  186.8 48.0 all-gather.9
  237.1 136.5 all-gather.11
  375.8 136.2 all-gather.13
  514.1 136.2 all-gather.15
  710.1 65.9 reduce-scatter.10
  779.7 180.0 reduce-scatter.8
  963.4 160.5 reduce-scatter.12
  1127.6 162.5 reduce-scatter.14
  1293.6 162.5 reduce-scatter.16
  1460.1 60.3 reduce-scatter.18
  1523.1 91.6 all-reduce.10
where the time goes:
time: 1640 us; the launch traced here: 1630 us
  waiting for transfers between devices  1090 us (66%)
  blocking collectives  233 us (14%)
  matrix products  175 us (11%)
  local copies, waits for them, and re-layouts  66 us (4%)
  other arithmetic  39.3 us (2%)
    reduce_scatter x1, waiting for transfers between devices, body(): lax.psum_scatter(weight_grads[6].astype(jnp.bfloat16), 'fsdp', scatter_di...  166 us
    reduce_scatter x1, waiting for transfers between devices, body(): lax.psum_scatter(weight_grads[7].astype(jnp.bfloat16), 'fsdp', scatter_di...  166 us
    reduce_scatter x1, waiting for transfers between devices, body(): lax.psum_scatter(weight_grads[5].astype(jnp.bfloat16), 'fsdp', scatter_di...  164 us
    all_gather x1, waiting for transfers between devices, body(): lax.all_gather(up_weight, 'fsdp', axis=0, tiled=True)  125 us
    all_gather x1, waiting for transfers between devices, body(): lax.all_gather(down_weight, 'fsdp', axis=0, tiled=True)  125 us
    all_gather x1, waiting for transfers between devices, body(): lax.all_gather(gate_weight, 'fsdp', axis=0, tiled=True)  100 us
    all_to_all x1, blocking collectives, body(): lax.all_to_all(sent_tokens, 'fsdp', split_axis=0, concat_axis=1, tiled=True)  92.7 us
    dot_general x5, matrix products, over_cols(): lax.dot_general(left_side, right_side, (((1,), (1,)), ((), ())), preferre...  73 us
  transfers between devices with their start and end apart: 15, of which 10 were waited for; matrix products, arithmetic and copies ran while one was open for 12% of the time, Pallas kernels for 0%

commit v1 on v0

v1 whole, which is shorter than its diff:
```python
import jax
import jax.numpy as jnp
from jax import lax
from jax.sharding import PartitionSpec as P

EPS = 1e-05
F32 = jnp.float32
BF16 = jnp.bfloat16


def row_scale(values):
    return lax.rsqrt(jnp.mean(values * values, axis=-1, keepdims=True) + EPS)


def norm_back(grad_unit, unit_rows, scale_rows):
    return scale_rows * (
        grad_unit - unit_rows * jnp.mean(grad_unit * unit_rows, axis=-1, keepdims=True)
    )


def over_rows(left_side, right_side):
    return lax.dot_general(
        left_side, right_side, (((0,), (0,)), ((), ())), preferred_element_type=F32
    )


def over_cols(left_side, right_side):
    return lax.dot_general(
        left_side, right_side, (((1,), (1,)), ((), ())), preferred_element_type=F32
    )


def dot(left_side, right_side):
    return jnp.dot(left_side, right_side, preferred_element_type=F32)


def live_mask(lengths, deal, span):
    slots = jnp.arange(deal.shape[1], dtype=jnp.int32)
    picked = deal[0][:, None] == slots[None, :]
    source_len = jnp.sum(jnp.where(picked, lengths[0][:, None], 0), axis=0)
    position = lax.axis_index("fsdp") * span + jnp.arange(span, dtype=jnp.int32)
    return (position[None, :] < source_len[:, None]).astype(F32)[..., None]


def shift(values, amount):
    size = lax.axis_size("fsdp")
    pairs = [(i, i + amount) for i in range(size) if 0 <= i + amount < size]
    return lax.ppermute(values, "fsdp", pairs)


def body(
    tokens,
    cotangent,
    lengths,
    deal,
    norm_gain,
    in_weight,
    conv_weight,
    out_weight,
    ffn_gain,
    gate_weight,
    up_weight,
    down_weight,
):
    seqs, span, width = tokens.shape
    live = live_mask(lengths, deal, span)
    halo = shift(tokens[:, span - 2 :], 1)

    def gather(values):
        return lax.all_gather(values, "fsdp", axis=0, tiled=True)

    norm_gain, in_weight, conv_weight, out_weight = map(
        gather, (norm_gain, in_weight, conv_weight, out_weight)
    )
    ffn_gain, gate_weight, up_weight, down_weight = map(
        gather, (ffn_gain, gate_weight, up_weight, down_weight)
    )
    gain_one = norm_gain.astype(F32)
    gain_two = ffn_gain.astype(F32)
    taps = conv_weight.astype(F32)
    extended = jnp.concatenate([halo, tokens], axis=1).astype(F32)
    scale_ext = row_scale(extended)
    unit_ext = extended * scale_ext
    normed_ext = (unit_ext * gain_one).astype(BF16)
    projected = dot(normed_ext.reshape(-1, width), in_weight).reshape(seqs, span + 2, 3 * width)
    b_gate = projected[:, :, :width]
    c_gate = projected[:, 2:, width : 2 * width]
    x_value = projected[:, :, 2 * width :]
    product = b_gate * x_value
    lags = (product[:, :span], product[:, 1 : span + 1], product[:, 2:])
    convolved = taps[:, 0] * lags[0] + taps[:, 1] * lags[1] + taps[:, 2] * lags[2]
    gated = (c_gate * convolved).astype(BF16).reshape(-1, width)
    token_rows = tokens.astype(F32).reshape(-1, width)
    middle = token_rows + dot(gated, out_weight)
    scale_two = row_scale(middle)
    unit_two = middle * scale_two
    normed_two = (unit_two * gain_two).astype(BF16)
    grad_out = (cotangent.astype(F32) * live).reshape(-1, width)
    grad_ffn = grad_out.astype(BF16)
    gate_lin = dot(normed_two, gate_weight)
    up_lin = dot(normed_two, up_weight)
    sigma = jax.nn.sigmoid(gate_lin)
    hidden = (gate_lin * sigma * up_lin).astype(BF16)
    output = middle + dot(hidden, down_weight)
    down_grad = over_rows(hidden, grad_ffn)
    grad_hidden = over_cols(grad_ffn, down_weight)
    grad_gate = (grad_hidden * up_lin * sigma * (1.0 + gate_lin * (1.0 - sigma))).astype(BF16)
    grad_up = (grad_hidden * gate_lin * sigma).astype(BF16)
    gate_grad = over_rows(normed_two, grad_gate)
    up_grad = over_rows(normed_two, grad_up)
    grad_normed_two = over_cols(grad_gate, gate_weight) + over_cols(grad_up, up_weight)
    ffn_gain_grad = jnp.sum(grad_normed_two * unit_two, axis=0)
    grad_middle = grad_out + norm_back(grad_normed_two * gain_two, unit_two, scale_two)
    grad_mixed = grad_middle.astype(BF16)
    out_grad = over_rows(gated, grad_mixed)
    grad_gated = over_cols(grad_mixed, out_weight).reshape(seqs, span, width)
    grad_c = grad_gated * convolved
    grad_conv = grad_gated * c_gate
    conv_grad = jnp.stack([jnp.sum(grad_conv * lag, axis=(0, 1)) for lag in lags], axis=1)
    ahead = jnp.concatenate([grad_conv, shift(grad_conv[:, :2], -1)], axis=1)
    grad_product = (
        taps[:, 2] * ahead[:, :span]
        + taps[:, 1] * ahead[:, 1 : span + 1]
        + taps[:, 0] * ahead[:, 2:]
    )
    grad_projected = (
        jnp.concatenate(
            [grad_product * x_value[:, 2:], grad_c, grad_product * b_gate[:, 2:]], axis=2
        )
        .astype(BF16)
        .reshape(-1, 3 * width)
    )
    normed_one = normed_ext[:, 2:].reshape(-1, width)
    unit_one = unit_ext[:, 2:].reshape(-1, width)
    scale_one = scale_ext[:, 2:].reshape(-1, 1)
    in_grad = over_rows(normed_one, grad_projected)
    grad_normed_one = over_cols(grad_projected, in_weight)
    norm_gain_grad = jnp.sum(grad_normed_one * unit_one, axis=0)
    grad_tokens = grad_middle + norm_back(grad_normed_one * gain_one, unit_one, scale_one)

    def to_slots(rows):
        return (rows.reshape(seqs, span, width) * live).astype(BF16)

    def reduced(values):
        share = lax.psum_scatter(values.astype(BF16), "fsdp", scatter_dimension=0, tiled=True)
        return lax.psum(share, "rep").astype(F32)

    return (
        to_slots(output),
        to_slots(grad_tokens),
        *map(
            reduced,
            (
                norm_gain_grad,
                in_grad,
                conv_grad,
                out_grad,
                ffn_gain_grad,
                gate_grad,
                up_grad,
                down_grad,
            ),
        ),
    )


def solution(mesh):
    rows = P("rep", "fsdp", None)
    lists = P("rep", None)
    vector = P("fsdp")
    matrix = P("fsdp", None)
    return jax.shard_map(
        body,
        mesh=mesh,
        in_specs=(
            rows,
            rows,
            lists,
            lists,
            vector,
            matrix,
            matrix,
            matrix,
            vector,
            matrix,
            matrix,
            matrix,
        ),
        out_specs=(rows, rows, vector, matrix, matrix, matrix, vector, matrix, matrix, matrix),
        check_vma=False,
    )
```

time: 1640 us -> 1520 us (0.927)
  blocking collectives: 233 us -> 79.7 us
  local copies, waits for them, and re-layouts: 66 us -> 20.6 us
  waiting for transfers between devices: 1090 us -> 1130 us
  matrix products: 175 us -> 212 us
    all_to_all x1 -> x0, blocking collectives: 92.7 us -> none  [body(): lax.all_to_all(sent_tokens, 'fsdp', split_axis=0, concat_axis=1, tiled=True)]
    all_gather x5, waiting for transfers between devices: 350 us -> 440 us  [gather(): return lax.all_gather(values, 'fsdp', axis=0, tiled=True)]
    reduce_scatter x5, waiting for transfers between devices: 567 us -> 638 us  [reduced(): lax.psum_scatter(values.astype(BF16), 'fsdp', scatter_dimension=0, tiled=...]
    all_gather x3, blocking collectives: 115 us -> 53.8 us  [gather(): return lax.all_gather(values, 'fsdp', axis=0, tiled=True)]
    all_to_all x3 -> x0, waiting for transfers between devices: 54.8 us -> none  [the longest x1 54.8 us: body(): lax.all_to_all(out_slots, 'fsdp', split_axis=1, concat_axis=0, tiled=True)]
    unnamed x13, waiting for transfers between devices: 46.5 us -> 3.23 us
    gather x8 -> x0, local copies, waits for them, and re-layouts: 32.3 us -> none  [the longest x2 10.7 us: to_slots(): jnp.take(packed_rows, back_index, axis=0)]
    psum x1, waiting for transfers between devices: 69.7 us -> 45.5 us  [reduced(): return lax.psum(share, 'rep').astype(F32)]
  transfers between devices with their start and end apart: 15 -> 14, of which waited for: 10 -> 12; matrix products, arithmetic and copies ran while one was open for 12% -> 12% of each run, Pallas kernels for 0% -> 0%
where the time goes in v1:
time: 1520 us; the launch traced here: 1510 us
  waiting for transfers between devices  1130 us (74%)
  matrix products  212 us (14%)
  blocking collectives  79.7 us (5%)
  other arithmetic  49.1 us (3%)
  local copies, waits for them, and re-layouts  20.6 us (1%)
  between operations  15.7 us (1%)
    reduce_scatter x5, waiting for transfers between devices, reduced(): lax.psum_scatter(values.astype(BF16), 'fsdp', scatter_dimension=0, tiled=...  638 us
    all_gather x5, waiting for transfers between devices, gather(): return lax.all_gather(values, 'fsdp', axis=0, tiled=True)  440 us
    dot_general x5, matrix products, over_cols(): lax.dot_general(left_side, right_side, (((1,), (1,)), ((), ())), preferre...  79.8 us
    dot_general x5, matrix products, dot(): return jnp.dot(left_side, right_side, preferred_element_type=F32)  66.7 us
    dot_general x5, matrix products, over_rows(): lax.dot_general(left_side, right_side, (((0,), (0,)), ((), ())), preferre...  65.9 us
    all_gather x3, blocking collectives, gather(): return lax.all_gather(values, 'fsdp', axis=0, tiled=True)  53.8 us
    psum x1, waiting for transfers between devices, reduced(): return lax.psum(share, 'rep').astype(F32)  45.5 us
  transfers between devices with their start and end apart: 14, of which 12 were waited for; matrix products, arithmetic and copies ran while one was open for 12% of the time, Pallas kernels for 0%

profile of v1, /device:TPU:0, one launch (start us, length us, event | category | flops | bytes accessed | tf_op | source)
XLA Modules:
  0.0 1513.2 jit_solution(15626529436629893880)
XLA Ops:
  15.6 19.0 %all_gather.26 = bf16[1024,3]{0,1:T(4,128)(2,1)S(1)} all-gather(bf16[128,3]{0,1:T(4,128)(2,1)S(1)} %copy-done.37), channel_id=1, replica_groups=mesh['rep'=4,'fsdp'=8] {'fsdp'}, dimensions={0}, use_global_device_ids=true | all-gather | bytes 6912 | tf_op jit(solution)/shard_map/all_gather | solution.py:70
  39.3 16.4 %all-gather = bf16[8,1,128]{2,1,0:T(2,128)(2,1)S(1)} all-gather(bf16[1,1,128]{2,1,0:T(2,128)(2,1)S(1)} %bitcast.93), channel_id=1, replica_groups=mesh['rep'=4,'fsdp'=8] {'fsdp'}, dimensions={0}, use_global_device_ids=true | all-gather | bytes 2304 | tf_op jit(solution)/shard_map/all_gather | solution.py:70
  55.7 18.4 %all-gather.1 = bf16[8,1,128]{2,1,0:T(2,128)(2,1)S(1)} all-gather(bf16[1,1,128]{2,1,0:T(2,128)(2,1)S(1)} %bitcast.94), channel_id=1, replica_groups=mesh['rep'=4,'fsdp'=8] {'fsdp'}, dimensions={0}, use_global_device_ids=true | all-gather | bytes 2304 | tf_op jit(solution)/shard_map/all_gather | solution.py:70
  75.6 36.5 %all-gather.8.cloned.1.call-done = bf16[1024,3072]{1,0:T(8,128)(2,1)} async-done(((bf16[128,3072]{1,0:T(8,128)(2,1)}), bf16[1024,3072]{1,0:T(8,128)(2,1)}) %all-gather.8.cloned.1.call-update) | async-done | bytes 6291472 | tf_op jit(solution)/shard_map/all_gather | solution.py:70
  112.1 11.4 fusion.11
  133.6 28.2 %all-gather.10.cloned.1.call-done = bf16[1024,1024]{1,0:T(8,128)(2,1)} async-done(((bf16[128,1024]{1,0:T(8,128)(2,1)}), bf16[1024,1024]{1,0:T(8,128)(2,1)}) %all-gather.10.cloned.1.call-update) | async-done | bytes 2097168 | tf_op jit(solution)/shard_map/all_gather | solution.py:70
  168.8 131.7 %all-gather.12.cloned.1.call-done = bf16[1024,4608]{1,0:T(8,128)(2,1)} async-done(((bf16[128,4608]{1,0:T(8,128)(2,1)}), bf16[1024,4608]{1,0:T(8,128)(2,1)}) %all-gather.12.cloned.1.call-update) | async-done | bytes 9437200 | tf_op jit(solution)/shard_map/all_gather | solution.py:70
  300.5 16.1 %fusion.35 = f32[1024,4608]{1,0:T(8,128)} fusion(bf16[1024,1024]{1,0:T(8,128)(2,1)S(1)} %multiply_convert_fusion.7, bf16[1024,4608]{1,0:T(8,128)(2,1)} %all-gather.12.cloned.1.call-done), kind=kOutput, calls=%fused_computation.84 | convolution fusion | flops 9663676416 | bytes 30408704 | tf_op jit(solution)/shard_map/dot_general | solution.py:34
  316.7 122.2 %all-gather.14.cloned.1.call-done = bf16[1024,4608]{1,0:T(8,128)(2,1)} async-done(((bf16[128,4608]{1,0:T(8,128)(2,1)}), bf16[1024,4608]{1,0:T(8,128)(2,1)}) %all-gather.14.cloned.1.call-update) | async-done | bytes 9437200 | tf_op jit(solution)/shard_map/all_gather | solution.py:70
  438.8 17.0 %fusion.36 = f32[1024,4608]{1,0:T(8,128)} fusion(bf16[1024,1024]{1,0:T(8,128)(2,1)} %copy-done.15, bf16[1024,4608]{1,0:T(8,128)(2,1)} %all-gather.14.cloned.1.call-done), kind=kOutput, calls=%fused_computation.85 | convolution fusion | flops 9663676416 | bytes 30408704 | tf_op jit(solution)/shard_map/dot_general | solution.py:34
  455.8 121.3 %all-gather.16.cloned.1.call-done = bf16[4608,1024]{1,0:T(8,128)(2,1)} async-done(((bf16[576,1024]{1,0:T(8,128)(2,1)}), bf16[4608,1024]{1,0:T(8,128)(2,1)}) %all-gather.16.cloned.1.call-update) | async-done | bytes 9437200 | tf_op jit(solution)/shard_map/all_gather | solution.py:70
  577.2 31.1 %multiply_convert_fusion = (bf16[1024,4608]{1,0:T(8,128)(2,1)}, bf16[1024,4608]{1,0:T(8,128)(2,1)}, bf16[1024,4608]{1,0:T(8,128)(2,1)}) fusion(f32[1024,4608]{1,0:T(8,128)} %fusion.35, f32[1024,4608]{1,0:T(8,128)} %fusion.36, bf16[1024,1024]{1,0:T(8,128)(2,1)S(1)} %copy-done.13, bf16[4608,1024]{1,0:T(8,128)(2,1)} %all-gather.16.cloned.1.call-done), kind=kOutput, calls=%fused_computation | convolution fusion | flops 9739173888 | bytes 77594624 | tf_op jit(solution)/shard_map/dot_general | solution.py:28
  608.2 16.1 %fusion.37 = f32[1024,1024]{1,0:T(8,128)} fusion(bf16[1024,4608]{1,0:T(8,128)(2,1)} %get-tuple-element.33, bf16[1024,4608]{1,0:T(8,128)(2,1)} %all-gather.12.cloned.1.call-done), kind=kOutput, calls=%fused_computation.86 | convolution fusion | flops 9663676416 | bytes 23068672 | tf_op jit(solution)/shard_map/dot_general | solution.py:28
  624.3 17.7 %multiply_reduce_fusion = (bf16[1024]{0:T(1024)(128)(2,1)}, f32[1024]{0:T(1024)S(1)}, f32[1024,1024]{1,0:T(8,128)S(1)}) fusion(f32[1024,1024]{1,0:T(8,128)S(1)} %copy-done.7, f32[1024]{0:T(1024)S(1)} %add_rsqrt_fusion.1, f32[1024]{0:T(1024)S(1)} %bitcast.85, f32[1024,1024]{1,0:T(8,128)} %fusion.37, bf16[1024,4608]{1,0:T(8,128)(2,1)} %get-tuple-element.32, ...), kind=kOutput, calls=%fused_computation.49 | convolution fusion | flops 9671014400 | bytes 31471616 | tf_op jit(solution)/shard_map/dot_general | solution.py:28
  647.8 6.0 multiply_reduce_fusion.3
  654.8 6.7 convolution_convert_fusion.3
  679.7 9.4 bitcast_convert_fusion
  689.1 16.4 %convolution_convert_fusion.1 = bf16[1024,4608]{1,0:T(8,128)(2,1)} fusion(bf16[1024,1024]{1,0:T(8,128)(2,1)} %copy-done.15, bf16[1024,4608]{1,0:T(8,128)(2,1)} %get-tuple-element.33), kind=kOutput, calls=%fused_computation.6 | convolution fusion | flops 9668395008 | bytes 20971520 | tf_op jit(solution)/shard_map/dot_general | solution.py:22
  705.6 16.6 %convolution_convert_fusion = bf16[1024,4608]{1,0:T(8,128)(2,1)} fusion(bf16[1024,1024]{1,0:T(8,128)(2,1)} %copy-done.15, bf16[1024,4608]{1,0:T(8,128)(2,1)} %get-tuple-element.32), kind=kOutput, calls=%fused_computation.5 | convolution fusion | flops 9668395008 | bytes 20971520 | tf_op jit(solution)/shard_map/dot_general | solution.py:22
  722.3 16.7 %convolution_convert_fusion.2 = bf16[4608,1024]{1,0:T(8,128)(2,1)} fusion(bf16[1024,4608]{1,0:T(8,128)(2,1)} %get-tuple-element.34, bf16[1024,1024]{1,0:T(8,128)(2,1)} %bitcast_convert_fusion.1), kind=kOutput, calls=%fused_computation.7 | convolution fusion | flops 9668395008 | bytes 20971520 | tf_op jit(solution)/shard_map/dot_general | solution.py:22
  741.0 5.2 slice.92
  746.4 17.6 %convolution_add_fusion.1 = f32[1024,1024]{1,0:T(8,128)} fusion(f32[1024,1024]{1,0:T(8,128)} %copy-done.6, bf16[1024,4608]{1,0:T(8,128)(2,1)} %get-tuple-element.34, bf16[4608,1024]{1,0:T(8,128)(2,1)} %all-gather.16.cloned.1.call-done), kind=kOutput, calls=%fused_computation.66 | convolution fusion | flops 9664724992 | bytes 27262976 | tf_op jit(solution)/shard_map/dot_general | solution.py:34
  764.8 19.7 %reduce-scatter.11.cloned.1.call-done = bf16[128,1024]{1,0:T(8,128)(2,1)} async-done(((bf16[1024,1024]{1,0:T(8,128)(2,1)}), bf16[128,1024]{1,0:T(8,128)(2,1)}) %reduce-scatter.11.cloned.1.call-update) | async-done | bytes 262160 | tf_op jit(solution)/shard_map/reduce_scatter | solution.py:145
  784.5 120.6 %reduce-scatter.9.cloned.1.call-done = bf16[128,3072]{1,0:T(8,128)(2,1)} async-done(((bf16[1024,3072]{1,0:T(8,128)(2,1)}), bf16[128,3072]{1,0:T(8,128)(2,1)}) %reduce-scatter.9.cloned.1.call-update) | async-done | bytes 786448 | tf_op jit(solution)/shard_map/reduce_scatter | solution.py:145
  905.1 166.1 %reduce-scatter.13.cloned.1.call-done = bf16[128,4608]{1,0:T(8,128)(2,1)} async-done(((bf16[1024,4608]{1,0:T(8,128)(2,1)}), bf16[128,4608]{1,0:T(8,128)(2,1)}) %reduce-scatter.13.cloned.1.call-update) | async-done | bytes 1179664 | tf_op jit(solution)/shard_map/reduce_scatter | solution.py:145
  1071.2 165.9 %reduce-scatter.15.cloned.1.call-done = bf16[128,4608]{1,0:T(8,128)(2,1)} async-done(((bf16[1024,4608]{1,0:T(8,128)(2,1)}), bf16[128,4608]{1,0:T(8,128)(2,1)}) %reduce-scatter.15.cloned.1.call-update) | async-done | bytes 1179664 | tf_op jit(solution)/shard_map/reduce_scatter | solution.py:145
  1237.0 166.0 %reduce-scatter.17.cloned.1.call-done = bf16[576,1024]{1,0:T(8,128)(2,1)} async-done(((bf16[4608,1024]{1,0:T(8,128)(2,1)}), bf16[576,1024]{1,0:T(8,128)(2,1)}) %reduce-scatter.17.cloned.1.call-update) | async-done | bytes 1179664 | tf_op jit(solution)/shard_map/reduce_scatter | solution.py:145
  1403.1 12.6 fusion.25
  1415.7 19.4 %all-reduce.2 = (bf16[1024]{0:T(1024)(128)(2,1)S(1)}, bf16[1024]{0:T(1024)(128)(2,1)S(1)}) all-reduce(bf16[1024]{0:T(1024)(128)(2,1)S(1)} %get-tuple-element.15, bf16[1024]{0:T(1024)(128)(2,1)S(1)} %copy-done.36), channel_id=2, replica_groups=mesh['rep'=4,'fsdp'=8] {'fsdp'}, use_global_device_ids=true, to_apply=%region_6.7.clone | all-reduce | flops 2048 | bytes 8192
  1435.3 6.5 all-reduce.3
  1443.5 5.8 fusion.24
  1452.1 45.5 %all-reduce.7.cloned.1.call-done = (bf16[128,3072]{1,0:T(8,128)(2,1)}, bf16[128,1024]{1,0:T(8,128)(2,1)}, bf16[128,4608]{1,0:T(8,128)(2,1)}, bf16[128,4608]{1,0:T(8,128)(2,1)}, bf16[576,1024]{1,0:T(8,128)(2,1)}) async-done(((bf16[128,3072]{1,0:T(8,128)(2,1)}, bf16[128,1024]{1,0:T(8,128)(2,1)}, bf16[128,4608]{1,0:T(8,128)(2,1)}, bf16[128,4608]{1,0:T(8,128)(2,1)}, bf16[576,1024]{1,0:T(8,128)(2,1)}), ...) | async-done | bytes 4587536 | tf_op jit(solution)/shard_map/psum | solution.py:146
  (166 shorter events, 71.7 us)
Async XLA Ops:
  7.2 27.5 %copy-start.42 = (s32[1,16]{1,0:T(1,128)S(1)}, s32[1,16]{1,0:T(1,128)}, u32[]{:S(2)}) copy-start(s32[1,16]{1,0:T(1,128)} %param.15) | copy-start | bytes 196
  7.2 27.4 %copy-start.41 = (s32[1,16]{1,0:T(1,128)S(1)}, s32[1,16]{1,0:T(1,128)}, u32[]{:S(2)}) copy-start(s32[1,16]{1,0:T(1,128)} %param.14) | copy-start | bytes 196
  7.2 104.9 %all-gather.8.cloned.1.call-start = ((), (), s32[]{:S(2)}) async-start(), calls=%async_computation.6 | async-start | bytes 7077888 | tf_op jit(solution)/shard_map/all_gather | solution.py:70
  8.0 153.8 %all-gather.10.cloned.1.call-start = ((), (), s32[]{:S(2)}) async-start(), calls=%async_computation.7 | async-start | bytes 2359296 | tf_op jit(solution)/shard_map/all_gather | solution.py:70
  8.7 291.8 %all-gather.12.cloned.1.call-start = ((), (), s32[]{:S(2)}) async-start(), calls=%async_computation.8 | async-start | bytes 10616832 | tf_op jit(solution)/shard_map/all_gather | solution.py:70
  9.4 429.4 %all-gather.14.cloned.1.call-start = ((), (), s32[]{:S(2)}) async-start(), calls=%async_computation.9 | async-start | bytes 10616832 | tf_op jit(solution)/shard_map/all_gather | solution.py:70
  10.0 567.1 %all-gather.16.cloned.1.call-start = ((), (), s32[]{:S(2)}) async-start(), calls=%async_computation.10 | async-start | bytes 10616832 | tf_op jit(solution)/shard_map/all_gather | solution.py:70
  10.6 753.3 %reduce-scatter.19.cloned.1.call-start = ((), (), s32[]{:S(2)}) async-start(), calls=%async_computation.16 | async-start | bytes 294912
  10.7 63.3 %collective-permute-start = (bf16[16,2,1024]{2,1,0:T(2,128)(2,1)S(1)}, bf16[16,2,1024]{2,1,0:T(2,128)(2,1)S(1)}, u32[]{:S(2)}, u32[]{:S(2)}) collective-permute-start(bf16[16,2,1024]{2,1,0:T(2,128)(2,1)S(1)} %slice.59), channel_id=1, source_target_pairs={{0,1},{1,2},{2,3},{3,4},{4,5},{5,6},{6,7},{8,9},{9,10},{10,11},{11... | collective-permute-start | bytes 196616 | tf_op jit(solution)/shard_map/ppermute | solution.py:48
  37.4 37.7 %copy-start.2 = (f32[16,64,1024]{2,1,0:T(8,128)}, f32[16,64,1024]{2,1,0:T(8,128)S(1)}, u32[]{:S(2)}) copy-start(f32[16,64,1024]{2,1,0:T(8,128)S(1)} %convert_multiply_fusion.2) | copy-start | bytes 12582916
  37.4 18.3 %copy-start.39 = (bf16[128]{0:T(256)(128)(2,1)S(1)}, bf16[128]{0:T(256)(128)(2,1)}, u32[]{:S(2)}) copy-start(bf16[128]{0:T(256)(128)(2,1)} %param.20) | copy-start | bytes 772
  39.2 85.9 %copy-start.27 = (f32[1024,1]{0,1:T(1,128)}, f32[1024,1]{0,1:T(1,128)S(1)}, u32[]{:S(2)}) copy-start(f32[1024,1]{0,1:T(1,128)S(1)} %get-tuple-element.42) | copy-start | bytes 12292
  39.3 85.9 %copy-start.29 = (f32[1024,1]{0,1:T(1,128)}, f32[1024,1]{0,1:T(1,128)S(1)}, u32[]{:S(2)}) copy-start(f32[1024,1]{0,1:T(1,128)S(1)} %get-tuple-element.43) | copy-start | bytes 12292
  39.3 85.9 %copy-start.31 = (f32[1024,1]{0,1:T(1,128)}, f32[1024,1]{0,1:T(1,128)S(1)}, u32[]{:S(2)}) copy-start(f32[1024,1]{0,1:T(1,128)S(1)} %get-tuple-element.44) | copy-start | bytes 12292
  55.7 67.8 %copy-start.25 = (f32[8,1,128]{2,1,0:T(1,128)}, f32[8,1,128]{2,1,0:T(1,128)S(1)}, u32[]{:S(2)}) copy-start(f32[8,1,128]{2,1,0:T(1,128)S(1)} %convert_element_type.136) | copy-start | bytes 12292
  74.1 49.5 %copy-start.20 = (bf16[16,2,1024]{2,1,0:T(2,128)(2,1)}, bf16[16,2,1024]{2,1,0:T(2,128)(2,1)S(1)}, u32[]{:S(2)}) copy-start(bf16[16,2,1024]{2,1,0:T(2,128)(2,1)S(1)} %collective-permute-done) | copy-start | bytes 196612
  75.6 47.9 %copy-start.33 = (f32[16,66]{1,0:T(8,128)}, f32[16,66]{1,0:T(8,128)S(1)}, u32[]{:S(2)}) copy-start(f32[16,66]{1,0:T(8,128)S(1)} %get-tuple-element.41) | copy-start | bytes 12676
  168.8 131.7 %copy-start.15 = (bf16[1024,1024]{1,0:T(8,128)(2,1)}, bf16[1024,1024]{1,0:T(8,128)(2,1)S(1)}, u32[]{:S(2)}) copy-start(bf16[1024,1024]{1,0:T(8,128)(2,1)S(1)} %multiply_convert_fusion.7) | copy-start | bytes 6291460
  316.7 260.5 %copy-start.13 = (bf16[1024,1024]{1,0:T(8,128)(2,1)S(1)}, bf16[1024,1024]{1,0:T(8,128)(2,1)}, u32[]{:S(2)}) copy-start(bf16[1024,1024]{1,0:T(8,128)(2,1)} %bitcast_convert_fusion.1) | copy-start | bytes 6291460
  608.2 16.1 %copy-start.7 = (f32[1024,1024]{1,0:T(8,128)S(1)}, f32[1024,1024]{1,0:T(8,128)}, u32[]{:S(2)}) copy-start(f32[1024,1024]{1,0:T(8,128)} %copy-done.6) | copy-start | bytes 12582916
  624.3 17.7 %copy-start.3 = (f32[16,64,1024]{2,1,0:T(8,128)S(1)}, f32[16,64,1024]{2,1,0:T(8,128)}, u32[]{:S(2)}) copy-start(f32[16,64,1024]{2,1,0:T(8,128)} %copy-done.2) | copy-start | bytes 12582916
  654.7 9.6 copy-start.10
  654.8 9.6 copy-start.21
  654.8 9.6 copy-start.26
  654.8 129.7 %reduce-scatter.11.cloned.1.call-start = ((), (), s32[]{:S(2)}) async-start(), calls=%async_computation.12 | async-start | bytes 2359296 | tf_op jit(solution)/shard_map/reduce_scatter | solution.py:145
  661.6 243.5 %reduce-scatter.9.cloned.1.call-start = ((), (), s32[]{:S(2)}) async-start(), calls=%async_computation.11 | async-start | bytes 7077888 | tf_op jit(solution)/shard_map/reduce_scatter | solution.py:145
  662.8 7.1 collective-permute-start.1
  689.1 382.1 %reduce-scatter.13.cloned.1.call-start = ((), (), s32[]{:S(2)}) async-start(), calls=%async_computation.13 | async-start | bytes 10616832 | tf_op jit(solution)/shard_map/reduce_scatter | solution.py:145
  705.6 531.4 %reduce-scatter.15.cloned.1.call-start = ((), (), s32[]{:S(2)}) async-start(), calls=%async_computation.14 | async-start | bytes 10616832 | tf_op jit(solution)/shard_map/reduce_scatter | solution.py:145
  722.3 680.8 %reduce-scatter.17.cloned.1.call-start = ((), (), s32[]{:S(2)}) async-start(), calls=%async_computation.15 | async-start | bytes 10616832 | tf_op jit(solution)/shard_map/reduce_scatter | solution.py:145
  739.1 758.4 %all-reduce.7.cloned.1.call-start = ((), (), s32[]{:S(2)}) async-start(), calls=%async_computation.17 | async-start | bytes 9175040 | tf_op jit(solution)/shard_map/psum | solution.py:146
  1403.1 12.7 copy-start.36
  (28 other events, 124.7 us)
Sparse Core Ops, SparseCore 0:
  10.2 101.8 all-gather.7
  114.2 47.4 all-gather.9
  163.9 136.5 all-gather.11
  302.6 136.2 all-gather.13
  440.9 136.2 all-gather.15
  654.9 59.4 reduce-scatter.18
  717.9 66.6 reduce-scatter.10
  788.1 116.9 reduce-scatter.8
  908.7 162.4 reduce-scatter.12
  1074.6 162.3 reduce-scatter.14
  1240.6 162.3 reduce-scatter.16
  1405.6 91.8 all-reduce.6

commit v2 on v1

--- a/solution.py
+++ b/solution.py
@@ -1,11 +1,502 @@
+import functools
 import jax
 import jax.numpy as jnp
 from jax import lax
-from jax.sharding import PartitionSpec as P
+from jax.experimental import pallas as pl
+from jax.experimental.pallas import tpu as pltpu
+from jax.sharding import Mesh, PartitionSpec as P
 
 EPS = 1e-05
 F32 = jnp.float32
 BF16 = jnp.bfloat16
+NT = (((1,), (1,)), ((), ()))
+TN = (((0,), (0,)), ((), ()))
+MESH = pl.DeviceIdType.MESH
+CHUNK = 256
+BLOCK = 128
+GROUP = ("z", "y")
+
+
+def ffn_kernel(
+    sizes,
+    n2_in, ef_in, gate_in, up_in, down_in,
+    ffn_out, dn2_out, gu_out, down_out, all_gu, all_down,
+    n2v, efv, n2t, wgu, wd, outv, dnv, qs, ggs, gvs,
+    ggu, gd, rxg, rxd, s1g, s1d, ryg, ryd, s2g, s2d, rzg, rzd, fing, find, give, take,
+    sem_in, sem_load, sem_own, sem_pair,
+    ag_z, ag_y, ag_dz, ag_dy, ag_send, ag_relay, ag_dsend, ag_drelay,
+    rx_g, rx_d, ry_g, ry_d, rz_g, rz_d, sx_g, sx_d, sy_g, sy_d, sz_g, sz_d, sem_fin,
+):
+    nx, nz, ny, rows, width, hidden = sizes
+    n = nz * ny
+    dn = width // n
+    half = hidden // 2
+    steps = half // CHUNK
+    per_half = half // BLOCK // 2
+    own_rows = hidden // n
+    gp = min(BLOCK, own_rows & -own_rows)
+    pieces = CHUNK // gp
+    slots = ggu.shape[0]
+    lag = slots // 2
+    x, c = lax.axis_index("x"), lax.axis_index("core")
+    z, y = lax.axis_index("z"), lax.axis_index("y")
+    me = z * ny + y
+
+    def at(x=x, c=c, z=z, y=y):
+        return (x, c, z, y)
+
+    def zp(d):
+        return lax.rem(z + d, nz)
+
+    def yp(d):
+        return lax.rem(y + d, ny)
+
+    def xp(d):
+        return lax.rem(x + d, nx)
+
+    def blocks(m):
+        h, i = m % 2, m // 2
+        return per_half * h + i, per_half * h + per_half - 1 - i + per_half * (m // (2 * (per_half // 2)))
+
+    def column(b):
+        return pl.multiple_of(c * half + b * BLOCK, BLOCK)
+
+    def owner(m, q):
+        b = blocks(m)[q * gp // BLOCK]
+        row = c * half + b * BLOCK + (q * gp) % BLOCK
+        j = row // own_rows
+        return j // ny, j % ny, pl.multiple_of(row - j * own_rows, gp)
+
+    def remote(src, dst, ssem, rsem, dev):
+        return pltpu.make_async_remote_copy(
+            src_ref=src, dst_ref=dst, send_sem=ssem, recv_sem=rsem, device_id=dev, device_id_type=MESH
+        )
+
+    def landed(ref, sem):
+        pltpu.make_async_copy(ref, ref, sem).wait()
+
+    barrier = pltpu.get_barrier_semaphore()
+    peers = [at(z=zp(d)) for d in range(1, nz)] + [at(y=yp(d)) for d in range(1, ny)]
+    peers += [at(x=xp(d)) for d in range(1, nx)] + [at(c=1 - c)]
+    for dev in peers:
+        pl.semaphore_signal(barrier, inc=1, device_id=dev, device_id_type=MESH)
+    pl.semaphore_wait(barrier, len(peers))
+
+    mine = pl.ds(pl.multiple_of(c * rows, rows), rows)
+    other = pl.ds(pl.multiple_of((1 - c) * rows, rows), rows)
+    pair = []
+    for i, (src, dst) in enumerate(((n2_in, n2v), (ef_in, efv))):
+        pltpu.make_async_copy(src, dst.at[mine], sem_in.at[i]).start()
+        pair.append(remote(src, dst.at[mine], sem_pair.at[0, i], sem_pair.at[1, i], at(c=1 - c)))
+        pair[i].start()
+
+    ag_peers = [(0, d) for d in range(1, nz)] + [(1, d) for d in range(1, ny)]
+
+    def first_hop(m):
+        b = blocks(m)
+        for k in range(2):
+            src_cols = pl.ds(column(b[k]), BLOCK)
+            dst_cols = pl.ds(k * BLOCK, BLOCK)
+            for w, src in enumerate((gate_in, up_in)):
+                here = src.at[:, src_cols]
+                there = all_gu.at[m, w, z, y, :, dst_cols]
+                pltpu.make_async_copy(here, there, sem_own.at[0]).start()
+                for p, (ax, d) in enumerate(ag_peers):
+                    if ax == 0:
+                        remote(here, there, ag_send.at[p], ag_z.at[m, d - 1], at(z=zp(d))).start()
+                    else:
+                        remote(here, there, ag_send.at[p], ag_y.at[m, d - 1], at(y=yp(d))).start()
+        for q in range(pieces):
+            zo, yo, row = owner(m, q)
+
+            @pl.when(jnp.logical_and(zo == z, yo == y))
+            def _():
+                here = down_in.at[pl.ds(row, gp)]
+                there = all_down.at[m, pl.ds(q * gp, gp)]
+                pltpu.make_async_copy(here, there, sem_own.at[1]).start()
+                for p, (ax, d) in enumerate(ag_peers):
+                    if ax == 0:
+                        remote(here, there, ag_dsend.at[p], ag_dz.at[m, q], at(z=zp(d))).start()
+                    else:
+                        remote(here, there, ag_dsend.at[p], ag_dy.at[m, q], at(y=yp(d))).start()
+
+    def second_hop(m):
+        for d in range(1, nz):
+            zs = lax.rem(z - d + nz, nz)
+            block = all_gu.at[m, :, zs, y]
+            landed(block, ag_z.at[m, d - 1])
+            for e in range(1, ny):
+                remote(block, block, ag_relay.at[d - 1, e - 1], ag_y.at[m, e - 1], at(y=yp(e))).start()
+        for q in range(pieces):
+            zo, yo, _ = owner(m, q)
+
+            @pl.when(jnp.logical_and(zo != z, yo == y))
+            def _():
+                block = all_down.at[m, pl.ds(q * gp, gp)]
+                landed(block, ag_dz.at[m, q])
+                for e in range(1, ny):
+                    remote(block, block, ag_drelay.at[zo % 2, e - 1], ag_dy.at[m, q], at(y=yp(e))).start()
+
+    def load(m):
+        for e in range(1, ny):
+            ys = lax.rem(y - e + ny, ny)
+            landed(all_gu.at[m, :, :, ys], ag_y.at[m, e - 1])
+        for q in range(pieces):
+            _, yo, _ = owner(m, q)
+
+            @pl.when(yo != y)
+            def _():
+                landed(all_down.at[m, pl.ds(q * gp, gp)], ag_dy.at[m, q])
+        a = pltpu.make_async_copy(all_gu.at[m], wgu, sem_load.at[0])
+        b = pltpu.make_async_copy(all_down.at[m], wd, sem_load.at[1])
+        a.start()
+        b.start()
+        a.wait()
+        b.wait()
+
+    in_half = me // (n // 2) == c
+    relay = 2
+
+    @pl.loop(0, steps)
+    def _(m):
+        first_hop(m)
+
+    for i, (src, dst) in enumerate(((n2_in, n2v), (ef_in, efv))):
+        pltpu.make_async_copy(src, dst.at[mine], sem_in.at[i]).wait()
+        pair[i].wait_send()
+        landed(dst.at[other], sem_pair.at[1, i])
+
+    @pl.loop(0, 2 * rows // 256)
+    def _(r):
+        rs = pl.ds(pl.multiple_of(r * 256, 256), 256)
+        n2t[:, rs] = n2v[rs, :].T
+        outv[rs, :] = jnp.zeros((256, width), F32)
+        dnv[rs, :] = jnp.zeros((256, width), F32)
+
+    landed(all_gu.at[:, :, 0, 0], sem_own.at[0])
+
+    @pl.when(in_half)
+    def _():
+        landed(all_down.at[:, pl.ds(0, gp)], sem_own.at[1])
+
+    for m in range(relay):
+        second_hop(m)
+    load(0)
+
+    tile = 512
+
+    def compute(m):
+        slot = m % slots
+
+        @pl.loop(0, 2 * rows // tile)
+        def _(r):
+            rs = pl.ds(pl.multiple_of(r * tile, tile), tile)
+            gate = wgu[0].reshape(width, CHUNK)
+            up = wgu[1].reshape(width, CHUNK)
+            n2r = n2v[rs, :]
+            g = jnp.dot(n2r, gate, preferred_element_type=F32)
+            v = jnp.dot(n2r, up, preferred_element_type=F32)
+            s = jax.nn.sigmoid(g)
+            sg = g * s
+            q = (sg * v).astype(BF16)
+            dq = lax.dot_general(efv[rs, :], wd[...], NT, preferred_element_type=F32)
+            gg = (dq * v * s * (1.0 + g * (1.0 - s))).astype(BF16)
+            gv = (dq * sg).astype(BF16)
+            qs[rs, :] = q
+            ggs[rs, :] = gg
+            gvs[rs, :] = gv
+            outv[rs, :] += jnp.dot(q, wd[...], preferred_element_type=F32)
+            dnv[rs, :] += lax.dot_general(gg, gate, NT, preferred_element_type=F32) + lax.dot_general(
+                gv, up, NT, preferred_element_type=F32
+            )
+
+        group = nz * ny // 4
+
+        @pl.loop(0, 4)
+        def _(t):
+            ts = pl.ds(pl.multiple_of(t * 256, 256), 256)
+            a = n2t[ts, :]
+            for w, src in enumerate((ggs, gvs)):
+                full = jnp.dot(a, src[...], preferred_element_type=F32).astype(BF16)
+                full = full.reshape(group, nx, dn // nx, CHUNK)
+                for h in range(nx):
+                    for k in range(group):
+                        j = t * group + k
+                        ggu[slot, w, h, j // ny, j % ny] = full[k, h]
+
+        for h in range(nx):
+            lanes = pl.ds(h * (width // nx), width // nx)
+            gd[slot, h] = lax.dot_general(
+                qs[...], efv[:, lanes], TN, preferred_element_type=F32
+            ).astype(BF16)
+
+    def send_x(m):
+        slot = m % slots
+        for d in range(1, nx):
+            xo = xp(d)
+            remote(ggu.at[slot, :, xo], rxg.at[slot, d - 1], sx_g.at[slot, d - 1], rx_g.at[slot, d - 1], at(x=xo)).start()
+            remote(gd.at[slot, xo], rxd.at[slot, d - 1], sx_d.at[slot, d - 1], rx_d.at[slot, d - 1], at(x=xo)).start()
+
+    def send_y(m):
+        slot = m % slots
+        for d in range(1, nx):
+            landed(rxg.at[slot, d - 1], rx_g.at[slot, d - 1])
+            landed(rxd.at[slot, d - 1], rx_d.at[slot, d - 1])
+            landed(rxg.at[slot, d - 1], sx_g.at[slot, d - 1])
+            landed(rxd.at[slot, d - 1], sx_d.at[slot, d - 1])
+
+        @pl.loop(0, nz)
+        def _(zi):
+            for yi in range(ny):
+                for w in range(2):
+                    total = ggu[slot, w, x, zi, yi].astype(F32)
+                    for d in range(1, nx):
+                        total += rxg[slot, d - 1, w, zi, yi].astype(F32)
+                    s1g[slot, yi, w, zi] = total.astype(BF16)
+
+        total = gd[slot, x].astype(F32)
+        for d in range(1, nx):
+            total += rxd[slot, d - 1].astype(F32)
+        s1d[slot] = total.astype(BF16)
+        for d in range(1, ny):
+            yo = yp(d)
+            remote(s1g.at[slot, yo], ryg.at[slot, d - 1], sy_g.at[slot, d - 1], ry_g.at[slot, d - 1], at(y=yo)).start()
+        for q in range(pieces):
+            zo, yo, _ = owner(m, q)
+            part = pl.ds(q * gp, gp)
+
+            @pl.when(yo != y)
+            def _():
+                d = lax.rem(yo - y + ny, ny)
+                remote(
+                    s1d.at[slot, part], ryd.at[slot, d - 1, part], sy_d.at[slot, q], ry_d.at[slot, d - 1, q], at(y=yo)
+                ).start()
+
+    def send_z(m):
+        slot = m % slots
+        for d in range(1, ny):
+            landed(ryg.at[slot, d - 1], ry_g.at[slot, d - 1])
+            landed(ryg.at[slot, d - 1], sy_g.at[slot, d - 1])
+        for zi in range(nz):
+            for w in range(2):
+                total = s1g[slot, y, w, zi].astype(F32)
+                for d in range(1, ny):
+                    total += ryg[slot, d - 1, w, zi].astype(F32)
+                s2g[slot, zi, w] = total.astype(BF16)
+        for d in range(1, nz):
+            zo = zp(d)
+            remote(s2g.at[slot, zo], rzg.at[slot, d - 1], sz_g.at[slot, d - 1], rz_g.at[slot, d - 1], at(z=zo)).start()
+        for q in range(pieces):
+            zo, yo, _ = owner(m, q)
+            part = pl.ds(q * gp, gp)
+
+            @pl.when(yo != y)
+            def _():
+                landed(s1d.at[slot, part], sy_d.at[slot, q])
+
+            @pl.when(yo == y)
+            def _():
+                total = s1d[slot, part].astype(F32)
+                for d in range(1, ny):
+                    landed(ryd.at[slot, d - 1, part], ry_d.at[slot, d - 1, q])
+                    total += ryd[slot, d - 1, part].astype(F32)
+                s2d[slot, part] = total.astype(BF16)
+
+                @pl.when(zo != z)
+                def _():
+                    d = lax.rem(zo - z + nz, nz)
+                    remote(
+                        s2d.at[slot, part], rzd.at[slot, d - 1, part], sz_d.at[slot, q], rz_d.at[slot, d - 1, q], at(z=zo)
+                    ).start()
+
+    def finish(m):
+        slot = m % slots
+        for d in range(1, nz):
+            landed(rzg.at[slot, d - 1], rz_g.at[slot, d - 1])
+            landed(rzg.at[slot, d - 1], sz_g.at[slot, d - 1])
+        for w in range(2):
+            total = s2g[slot, z, w].astype(F32)
+            for d in range(1, nz):
+                total += rzg[slot, d - 1, w].astype(F32)
+            fing[w] = total.astype(BF16)
+        for q in range(pieces):
+            zo, yo, row = owner(m, q)
+            part = pl.ds(q * gp, gp)
+
+            @pl.when(jnp.logical_and(yo == y, zo != z))
+            def _():
+                landed(s2d.at[slot, part], sz_d.at[slot, q])
+
+            @pl.when(jnp.logical_and(yo == y, zo == z))
+            def _():
+                total = s2d[slot, part].astype(F32)
+                for d in range(1, nz):
+                    landed(rzd.at[slot, d - 1, part], rz_d.at[slot, d - 1, q])
+                    total += rzd[slot, d - 1, part].astype(F32)
+                find[part] = total.astype(BF16)
+                out = pltpu.make_async_copy(find.at[part], down_out.at[pl.ds(row, gp)], sem_fin.at[2])
+                out.start()
+                out.wait()
+        b = blocks(m)
+        outs = []
+        for k in range(2):
+            cols = pl.ds(pl.multiple_of(b[k] * BLOCK, BLOCK), BLOCK)
+            outs.append(
+                pltpu.make_async_copy(fing.at[:, :, pl.ds(k * BLOCK, BLOCK)], gu_out.at[:, :, cols], sem_fin.at[k])
+            )
+            outs[k].start()
+        for k in range(2):
+            outs[k].wait()
+
+    @pl.loop(0, steps + 3 * lag)
+    def _(m):
+        @pl.when(m < steps)
+        def _():
+            compute(m)
+
+        @pl.when(m >= 3 * lag)
+        def _():
+            finish(m - 3 * lag)
+
+        @pl.when(jnp.logical_and(m >= 2 * lag, m < steps + 2 * lag))
+        def _():
+            send_z(m - 2 * lag)
+
+        @pl.when(jnp.logical_and(m >= lag, m < steps + lag))
+        def _():
+            send_y(m - lag)
+
+        @pl.when(m < steps)
+        def _():
+            send_x(m)
+
+        @pl.when(m + relay < steps)
+        def _():
+            second_hop(m + relay)
+
+        @pl.when(m + 1 < steps)
+        def _():
+            load(m + 1)
+
+        @pl.when(m == steps - 1)
+        def _():
+            for i, src in enumerate((outv, dnv)):
+                give[i] = src[other, :].astype(BF16)
+                remote(give.at[i], take.at[i], sem_pair.at[2, i], sem_pair.at[3, i], at(c=1 - c)).start()
+
+    for i, (src, dst) in enumerate(((outv, ffn_out), (dnv, dn2_out))):
+        landed(take.at[i], sem_pair.at[3, i])
+        landed(take.at[i], sem_pair.at[2, i])
+        src[mine, :] += take[i].astype(F32)
+        out = pltpu.make_async_copy(src.at[mine], dst, sem_fin.at[i])
+        out.start()
+    for i, (src, dst) in enumerate(((outv, ffn_out), (dnv, dn2_out))):
+        pltpu.make_async_copy(src.at[mine], dst, sem_fin.at[i]).wait()
+
+    for p in range(len(ag_peers)):
+        landed(all_gu.at[:, :, 0, 0], ag_send.at[p])
+
+        @pl.when(in_half)
+        def _():
+            landed(all_down.at[:, pl.ds(0, gp)], ag_dsend.at[p])
+
+    for d in range(1, nz):
+        for e in range(1, ny):
+            landed(all_gu.at[:, :, 0, 0], ag_relay.at[d - 1, e - 1])
+    for k in range(2):
+        zo = (n // 2 * c) // ny + k
+
+        @pl.when(zo != z)
+        def _():
+            for e in range(1, ny):
+                landed(all_down.at[:, pl.ds(0, gp)], ag_drelay.at[zo % 2, e - 1])
+
+
+def ffn_call(sizes, n2, ef, gate, up, down, lag=1):
+    nx, nz, ny, rows, width, hidden = sizes
+    n = nz * ny
+    dn = width // n
+    half = hidden // 2
+    steps = half // CHUNK
+    own_rows = hidden // n
+    gp = min(BLOCK, own_rows & -own_rows)
+    pieces = CHUNK // gp
+    s = 2 * lag
+    dnx = dn // nx
+    lanes = width // nx
+    dma = pltpu.SemaphoreType.DMA
+    anywhere = pl.BlockSpec(memory_space=pl.ANY)
+    shape = jax.ShapeDtypeStruct
+    return pl.pallas_call(
+        functools.partial(ffn_kernel, sizes),
+        out_shape=[
+            shape((rows, width), F32),
+            shape((rows, width), F32),
+            shape((2, dnx, half), BF16),
+            shape((own_rows, lanes), BF16),
+            shape((steps, 2, nz, ny, dn, CHUNK), BF16),
+            shape((steps, CHUNK, width), BF16),
+        ],
+        in_specs=[anywhere] * 5,
+        out_specs=[anywhere] * 6,
+        scratch_shapes=[
+            pltpu.VMEM((2 * rows, width), BF16),
+            pltpu.VMEM((2 * rows, width), BF16),
+            pltpu.VMEM((width, 2 * rows), BF16),
+            pltpu.VMEM((2, nz, ny, dn, CHUNK), BF16),
+            pltpu.VMEM((CHUNK, width), BF16),
+            pltpu.VMEM((2 * rows, width), F32),
+            pltpu.VMEM((2 * rows, width), F32),
+            pltpu.VMEM((2 * rows, CHUNK), BF16),
+            pltpu.VMEM((2 * rows, CHUNK), BF16),
+            pltpu.VMEM((2 * rows, CHUNK), BF16),
+            pltpu.VMEM((s, 2, nx, nz, ny, dnx, CHUNK), BF16),
+            pltpu.VMEM((s, nx, CHUNK, lanes), BF16),
+            pltpu.VMEM((s, nx - 1, 2, nz, ny, dnx, CHUNK), BF16),
+            pltpu.VMEM((s, nx - 1, CHUNK, lanes), BF16),
+            pltpu.VMEM((s, ny, 2, nz, dnx, CHUNK), BF16),
+            pltpu.VMEM((s, CHUNK, lanes), BF16),
+            pltpu.VMEM((s, ny - 1, 2, nz, dnx, CHUNK), BF16),
+            pltpu.VMEM((s, ny - 1, CHUNK, lanes), BF16),
+            pltpu.VMEM((s, nz, 2, dnx, CHUNK), BF16),
+            pltpu.VMEM((s, CHUNK, lanes), BF16),
+            pltpu.VMEM((s, nz - 1, 2, dnx, CHUNK), BF16),
+            pltpu.VMEM((s, nz - 1, CHUNK, lanes), BF16),
+            pltpu.VMEM((2, dnx, CHUNK), BF16),
+            pltpu.VMEM((CHUNK, lanes), BF16),
+            pltpu.VMEM((2, rows, width), BF16),
+            pltpu.VMEM((2, rows, width), BF16),
+            dma((2,)),
+            dma((2,)),
+            dma((2,)),
+            dma((4, 2)),
+            dma((steps, nz - 1)),
+            dma((steps, ny - 1)),
+            dma((steps, pieces)),
+            dma((steps, pieces)),
+            dma((nz + ny - 2,)),
+            dma((nz - 1, ny - 1)),
+            dma((nz + ny - 2,)),
+            dma((2, ny - 1)),
+            dma((s, nx - 1)),
+            dma((s, nx - 1)),
+            dma((s, ny - 1)),
+            dma((s, ny - 1, pieces)),
+            dma((s, nz - 1)),
+            dma((s, nz - 1, pieces)),
+            dma((s, nx - 1)),
+            dma((s, nx - 1)),
+            dma((s, ny - 1)),
+            dma((s, pieces)),
+            dma((s, nz - 1)),
+            dma((s, pieces)),
+            dma((3,)),
+        ],
+        compiler_params=pltpu.CompilerParams(
+            collective_id=0, has_side_effects=True, vmem_limit_bytes=63 << 20
+        ),
+        name="feed_forward",
+    )(n2, ef, gate, up, down)[:4]
 
 
 def row_scale(values):
@@ -38,14 +529,14 @@
     slots = jnp.arange(deal.shape[1], dtype=jnp.int32)
     picked = deal[0][:, None] == slots[None, :]
     source_len = jnp.sum(jnp.where(picked, lengths[0][:, None], 0), axis=0)
-    position = lax.axis_index("fsdp") * span + jnp.arange(span, dtype=jnp.int32)
+    position = lax.axis_index(GROUP) * span + jnp.arange(span, dtype=jnp.int32)
     return (position[None, :] < source_len[:, None]).astype(F32)[..., None]
 
 
 def shift(values, amount):
-    size = lax.axis_size("fsdp")
+    size = (lax.axis_size("z") * lax.axis_size("y"))
     pairs = [(i, i + amount) for i in range(size) if 0 <= i + amount < size]
-    return lax.ppermute(values, "fsdp", pairs)
+    return lax.ppermute(values, GROUP, pairs)
 
 
 def body(
@@ -67,14 +558,12 @@
     halo = shift(tokens[:, span - 2 :], 1)
 
     def gather(values):
-        return lax.all_gather(values, "fsdp", axis=0, tiled=True)
+        return lax.all_gather(values, GROUP, axis=0, tiled=True)
 
     norm_gain, in_weight, conv_weight, out_weight = map(
         gather, (norm_gain, in_weight, conv_weight, out_weight)
     )
-    ffn_gain, gate_weight, up_weight, down_weight = map(
-        gather, (ffn_gain, gate_weight, up_weight, down_weight)
-    )
+    ffn_gain = gather(ffn_gain)
     gain_one = norm_gain.astype(F32)
     gain_two = ffn_gain.astype(F32)
     taps = conv_weight.astype(F32)
@@ -97,18 +586,19 @@
     normed_two = (unit_two * gain_two).astype(BF16)
     grad_out = (cotangent.astype(F32) * live).reshape(-1, width)
     grad_ffn = grad_out.astype(BF16)
-    gate_lin = dot(normed_two, gate_weight)
-    up_lin = dot(normed_two, up_weight)
-    sigma = jax.nn.sigmoid(gate_lin)
-    hidden = (gate_lin * sigma * up_lin).astype(BF16)
-    output = middle + dot(hidden, down_weight)
-    down_grad = over_rows(hidden, grad_ffn)
-    grad_hidden = over_cols(grad_ffn, down_weight)
-    grad_gate = (grad_hidden * up_lin * sigma * (1.0 + gate_lin * (1.0 - sigma))).astype(BF16)
-    grad_up = (grad_hidden * gate_lin * sigma).astype(BF16)
-    gate_grad = over_rows(normed_two, grad_gate)
-    up_grad = over_rows(normed_two, grad_up)
-    grad_normed_two = over_cols(grad_gate, gate_weight) + over_cols(grad_up, up_weight)
+    sizes = (
+        lax.axis_size("x"),
+        lax.axis_size("z"),
+        lax.axis_size("y"),
+        seqs * span,
+        width,
+        gate_weight.shape[1],
+    )
+    ffn_rows, grad_normed_two, gu_part, down_part = ffn_call(
+        sizes, normed_two, grad_ffn, gate_weight, up_weight, down_weight
+    )
+    output = middle + ffn_rows
+    gate_grad, up_grad, down_grad = whole_parts(sizes, gu_part, down_part)
     ffn_gain_grad = jnp.sum(grad_normed_two * unit_two, axis=0)
     grad_middle = grad_out + norm_back(grad_normed_two * gain_two, unit_two, scale_two)
     grad_mixed = grad_middle.astype(BF16)
@@ -142,36 +632,47 @@
         return (rows.reshape(seqs, span, width) * live).astype(BF16)
 
     def reduced(values):
-        share = lax.psum_scatter(values.astype(BF16), "fsdp", scatter_dimension=0, tiled=True)
-        return lax.psum(share, "rep").astype(F32)
+        share = lax.psum_scatter(values.astype(BF16), GROUP, scatter_dimension=0, tiled=True)
+        return lax.psum(share, ("x", "core")).astype(F32)
 
     return (
         to_slots(output),
         to_slots(grad_tokens),
-        *map(
-            reduced,
-            (
-                norm_gain_grad,
-                in_grad,
-                conv_grad,
-                out_grad,
-                ffn_gain_grad,
-                gate_grad,
-                up_grad,
-                down_grad,
-            ),
-        ),
-    )
+        reduced(norm_gain_grad),
+        reduced(in_grad),
+        reduced(conv_grad),
+        reduced(out_grad),
+        reduced(ffn_gain_grad),
+        gate_grad,
+        up_grad,
+        down_grad,
+    )
+
+
+def whole_parts(sizes, gu_part, down_part):
+    nx, nz, ny, _, width, hidden = sizes
+    both = lax.all_gather(gu_part, ("x", "core"))
+    both = both.reshape(nx, 2, *gu_part.shape).transpose(2, 0, 3, 1, 4)
+    both = both.reshape(2, width // (nz * ny), hidden).astype(F32)
+    down = lax.all_gather(down_part, ("x", "core"))
+    down = down.reshape(nx, 2, *down_part.shape)
+    down = lax.dynamic_index_in_dim(down, lax.axis_index("z") // (nz // 2), 1, keepdims=False)
+    down = down.transpose(1, 0, 2).reshape(down_part.shape[0], width).astype(F32)
+    return both[0], both[1], down
 
 
 def solution(mesh):
-    rows = P("rep", "fsdp", None)
-    lists = P("rep", None)
-    vector = P("fsdp")
-    matrix = P("fsdp", None)
+    rep, fsdp = mesh.shape["rep"], mesh.shape["fsdp"]
+    grid = (rep // 2, 2, 4, fsdp // 4)
+    split = Mesh(mesh.devices.reshape(grid), ("x", "core", "z", "y"))
+    copies = ("x", "core")
+    rows = P(copies, GROUP, None)
+    lists = P(copies, None)
+    vector = P(GROUP)
+    matrix = P(GROUP, None)
     return jax.shard_map(
         body,
-        mesh=mesh,
+        mesh=split,
         in_specs=(
             rows,
             rows,

time: 1520 us -> 857 us (0.56)
  waiting for transfers between devices: 1130 us -> 302 us
  Pallas kernels: 0 us -> 304 us
  matrix products: 212 us -> 47.3 us
    reduce_scatter x5 -> x2, waiting for transfers between devices: 638 us -> 186 us  [reduced(): lax.psum_scatter(values.astype(BF16), GROUP, scatter_dimension=0, tiled=T...]
    all_gather x5 -> x4, waiting for transfers between devices: 440 us -> 67.1 us  [the longest x2 67.1 us: gather(): return lax.all_gather(values, GROUP, axis=0, tiled=True)]
    pallas_call x0 -> x1, Pallas kernels: none -> 304 us  [ffn_call(): pl.pallas_call(functools.partial(ffn_kernel, sizes), out_shape=[shape((ro...]
    dot_general x5 -> x2, matrix products: 79.8 us -> 15.1 us  [over_cols(): lax.dot_general(left_side, right_side, (((1,), (1,)), ((), ())), preferre...]
    dot_general x5 -> x2, matrix products: 66.7 us -> 15.9 us  [dot(): return jnp.dot(left_side, right_side, preferred_element_type=F32)]
    dot_general x5 -> x2, matrix products: 65.9 us -> 16.3 us  [over_rows(): lax.dot_general(left_side, right_side, (((0,), (0,)), ((), ())), preferre...]
    psum x1, waiting for transfers between devices: 45.5 us -> 28.3 us  [reduced(): return lax.psum(share, ('x', 'core')).astype(F32)]
    unnamed x13 -> x9, waiting for transfers between devices: 3.23 us -> 19.2 us
  transfers between devices with their start and end apart: 14 -> 10, of which waited for: 12 -> 7; matrix products, arithmetic and copies ran while one was open for 12% -> 12% of each run, Pallas kernels for 0% -> 0%
where the time goes in v2:
time: 857 us; the launch traced here: 849 us
  Pallas kernels  304 us (35%)
  waiting for transfers between devices  302 us (35%)
  blocking collectives  79.4 us (9%)
  other arithmetic  62.1 us (7%)
  matrix products  47.3 us (6%)
  local copies, waits for them, and re-layouts  31.2 us (4%)
  between operations  15.7 us (2%)
    pallas_call x1, Pallas kernels, ffn_call(): pl.pallas_call(functools.partial(ffn_kernel, sizes), out_shape=[shape((ro...  304 us
    reduce_scatter x2, waiting for transfers between devices, reduced(): lax.psum_scatter(values.astype(BF16), GROUP, scatter_dimension=0, tiled=T...  186 us
    all_gather x2, waiting for transfers between devices, gather(): return lax.all_gather(values, GROUP, axis=0, tiled=True)  67.1 us
    all_gather x3, blocking collectives, gather(): return lax.all_gather(values, GROUP, axis=0, tiled=True)  53.9 us
    psum x1, waiting for transfers between devices, reduced(): return lax.psum(share, ('x', 'core')).astype(F32)  28.3 us
    unnamed x1, blocking collectives  19.4 us
    unnamed x9, waiting for transfers between devices  19.2 us
  transfers between devices with their start and end apart: 10, of which 7 were waited for; matrix products, arithmetic and copies ran while one was open for 12% of the time, Pallas kernels for 0%

profile of v2, /device:TPU:0, one launch (start us, length us, event | category | flops | bytes accessed | tf_op | source)
XLA Modules:
  0.0 848.6 jit_solution(3627182453709519983)
XLA Ops:
  9.0 4.9 collective-permute-start
  16.8 19.1 %all_gather.29 = bf16[1024,3]{0,1:T(4,128)(2,1)S(1)} all-gather(bf16[128,3]{0,1:T(4,128)(2,1)S(1)} %copy-done.14), channel_id=1, replica_groups=mesh['x'=2,'core'=2,'z'=4,'y'=2] {'z','y'}, dimensions={0}, use_global_device_ids=true | all-gather | bytes 6912 | tf_op jit(solution)/shard_map/all_gather | solution.py:561
  37.5 16.4 %all-gather.2 = bf16[8,1,128]{2,1,0:T(2,128)(2,1)S(1)} all-gather(bf16[1,1,128]{2,1,0:T(2,128)(2,1)S(1)} %bitcast.100), channel_id=1, replica_groups=mesh['x'=2,'core'=2,'z'=4,'y'=2] {'z','y'}, dimensions={0}, use_global_device_ids=true | all-gather | bytes 2304 | tf_op jit(solution)/shard_map/all_gather | solution.py:561
  53.9 18.4 %all-gather.3 = bf16[8,1,128]{2,1,0:T(2,128)(2,1)S(1)} all-gather(bf16[1,1,128]{2,1,0:T(2,128)(2,1)S(1)} %bitcast.101), channel_id=1, replica_groups=mesh['x'=2,'core'=2,'z'=4,'y'=2] {'z','y'}, dimensions={0}, use_global_device_ids=true | all-gather | bytes 2304 | tf_op jit(solution)/shard_map/all_gather | solution.py:561
  73.3 38.8 %all-gather.9.cloned.1.call-done = bf16[1024,3072]{1,0:T(8,128)(2,1)} async-done(((bf16[128,3072]{1,0:T(8,128)(2,1)}), bf16[1024,3072]{1,0:T(8,128)(2,1)}) %all-gather.9.cloned.1.call-update) | async-done | bytes 6291472 | tf_op jit(solution)/shard_map/all_gather | solution.py:561
  112.1 11.2 %fusion.11 = f32[16,66,3072]{2,1,0:T(8,128)S(1)} fusion(bf16[1024,3072]{1,0:T(8,128)(2,1)} %all-gather.9.cloned.1.call-done, f32[1024]{0:T(1024)S(1)} %bitcast.90, f32[16,66]{1,0:T(8,128)S(1)} %get-tuple-element.47, bf16[16,64,1024]{2,1,0:T(8,128)(2,1)S(1)} %copy-done.9, bf16[16,2,1024]{2,1,0:T(2,128)(2,1)S(1)} %collective-permute-done), kind=kOutput, calls=%fused_computation.12 | convolution fusion | flops 6651346944 | bytes 21438592 | tf_op jit(solution)/shard_map/dot_general | solution.py:525
  124.9 4.0 copy-done.1
  129.8 3.6 multiply_convert_fusion.5
  133.4 28.3 %all-gather.11.cloned.1.call-done = bf16[1024,1024]{1,0:T(8,128)(2,1)} async-done(((bf16[128,1024]{1,0:T(8,128)(2,1)}), bf16[1024,1024]{1,0:T(8,128)(2,1)}) %all-gather.11.cloned.1.call-update) | async-done | bytes 2097168 | tf_op jit(solution)/shard_map/all_gather | solution.py:561
  161.7 4.7 multiply_reduce_fusion.5
  170.1 303.6 %feed_forward.1 = (f32[1024,1024]{1,0:T(8,128)}, f32[1024,1024]{1,0:T(8,128)}, bf16[2,64,2304]{2,1,0:T(8,128)(2,1)}, bf16[576,512]{1,0:T(8,128)(2,1)}, bf16[9,2,...) custom-call(bf16[1024,1024]{1,0:T(8,128)(2,1)} %multiply_convert_fusion.4.n2_in, ...), custom_call_target="tpu_custom_call" | custom-call | tf_op jit(solution)/shard_map/feed_forward/pallas_call | solution.py:430
  473.8 4.7 multiply_reduce_fusion
  478.5 7.2 bitcast_add_fusion
  489.4 6.0 multiply_reduce_fusion.3
  497.9 6.7 convolution_convert_fusion
  507.3 3.8 multiply_convert_fusion
  512.8 3.9 fusion.19
  516.7 4.3 fusion.18
  522.4 9.6 %bitcast_convert_fusion = bf16[1024,3072]{1,0:T(8,128)(2,1)} fusion(bf16[16,64,1024]{2,1,0:T(8,128)(2,1)S(1)} %fusion.18, bf16[16,64,1024]{2,1,0:T(8,128)(2,1)S(1)} %copy-done.11, bf16[16,64,1024]{2,1,0:T(8,128)(2,1)S(1)} %get-tuple-element.33, bf16[16,66,1024]{2,1,0:T(8,128)(2,1)S(1)} %get-tuple-element.42), kind=kOutput, calls=%fused_computation | convolution fusion | flops 6464471040 | bytes 14680064 | tf_op jit(solution)/shard_map/dot_general | solution.py:513
  533.9 5.3 slice.102
  539.3 17.4 %reduce-scatter.10.cloned.1.call-done = bf16[128,3]{1,0:T(8,128)(2,1)} async-done(((bf16[1024,3]{1,0:T(8,128)(2,1)}), bf16[128,3]{1,0:T(8,128)(2,1)}) %reduce-scatter.10.cloned.1.call-update) | async-done | bytes 784
  557.5 12.7 %fusion.25 = (bf16[1024]{0:T(1024)(128)(2,1)S(1)}, f32[1024]{0:T(1024)S(1)}, f32[1024,1024]{1,0:T(8,128)}) fusion(f32[16,64,1024]{2,1,0:T(8,128)} %slice.102, f32[1024]{0:T(1024)S(1)} %bitcast.92, bf16[1024,3072]{1,0:T(8,128)(2,1)} %all-gather.9.cloned.1.call-done, bf16[1024,1024]{1,0:T(8,128)(2,1)} %bitcast.84, bf16[1024,1024]{1,0:T(8,128)(2,1)S(1)} %bitcast.81, ...), kind=kOutput, calls=%fused_computation.40 | convolution fusion | flops 6466566144 | bytes 20981760 | tf_op jit(solution)/shard_map/dot_general | solution.py:519
  570.3 19.4 %all-reduce.2 = (bf16[1024]{0:T(1024)(128)(2,1)S(1)}, bf16[1024]{0:T(1024)(128)(2,1)S(1)}) all-reduce(bf16[1024]{0:T(1024)(128)(2,1)S(1)} %get-tuple-element.23, bf16[1024]{0:T(1024)(128)(2,1)S(1)} %get-tuple-element.21), channel_id=4, replica_groups=mesh['x'=2,'core'=2,'z'=4,'y'=2] {'z','y'}, use_global_device_ids=true, to_apply=%region_6.7.clone | all-reduce | flops 2048 | bytes 8192
  589.8 6.1 all-reduce.3
  597.5 5.7 fusion.24
  603.5 2.5 multiply_convert_fusion.1
  609.3 4.3 convert_bitcast_fusion
  613.6 65.2 %reduce-scatter.8.cloned.1.call-done = bf16[128,1024]{1,0:T(8,128)(2,1)} async-done(((bf16[1024,1024]{1,0:T(8,128)(2,1)}), bf16[128,1024]{1,0:T(8,128)(2,1)}) %reduce-scatter.8.cloned.1.call-update) | async-done | bytes 262160 | tf_op jit(solution)/shard_map/reduce_scatter | solution.py:635
  678.8 120.6 %reduce-scatter.6.cloned.1.call-done = bf16[128,3072]{1,0:T(8,128)(2,1)} async-done(((bf16[1024,3072]{1,0:T(8,128)(2,1)}), bf16[128,3072]{1,0:T(8,128)(2,1)}) %reduce-scatter.6.cloned.1.call-update) | async-done | bytes 786448 | tf_op jit(solution)/shard_map/reduce_scatter | solution.py:635
  799.4 2.7 fusion.34
  808.9 28.3 %all-reduce.7.cloned.1.call-done = (bf16[128,3072]{1,0:T(8,128)(2,1)}, bf16[128,1024]{1,0:T(8,128)(2,1)}) async-done(((bf16[128,3072]{1,0:T(8,128)(2,1)}, bf16[128,1024]{1,0:T(8,128)(2,1)}), (bf16[128,3072]{1,0:T(8,128)(2,1)}, bf16[128,1024]{1,0:T(8,128)(2,1)})) %all-reduce.7.cloned.1.call-update) | async-done | bytes 1048592 | tf_op jit(solution)/shard_map/psum | solution.py:636
  837.1 2.4 convert_element_type.116
  (102 shorter events, 41.2 us)
Async XLA Ops:
  7.2 9.6 %copy-start.14 = (bf16[128,3]{0,1:T(4,128)(2,1)S(1)}, bf16[128,3]{0,1:T(4,128)(2,1)}, u32[]{:S(2)}) copy-start(bf16[128,3]{0,1:T(4,128)(2,1)} %param.18) | copy-start | bytes 2308
  7.2 104.9 %all-gather.9.cloned.1.call-start = ((), (), s32[]{:S(2)}) async-start(), calls=%async_computation.3 | async-start | bytes 7077888 | tf_op jit(solution)/shard_map/all_gather | solution.py:561
  7.9 153.8 %all-gather.11.cloned.1.call-start = ((), (), s32[]{:S(2)}) async-start(), calls=%async_computation.4 | async-start | bytes 2359296 | tf_op jit(solution)/shard_map/all_gather | solution.py:561
  9.0 63.4 %collective-permute-start = (bf16[16,2,1024]{2,1,0:T(2,128)(2,1)S(1)}, bf16[16,2,1024]{2,1,0:T(2,128)(2,1)S(1)}, u32[]{:S(2)}, u32[]{:S(2)}) collective-permute-start(bf16[16,2,1024]{2,1,0:T(2,128)(2,1)S(1)} %slice.67), channel_id=1, source_target_pairs={{0,1},{1,2},{2,3},{3,4},{4,5},{5,6},{6,7},{8,9},{9,10},{10,11},{11... | collective-permute-start | bytes 196616 | tf_op jit(solution)/shard_map/ppermute | solution.py:539
  13.9 542.8 %reduce-scatter.10.cloned.1.call-start = ((), (), s32[]{:S(2)}) async-start(), calls=%async_computation.9 | async-start | bytes 294912
  16.7 56.6 %copy-start.2 = (f32[16,64,1024]{2,1,0:T(8,128)}, f32[16,64,1024]{2,1,0:T(8,128)S(1)}, u32[]{:S(2)}) copy-start(f32[16,64,1024]{2,1,0:T(8,128)S(1)} %convert_multiply_fusion.2) | copy-start | bytes 12582916
  16.8 20.8 %copy-start.15 = (bf16[128]{0:T(256)(128)(2,1)S(1)}, bf16[128]{0:T(256)(128)(2,1)}, u32[]{:S(2)}) copy-start(bf16[128]{0:T(256)(128)(2,1)} %param.16) | copy-start | bytes 772
  16.8 37.2 %copy-start.16 = (bf16[128]{0:T(256)(128)(2,1)S(1)}, bf16[128]{0:T(256)(128)(2,1)}, u32[]{:S(2)}) copy-start(bf16[128]{0:T(256)(128)(2,1)} %param.20) | copy-start | bytes 772
  16.8 55.6 %copy-start.9 = (bf16[16,64,1024]{2,1,0:T(8,128)(2,1)S(1)}, bf16[16,64,1024]{2,1,0:T(8,128)(2,1)}, u32[]{:S(2)}) copy-start(bf16[16,64,1024]{2,1,0:T(8,128)(2,1)} %param.12) | copy-start | bytes 6291460
  123.3 5.6 copy-start.1
  124.9 4.9 copy-start
  166.4 1.9 copy-start.4
  473.8 4.7 copy-start.3
  473.8 14.4 %slice-start = ((s8[4718592]{0:T(1024)(128)(4,1)}), s8[4194304]{0:T(1024)(128)(4,1)S(1)}, s32[]{:S(2)}) async-start(s8[4718592]{0:T(1024)(128)(4,1)} %bitcast.71), calls=%async_computation.11 | async-start | bytes 8388608
  478.5 7.3 copy-start.17
  478.5 9.7 %slice-start.1 = ((s8[4718592]{0:T(1024)(128)(4,1)}), s8[524288]{0:T(1024)(128)(4,1)S(1)}, s32[]{:S(2)}) async-start(s8[4718592]{0:T(1024)(128)(4,1)} %bitcast.71), calls=%async_computation.12 | async-start | bytes 1048576
  485.7 2.4 copy-start.7
  485.7 3.7 copy-start.8
  496.4 109.6 %all-gather.15.cloned.1.call-start = ((), (), s32[]{:S(2)}) async-start(), calls=%async_computation.8 | async-start | bytes 2949120 | tf_op jit(solution)/shard_map/all_gather | solution.py:657
  497.0 112.3 %all-gather.13.cloned.1.call-start = ((), (), s32[]{:S(2)}) async-start(), calls=%async_computation.7 | async-start | bytes 2949120 | tf_op jit(solution)/shard_map/all_gather | solution.py:654
  497.6 9.7 %copy-start.10 = (bf16[16,64,1024]{2,1,0:T(8,128)(2,1)S(1)}, bf16[16,64,1024]{2,1,0:T(8,128)(2,1)}, u32[]{:S(2)}) copy-start(bf16[16,64,1024]{2,1,0:T(8,128)(2,1)} %param.12) | copy-start | bytes 6291460
  497.6 181.2 %reduce-scatter.8.cloned.1.call-start = ((), (), s32[]{:S(2)}) async-start(), calls=%async_computation.6 | async-start | bytes 2359296 | tf_op jit(solution)/shard_map/reduce_scatter | solution.py:635
  504.5 294.8 %reduce-scatter.6.cloned.1.call-start = ((), (), s32[]{:S(2)}) async-start(), calls=%async_computation.5 | async-start | bytes 7077888 | tf_op jit(solution)/shard_map/reduce_scatter | solution.py:635
  505.7 7.1 copy-start.5
  505.7 7.1 collective-permute-start.1
  516.7 4.4 copy-start.13
  516.7 5.7 copy-start.11
  521.1 1.3 copy-start.12
  532.0 0.7 copy-start.18
  532.0 305.1 %all-reduce.7.cloned.1.call-start = ((), (), s32[]{:S(2)}) async-start(), calls=%async_computation.10 | async-start | bytes 2097152 | tf_op jit(solution)/shard_map/psum | solution.py:636
  597.5 5.9 copy-start.6
Sparse Core Ops, SparseCore 0:
  10.2 101.8 all-gather.8
  114.2 47.4 all-gather.10
  496.5 60.1 reduce-scatter.9
  558.1 23.0 all-gather.14
  582.7 24.1 all-gather.12
  610.9 67.8 reduce-scatter.7
  682.3 116.9 reduce-scatter.5
  801.7 35.3 all-reduce.6

commit v3 on v1

v3 whole, which is shorter than its diff:
```python
import functools
import jax
import jax.numpy as jnp
from jax import lax
from jax.experimental import pallas as pl
from jax.experimental.pallas import tpu as pltpu
from jax.sharding import Mesh, PartitionSpec as P

EPS = 1e-05
F32 = jnp.float32
BF16 = jnp.bfloat16
NT = (((1,), (1,)), ((), ()))
TN = (((0,), (0,)), ((), ()))
MESH = pl.DeviceIdType.MESH
GROUP = ("z", "y")
CHUNK = 256
BLOCK = 128
TILE = 256
EDGE = 8
LAG = 1
AHEAD = 4
RELAY = 2


def dot(left, right):
    return jnp.dot(left, right, preferred_element_type=F32)


def dot_nt(left, right):
    return lax.dot_general(left, right, NT, preferred_element_type=F32)


def dot_tn(left, right):
    return lax.dot_general(left, right, TN, preferred_element_type=F32)


def row_scale(values):
    return lax.rsqrt(jnp.mean(values * values, axis=-1, keepdims=True) + EPS)


def block_kernel(
    sizes,
    tok_in, edge_in, cot_in, live_in, small_in, in_in, out_in, gate_in, up_in, down_in,
    y_out, dx_out, gu_full, down_full, in_full, out_full, small_out,
    all_gu, all_down, all_in, all_out, spill_p, spill_h, spill_t,
    act_a, act_b, tr, wgu, wd, outv, dnv, acts, wout, zv, take, og,
    ub, vb, hal, uh, kh, ks, chd, hf, smallv, vec, conv_acc, sg,
    ggu, gd, rxg, rxd, s1g, s1d, ryg, ryd, s2g, s2d, rzg, rzd, fing, find,
    sem_in, sem_load, sem_own, sem_pair, sem_small, sem_edge, sem_kh, sem_spill,
    ag_z, ag_y, ag_dz, ag_dy, ag_send, ag_relay, ag_dsend, ag_drelay,
    mg_own, mg_z, mg_y, mg_oz, mg_oy, mg_send, mg_relay, mg_osend, mg_orelay,
    rx_g, rx_d, ry_g, ry_d, rz_g, rz_d, sx_g, sx_d, sy_g, sy_d, sz_g, sz_d,
    sem_fin, fs_g, fs_d, fr_g, fr_i, fr_d, fr_o,
):
    nx, nz, ny, seqs, span, width, hidden = sizes
    n = nz * ny
    rows = seqs * span
    dn = width // n
    dnx = dn // nx
    half = hidden // 2
    chan = width // 2
    steps = half // CHUNK
    chunks = steps + 3
    per_half = half // BLOCK // 2
    own_rows = hidden // n
    gp = min(BLOCK, own_rows & -own_rows)
    pieces = CHUNK // gp
    lanes = width // nx
    slots = 2 * LAG
    tiles = rows // TILE
    tseq = TILE // span
    x, c = lax.axis_index("x"), lax.axis_index("core")
    z, y = lax.axis_index("z"), lax.axis_index("y")
    me = z * ny + y
    in_half = me // (n // 2) == c

    def at(x=x, c=c, z=z, y=y):
        return (x, c, z, y)

    def member(j, c=c):
        return at(c=c, z=j // ny, y=j % ny)

    def zp(d):
        return lax.rem(z + d, nz)

    def yp(d):
        return lax.rem(y + d, ny)

    def xp(d):
        return lax.rem(x + d, nx)

    def remote(src, dst, ssem, rsem, dev):
        return pltpu.make_async_remote_copy(
            src_ref=src, dst_ref=dst, send_sem=ssem, recv_sem=rsem, device_id=dev, device_id_type=MESH
        )

    def local(src, dst, sem):
        return pltpu.make_async_copy(src, dst, sem)

    def landed(ref, sem):
        pltpu.make_async_copy(ref, ref, sem).wait()

    def span_of(start, size, align):
        return pl.ds(pl.multiple_of(start, align), size)

    mine = span_of(c * rows, rows, rows)
    other = span_of((1 - c) * rows, rows, rows)

    barrier = pltpu.get_barrier_semaphore()
    peers = [member(lax.rem(me + d, n)) for d in range(1, n)]
    reps = [(d, e) for d in range(nx) for e in range(2) if d + e > 0]
    peers += [at(x=xp(d), c=lax.rem(c + e, 2)) for d, e in reps]
    peers += [member(lax.rem(me + d, n), c=1 - c) for d in (1, n - 1)]
    for dev in peers:
        pl.semaphore_signal(barrier, inc=1, device_id=dev, device_id_type=MESH)
    pl.semaphore_wait(barrier, len(peers))

    local(small_in, smallv.at[me], sem_small.at[0]).start()
    for d in range(1, n):
        remote(small_in, smallv.at[me], sem_small.at[1], sem_small.at[2], member(lax.rem(me + d, n))).start()

    @pl.when(me < n - 1)
    def _():
        for e in range(2):
            src = edge_in.at[:, pl.ds(span - EDGE, EDGE)]
            dev = member(lax.rem(me + 1, n), c=lax.rem(c + e, 2))
            remote(src, hal.at[c], sem_edge.at[e], sem_edge.at[2 + c], dev).start()

    local(tok_in, act_a.at[mine], sem_in.at[0]).start()
    local(cot_in, take.at[1], sem_in.at[1]).start()
    remote(tok_in, act_a.at[mine], sem_pair.at[0], sem_pair.at[1], at(c=1 - c)).start()

    ag_peers = [(0, d) for d in range(1, nz)] + [(1, d) for d in range(1, ny)]

    def toward(ax, d):
        return at(z=zp(d)) if ax == 0 else at(y=yp(d))

    for b in range(6):
        here = in_in.at[:, span_of((b // 2) * width + c * chan + (b % 2) * CHUNK, CHUNK, CHUNK)]
        there = all_in.at[b, z, y]
        local(here, there, mg_own.at[0]).start()
        for p, (ax, d) in enumerate(ag_peers):
            remote(here, there, mg_send.at[p], (mg_z, mg_y)[ax].at[d - 1], toward(ax, d)).start()

    @pl.when(in_half)
    def _():
        o = me - c * (n // 2)
        local(out_in, all_out.at[o], mg_own.at[1]).start()
        for p, (ax, d) in enumerate(ag_peers):
            remote(out_in, all_out.at[o], mg_osend.at[p], (mg_oz, mg_oy)[ax].at[o], toward(ax, d)).start()

    def out_owner(o):
        j = c * (n // 2) + o
        return j // ny, j % ny

    def mixer_second_hop():
        for d in range(1, nz):
            zs = lax.rem(z - d + nz, nz)
            block = all_in.at[:, zs, y]
            landed(block, mg_z.at[d - 1])
            for e in range(1, ny):
                remote(block, block, mg_relay.at[d - 1, e - 1], mg_y.at[e - 1], at(y=yp(e))).start()
        for o in range(n // 2):
            zo, yo = out_owner(o)

            @pl.when(jnp.logical_and(zo != z, yo == y))
            def _():
                landed(all_out.at[o], mg_oz.at[o])
                for e in range(1, ny):
                    remote(all_out.at[o], all_out.at[o], mg_orelay.at[o, e - 1], mg_oy.at[o], at(y=yp(e))).start()

    def mixer_arrived():
        for e in range(1, ny):
            landed(all_in.at[:, :, lax.rem(y - e + ny, ny)], mg_y.at[e - 1])
        for o in range(n // 2):
            _, yo = out_owner(o)

            @pl.when(yo != y)
            def _():
                landed(all_out.at[o], mg_oy.at[o])

        landed(all_in.at[:, 0, 0], mg_own.at[0])

        @pl.when(in_half)
        def _():
            landed(all_out.at[0], mg_own.at[1])

    def mixer_load():
        copies = [local(all_in, acts, sem_load.at[0])]
        copies += [local(all_out.at[o], wout.at[pl.ds(o * dn, dn)], sem_load.at[2 + o]) for o in range(n // 2)]
        for copy in copies:
            copy.start()
        for copy in copies:
            copy.wait()

    def blocks(m):
        h, i = m % 2, m // 2
        first = per_half * h + i
        return first, per_half * h + per_half - 1 - i + per_half * (m // (2 * (per_half // 2)))

    def column(b):
        return pl.multiple_of(c * half + b * BLOCK, BLOCK)

    def owner(m, q):
        b = blocks(m)[q * gp // BLOCK]
        row = c * half + b * BLOCK + (q * gp) % BLOCK
        j = row // own_rows
        return j // ny, j % ny, pl.multiple_of(row - j * own_rows, gp)

    def grad_owner(m, q):
        zo, yo, row = owner(jnp.minimum(m, steps - 1), q)
        mixed = c * chan + jnp.maximum(m - steps, 0) * CHUNK + q * gp
        j = mixed // dn
        late = m >= steps
        return (
            jnp.where(late, j // ny, zo),
            jnp.where(late, j % ny, yo),
            pl.multiple_of(jnp.where(late, mixed - j * dn, row), gp),
        )

    def first_hop(m):
        b = blocks(m)
        for k in range(2):
            for w, src in enumerate((gate_in, up_in)):
                here = src.at[:, pl.ds(column(b[k]), BLOCK)]
                there = all_gu.at[m, w, z, y, :, pl.ds(k * BLOCK, BLOCK)]
                local(here, there, sem_own.at[0, m]).start()
                for p, (ax, d) in enumerate(ag_peers):
                    remote(here, there, ag_send.at[p], (ag_z, ag_y)[ax].at[m, d - 1], toward(ax, d)).start()
        for q in range(pieces):
            zo, yo, row = owner(m, q)

            @pl.when(jnp.logical_and(zo == z, yo == y))
            def _():
                here = down_in.at[pl.ds(row, gp)]
                there = all_down.at[m, pl.ds(q * gp, gp)]
                local(here, there, sem_own.at[1, m * pieces + q]).start()
                for p, (ax, d) in enumerate(ag_peers):
                    remote(here, there, ag_dsend.at[p], (ag_dz, ag_dy)[ax].at[m, q], toward(ax, d)).start()

    def second_hop(m):
        for d in range(1, nz):
            zs = lax.rem(z - d + nz, nz)
            block = all_gu.at[m, :, zs, y]
            landed(block, ag_z.at[m, d - 1])
            for e in range(1, ny):
                remote(block, block, ag_relay.at[d - 1, e - 1], ag_y.at[m, e - 1], at(y=yp(e))).start()
        for q in range(pieces):
            zo, yo, _ = owner(m, q)

            @pl.when(jnp.logical_and(zo != z, yo == y))
            def _():
                block = all_down.at[m, pl.ds(q * gp, gp)]
                landed(block, ag_dz.at[m, q])
                for e in range(1, ny):
                    remote(block, block, ag_drelay.at[zo % 2, e - 1], ag_dy.at[m, q], at(y=yp(e))).start()

    def load(m):
        landed(all_gu.at[m, :, 0, 0], sem_own.at[0, m])
        for e in range(1, ny):
            landed(all_gu.at[m, :, :, lax.rem(y - e + ny, ny)], ag_y.at[m, e - 1])
        for q in range(pieces):
            zo, yo, _ = owner(m, q)
            block = all_down.at[m, pl.ds(q * gp, gp)]

            @pl.when(jnp.logical_and(zo == z, yo == y))
            def _():
                landed(block, sem_own.at[1, m * pieces + q])

            @pl.when(yo != y)
            def _():
                landed(block, ag_dy.at[m, q])

        a = local(all_gu.at[m], wgu, sem_load.at[0])
        b = local(all_down.at[m], wd, sem_load.at[1])
        a.start()
        b.start()
        a.wait()
        b.wait()

    local(cot_in, take.at[1], sem_in.at[1]).wait()

    @pl.loop(0, tiles)
    def _(t):
        rl = span_of(t * TILE, TILE, TILE)
        rs = span_of(c * rows + t * TILE, TILE, TILE)
        act_b[rs, :] = (take[1, rl, :].astype(F32) * live_in[rl, :]).astype(BF16)

    remote(act_b.at[mine], act_b.at[mine], sem_pair.at[2], sem_pair.at[3], at(c=1 - c)).start()

    landed(small_in, sem_small.at[0])
    landed(smallv.at[pl.ds(0, n - 1)], sem_small.at[1])
    landed(smallv.at[pl.ds(0, n - 1)], sem_small.at[2])
    for j in range(n):
        vec[:, j * dn : (j + 1) * dn] = smallv[j]

    @pl.when(me < n - 1)
    def _():
        for e in range(2):
            landed(hal.at[0], sem_edge.at[e])

    @pl.when(me > 0)
    def _():
        for e in range(2):
            landed(hal.at[e], sem_edge.at[2 + e])

    @pl.when(me == 0)
    def _():
        hal[...] = jnp.zeros_like(hal)

    mixer_second_hop()
    first_hop(0)
    first_hop(1)
    local(tok_in, act_a.at[mine], sem_in.at[0]).wait()
    landed(act_a.at[mine], sem_pair.at[0])
    landed(act_a.at[other], sem_pair.at[1])
    local(act_a.at[other], spill_t, sem_spill.at[6]).start()
    mixer_arrived()
    mixer_load()

    def win(b):
        return acts[b].reshape(width, CHUNK)

    def tap(k, h):
        return vec[2 + k : 3 + k, span_of(c * chan + h * CHUNK, CHUNK, CHUNK)].reshape(1, 1, CHUNK)

    def normed(tokens):
        return (tokens * row_scale(tokens) * vec[0:1, :]).astype(BF16)

    for cc in range(2):
        edge = normed(hal[cc].astype(F32).reshape(seqs * EDGE, width))
        for h in range(2):
            product = dot(edge, win(h)) * dot(edge, win(4 + h))
            uh[cc * seqs : (cc + 1) * seqs, :, h * CHUNK : (h + 1) * CHUNK] = product.reshape(seqs, EDGE, CHUNK)

    def convolve(product, first, h):
        ub[:, :EDGE, :] = uh[pl.ds(first, tseq), :, h * CHUNK : (h + 1) * CHUNK]
        ub[:, EDGE:, :] = product.reshape(tseq, span, CHUNK)
        lag_two = ub[:, EDGE - 2 : EDGE - 2 + span, :]
        lag_one = ub[:, EDGE - 1 : EDGE - 1 + span, :]
        lag_none = ub[:, EDGE:, :]
        return lag_two, lag_one, lag_none, tap(0, h) * lag_two + tap(1, h) * lag_one + tap(2, h) * lag_none

    def spilled(t, i, rs):
        slot = t % 2
        src = dnv.at[span_of(slot * 3 * TILE + i * TILE, TILE, TILE), pl.ds(0, chan)]
        return local(src, spill_p.at[i, rs], sem_spill.at[slot * 3 + i])

    def tile_start(t):
        return lax.rem(t + (1 - c) * tiles, 2 * tiles) * TILE

    @pl.loop(0, 2 * tiles)
    def _(t):
        start = tile_start(t)
        rs = span_of(start, TILE, TILE)
        first = start // span
        tokens = act_a[rs, :].astype(F32)
        n1 = normed(tokens)

        @pl.when(t >= 2)
        def _():
            for i in range(3):
                spilled(t, i, rs).wait()

        for h in range(2):
            parts = [dot(n1, win(2 * i + h)) for i in range(3)]
            hl = pl.ds(h * CHUNK, CHUNK)
            for i in range(3):
                dnv[span_of((t % 2) * 3 * TILE + i * TILE, TILE, TILE), hl] = parts[i]
            chd[pl.ds(first, tseq), :, hl] = parts[1].reshape(tseq, span, CHUNK)[:, :EDGE]
            conv = convolve(parts[0] * parts[2], first, h)[3].reshape(TILE, CHUNK)
            zv[rs, hl] = (parts[1] * conv).astype(BF16)
        for i in range(3):
            spilled(t, i, rs).start()
        mixed = dot(zv[rs, :], wout[...])

        @pl.when(t < tiles)
        def _():
            tr[span_of(t * TILE, TILE, TILE), pl.ds(0, width)] = mixed.astype(BF16)

        @pl.when(t >= tiles)
        def _():
            outv[rs, :] = act_a[rs, :].astype(F32) + mixed

        @pl.when(t == tiles - 1)
        def _():
            landed(act_a.at[other], sem_spill.at[6])
            remote(tr.at[:, pl.ds(0, width)], take.at[0], sem_pair.at[4], sem_pair.at[5], at(c=1 - c)).start()

    first_hop(2)
    second_hop(0)
    for slot in range(2):
        for i in range(3):
            spilled(slot, i, pl.ds(0, TILE)).wait()
    landed(take.at[0], sem_pair.at[5])

    @pl.loop(0, tiles)
    def _(t):
        rs = span_of(c * rows + t * TILE, TILE, TILE)
        middle = outv[rs, :] + take[0, span_of(t * TILE, TILE, TILE), :].astype(F32)
        outv[rs, :] = middle
        act_a[rs, :] = (middle * row_scale(middle) * vec[1:2, :]).astype(BF16)

    remote(act_a.at[mine], act_a.at[mine], sem_pair.at[6], sem_pair.at[7], at(c=1 - c)).start()
    local(outv.at[mine], spill_h, sem_spill.at[7]).start()
    landed(take.at[0], sem_pair.at[4])
    first_hop(3)
    second_hop(1)

    @pl.loop(0, tiles)
    def _(t):
        ro = span_of((1 - c) * rows + t * TILE, TILE, TILE)
        rs = span_of(c * rows + t * TILE, TILE, TILE)
        outv[ro, :] = jnp.zeros((TILE, width), F32)
        dnv[ro, :] = jnp.zeros((TILE, width), F32)
        dnv[rs, :] = jnp.zeros((TILE, width), F32)

    landed(act_a.at[other], sem_pair.at[7])
    landed(act_a.at[mine], sem_pair.at[6])
    landed(act_b.at[other], sem_pair.at[3])
    landed(act_b.at[mine], sem_pair.at[2])

    @pl.loop(0, 2 * tiles)
    def _(t):
        rs = span_of(t * TILE, TILE, TILE)
        tr[:, rs] = act_a[rs, :].T

    local(outv.at[mine], spill_h, sem_spill.at[7]).wait()
    load(0)

    big = 512
    zb = big // (ny * dn)

    def hid(w):
        return acts[2 * w : 2 * w + 2].reshape(2 * rows, CHUNK)

    def compute(m):
        slot = m % slots

        @pl.loop(0, 2 * rows // big)
        def _(r):
            rs = span_of(r * big, big, big)
            gate = wgu[0].reshape(width, CHUNK)
            up = wgu[1].reshape(width, CHUNK)
            n2r = act_a[rs, :]
            g = dot(n2r, gate)
            v = dot(n2r, up)
            s = jax.nn.sigmoid(g)
            sg_ = g * s
            q = (sg_ * v).astype(BF16)
            dq = dot_nt(act_b[rs, :], wd[...])
            gg = (dq * v * s * (1.0 + g * (1.0 - s))).astype(BF16)
            gv = (dq * sg_).astype(BF16)
            zi = pl.ds((r % 2) * zb, zb)
            for w, value in enumerate((q, gg, gv)):
                acts[2 * w + r // 2, zi] = value.reshape(zb, ny, dn, CHUNK)
            outv[rs, :] += dot(q, wd[...])
            dnv[rs, :] += dot_nt(gg, gate) + dot_nt(gv, up)

        weight_grads(slot, hid(1), hid(2))
        for h in range(nx):
            gd[slot, h] = dot_tn(hid(0), act_b[:, pl.ds(h * lanes, lanes)]).astype(BF16)

    def weight_grads(slot, first, second):
        group = n // 4

        @pl.loop(0, 4)
        def _(t):
            a = tr[span_of(t * TILE, TILE, TILE), :]
            for w, src in enumerate((first, second)):
                full = dot(a, src).astype(BF16).reshape(group, nx, dnx, CHUNK)
                for h in range(nx):
                    for k in range(group):
                        j = t * group + k
                        ggu[slot, w, h, j // ny, j % ny] = full[k, h]

    def send_x(m):
        slot = m % slots
        for d in range(1, nx):
            xo = xp(d)
            remote(ggu.at[slot, :, xo], rxg.at[slot, d - 1], sx_g.at[slot, d - 1], rx_g.at[slot, d - 1], at(x=xo)).start()

            @pl.when(m < chunks - 1)
            def _():
                remote(gd.at[slot, xo], rxd.at[slot, d - 1], sx_d.at[slot, d - 1], rx_d.at[slot, d - 1], at(x=xo)).start()

    def send_y(m):
        slot = m % slots
        for d in range(1, nx):
            landed(rxg.at[slot, d - 1], rx_g.at[slot, d - 1])
            landed(rxg.at[slot, d - 1], sx_g.at[slot, d - 1])

        @pl.loop(0, nz)
        def _(zi):
            for yi in range(ny):
                for w in range(2):
                    total = ggu[slot, w, x, zi, yi].astype(F32)
                    for d in range(1, nx):
                        total += rxg[slot, d - 1, w, zi, yi].astype(F32)
                    s1g[slot, yi, w, zi] = total.astype(BF16)

        for d in range(1, ny):
            yo = yp(d)
            remote(s1g.at[slot, yo], ryg.at[slot, d - 1], sy_g.at[slot, d - 1], ry_g.at[slot, d - 1], at(y=yo)).start()

        @pl.when(m < chunks - 1)
        def _():
            for d in range(1, nx):
                landed(rxd.at[slot, d - 1], rx_d.at[slot, d - 1])
                landed(rxd.at[slot, d - 1], sx_d.at[slot, d - 1])
            total = gd[slot, x].astype(F32)
            for d in range(1, nx):
                total += rxd[slot, d - 1].astype(F32)
            s1d[slot] = total.astype(BF16)
            for q in range(pieces):
                _, yo, _ = grad_owner(m, q)
                part = pl.ds(q * gp, gp)

                @pl.when(yo != y)
                def _():
                    d = lax.rem(yo - y + ny, ny)
                    remote(
                        s1d.at[slot, part], ryd.at[slot, d - 1, part], sy_d.at[slot, q], ry_d.at[slot, d - 1, q], at(y=yo)
                    ).start()

    def send_z(m):
        slot = m % slots
        for d in range(1, ny):
            landed(ryg.at[slot, d - 1], ry_g.at[slot, d - 1])
            landed(ryg.at[slot, d - 1], sy_g.at[slot, d - 1])
        for zi in range(nz):
            for w in range(2):
                total = s1g[slot, y, w, zi].astype(F32)
                for d in range(1, ny):
                    total += ryg[slot, d - 1, w, zi].astype(F32)
                s2g[slot, zi, w] = total.astype(BF16)
        for d in range(1, nz):
            zo = zp(d)
            remote(s2g.at[slot, zo], rzg.at[slot, d - 1], sz_g.at[slot, d - 1], rz_g.at[slot, d - 1], at(z=zo)).start()

        @pl.when(m < chunks - 1)
        def _():
            for q in range(pieces):
                zo, yo, _ = grad_owner(m, q)
                part = pl.ds(q * gp, gp)

                @pl.when(yo != y)
                def _():
                    landed(s1d.at[slot, part], sy_d.at[slot, q])

                @pl.when(yo == y)
                def _():
                    total = s1d[slot, part].astype(F32)
                    for d in range(1, ny):
                        landed(ryd.at[slot, d - 1, part], ry_d.at[slot, d - 1, q])
                        total += ryd[slot, d - 1, part].astype(F32)
                    s2d[slot, part] = total.astype(BF16)

                    @pl.when(zo != z)
                    def _():
                        d = lax.rem(zo - z + nz, nz)
                        remote(
                            s2d.at[slot, part], rzd.at[slot, d - 1, part], sz_d.at[slot, q], rz_d.at[slot, d - 1, q], at(z=zo)
                        ).start()

    def rep(p):
        d, e = reps[p]
        return at(x=xp(d), c=lax.rem(c + e, 2))

    def finals_left(m):
        landed(fing, sem_fin.at[0])
        for p in range(len(reps)):
            landed(fing, fs_g.at[p])

        @pl.when(m < chunks - 1)
        def _():
            for q in range(pieces):
                zo, yo, _ = grad_owner(m, q)
                part = pl.ds(q * gp, gp)

                @pl.when(jnp.logical_and(yo == y, zo == z))
                def _():
                    landed(find.at[part], sem_fin.at[1 + q])
                    for p in range(len(reps)):
                        landed(find.at[part], fs_d.at[p, q])

    def finish(m):
        slot = m % slots

        @pl.when(m > 0)
        def _():
            finals_left(m - 1)

        for d in range(1, nz):
            landed(rzg.at[slot, d - 1], rz_g.at[slot, d - 1])
            landed(rzg.at[slot, d - 1], sz_g.at[slot, d - 1])
        for w in range(2):
            total = s2g[slot, z, w].astype(F32)
            for d in range(1, nz):
                total += rzg[slot, d - 1, w].astype(F32)
            fing[w] = total.astype(BF16)

        @pl.when(m < steps)
        def _():
            b = blocks(m)
            for k in range(2):
                here = fing.at[:, :, pl.ds(k * BLOCK, BLOCK)]
                there = gu_full.at[x, c, :, :, span_of(b[k] * BLOCK, BLOCK, BLOCK)]
                local(here, there, sem_fin.at[0]).start()
                for p in range(len(reps)):
                    remote(here, there, fs_g.at[p], fr_g.at[p], rep(p)).start()

        @pl.when(m >= steps)
        def _():
            there = in_full.at[x, c, pl.ds(2 * (m - steps), 2)]
            local(fing, there, sem_fin.at[0]).start()
            for p in range(len(reps)):
                remote(fing, there, fs_g.at[p], fr_i.at[p], rep(p)).start()

        @pl.when(m < chunks - 1)
        def _():
            for q in range(pieces):
                zo, yo, row = grad_owner(m, q)
                part = pl.ds(q * gp, gp)

                @pl.when(jnp.logical_and(yo == y, zo != z))
                def _():
                    landed(s2d.at[slot, part], sz_d.at[slot, q])

                @pl.when(jnp.logical_and(yo == y, zo == z))
                def _():
                    total = s2d[slot, part].astype(F32)
                    for d in range(1, nz):
                        landed(rzd.at[slot, d - 1, part], rz_d.at[slot, d - 1, q])
                        total += rzd[slot, d - 1, part].astype(F32)
                    find[part] = total.astype(BF16)

                    @pl.when(m < steps)
                    def _():
                        there = down_full.at[x, pl.ds(row, gp)]
                        local(find.at[part], there, sem_fin.at[1 + q]).start()
                        for p in range(len(reps)):
                            remote(find.at[part], there, fs_d.at[p, q], fr_d.at[p], rep(p)).start()

                    @pl.when(m >= steps)
                    def _():
                        there = out_full.at[x, pl.ds(row, gp)]
                        local(find.at[part], there, sem_fin.at[1 + q]).start()
                        for p in range(len(reps)):
                            remote(find.at[part], there, fs_d.at[p, q], fr_o.at[p], rep(p)).start()

    def give_sums():
        for i, src in enumerate((dnv, outv)):
            side = pl.ds((1 - i) * width, width)

            @pl.loop(0, tiles)
            def _(t):
                ro = span_of((1 - c) * rows + t * TILE, TILE, TILE)
                tr[span_of(t * TILE, TILE, TILE), side] = src[ro, :].astype(BF16)

            remote(tr.at[:, side], take.at[1 - i], sem_pair.at[8 + 2 * i], sem_pair.at[9 + 2 * i], at(c=1 - c)).start()
        local(spill_h, outv.at[other], sem_spill.at[7]).start()
        local(tok_in, act_a.at[mine], sem_in.at[0]).start()
        local(spill_t, act_a.at[other], sem_spill.at[6]).start()

    def loaded(t, i):
        src = spill_p.at[i, span_of(t * TILE, TILE, TILE)]
        dst = dnv.at[span_of((1 - c) * rows + i * TILE, TILE, TILE), span_of((t % 2) * chan, chan, chan)]
        return local(src, dst, sem_spill.at[(t % 2) * 3 + i])

    def mixer_back():
        mixer_load()
        conv_acc[...] = jnp.zeros_like(conv_acc)
        sg[...] = jnp.zeros_like(sg)
        for i in range(2):
            landed(take.at[1 - i], sem_pair.at[9 + 2 * i])
            landed(take.at[1 - i], sem_pair.at[8 + 2 * i])
        local(spill_h, outv.at[other], sem_spill.at[7]).wait()
        for i in range(3):
            loaded(0, i).start()

        @pl.loop(0, tiles)
        def _(t):
            rl = span_of(t * TILE, TILE, TILE)
            rs = span_of(c * rows + t * TILE, TILE, TILE)
            ro = span_of((1 - c) * rows + t * TILE, TILE, TILE)
            total = outv[rs, :] + take[0, rl, :].astype(F32)
            tr[rl, pl.ds(0, width)] = (total * live_in[rl, :]).astype(BF16)
            dn2 = dnv[rs, :] + take[1, rl, :].astype(F32)
            middle = outv[ro, :]
            scale = row_scale(middle)
            unit = middle * scale
            sg[1:2, :] += jnp.sum(dn2 * unit, axis=0, keepdims=True)
            d2 = dn2 * vec[1:2, :]
            back = scale * (d2 - unit * jnp.mean(d2 * unit, axis=-1, keepdims=True))
            back = act_b[rs, :].astype(F32) + back
            dnv[rs, :] = back
            act_b[rs, :] = back.astype(BF16)

        out = local(tr.at[:, pl.ds(0, width)], y_out, sem_in.at[1])
        out.start()
        remote(act_b.at[mine], act_b.at[mine], sem_pair.at[2], sem_pair.at[3], at(c=1 - c)).start()
        local(tok_in, act_a.at[mine], sem_in.at[0]).wait()
        local(spill_t, act_a.at[other], sem_spill.at[6]).wait()
        out.wait()

        @pl.loop(0, 2 * tiles)
        def _(t):
            rs = span_of(t * TILE, TILE, TILE)
            tr[:, rs] = normed(act_a[rs, :].astype(F32)).T

        landed(act_b.at[mine], sem_pair.at[2])
        landed(act_b.at[other], sem_pair.at[3])

        for cc in range(2):

            @pl.loop(0, seqs)
            def _(s):
                hf[span_of(s * EDGE, EDGE, EDGE), :] = act_b[span_of(cc * rows + s * span, EDGE, span), :].astype(F32)

            head = dot_nt(hf[...].astype(BF16), wout[...]).reshape(seqs, EDGE, chan)
            ks[cc * seqs : (cc + 1) * seqs] = head * chd[cc * seqs : (cc + 1) * seqs]

        @pl.when(me > 0)
        def _():
            remote(ks, kh, sem_kh.at[0], sem_kh.at[1], member(lax.rem(me + n - 1, n))).start()

        @pl.when(me == n - 1)
        def _():
            kh[...] = jnp.zeros_like(kh)

        for h in range(nx):
            side = pl.ds(h * lanes, lanes)
            gd[steps % slots, h] = dot_tn(zv[:, :CHUNK], act_b[:, side]).astype(BF16)
            og[h] = dot_tn(zv[:, CHUNK:], act_b[:, side]).astype(BF16)

        @pl.when(me < n - 1)
        def _():
            landed(kh, sem_kh.at[1])

        @pl.loop(0, 2 * tiles)
        def _(t):
            rs = span_of(t * TILE, TILE, TILE)
            first = t * tseq
            for i in range(3):
                loaded(t, i).wait()

            @pl.when(t + 1 < 2 * tiles)
            def _():
                for i in range(3):
                    loaded(t + 1, i).start()

            for h in range(2):
                hl = pl.ds(h * CHUNK, CHUNK)
                dz = dot_nt(act_b[rs, :], wout[hl, :]).reshape(tseq, span, CHUNK)
                b_gate, c_gate, x_value = (
                    dnv[
                        span_of((1 - c) * rows + i * TILE, TILE, TILE),
                        span_of((t % 2) * chan + h * CHUNK, CHUNK, CHUNK),
                    ].reshape(tseq, span, CHUNK)
                    for i in range(3)
                )
                *lags, conv = convolve((b_gate * x_value).reshape(TILE, CHUNK), first, h)
                dk = dz * c_gate
                for k in range(3):
                    conv_acc[k : k + 1, hl] += jnp.sum((dk * lags[k]).reshape(TILE, CHUNK), axis=0, keepdims=True)
                vb[:, :span, :] = dk
                vb[:, span:, :] = kh[pl.ds(first, tseq), :, hl]
                du = tap(2, h) * dk + tap(1, h) * vb[:, 1 : 1 + span, :] + tap(0, h) * vb[:, 2 : 2 + span, :]
                act_a[rs, hl] = (du * x_value).astype(BF16).reshape(TILE, CHUNK)
                act_a[rs, pl.ds(chan + h * CHUNK, CHUNK)] = (dz * conv).astype(BF16).reshape(TILE, CHUNK)
                zv[rs, hl] = (du * b_gate).astype(BF16).reshape(TILE, CHUNK)

    def share_back():
        @pl.loop(0, 2 * tiles)
        def _(t):
            rs = span_of(tile_start(t), TILE, TILE)
            total = dot_nt(act_a[rs, :CHUNK], win(0))
            for b in range(1, 6):
                src = act_a[rs, b * CHUNK : (b + 1) * CHUNK] if b < 4 else zv[rs, (b - 4) * CHUNK : (b - 3) * CHUNK]
                total += dot_nt(src, win(b))

            @pl.when(t < tiles)
            def _():
                act_b[rs, :] = total.astype(BF16)

            @pl.when(t >= tiles)
            def _():
                outv[rs, :] = total

            @pl.when(t == tiles - 1)
            def _():
                remote(act_b.at[other], take.at[0], sem_pair.at[4], sem_pair.at[5], at(c=1 - c)).start()
                local(tok_in, act_b.at[mine], sem_in.at[0]).start()

    def finish_back():
        landed(take.at[0], sem_pair.at[5])
        local(tok_in, act_b.at[mine], sem_in.at[0]).wait()

        @pl.loop(0, tiles)
        def _(t):
            rl = span_of(t * TILE, TILE, TILE)
            rs = span_of(c * rows + t * TILE, TILE, TILE)
            tokens = act_b[rs, :].astype(F32)
            scale = row_scale(tokens)
            unit = tokens * scale
            dn1 = outv[rs, :] + take[0, rl, :].astype(F32)
            sg[0:1, :] += jnp.sum(dn1 * unit, axis=0, keepdims=True)
            d1 = dn1 * vec[0:1, :]
            back = dnv[rs, :] + scale * (d1 - unit * jnp.mean(d1 * unit, axis=-1, keepdims=True))
            take[1, rl, :] = (back * live_in[rl, :]).astype(BF16)

        local(take.at[1], dx_out, sem_in.at[1]).start()
        sg[2:5, span_of(c * chan, chan, chan)] = conv_acc[0:3, :]
        local(sg, small_out, sem_in.at[0]).start()

    @pl.loop(0, chunks + 3 * LAG)
    def _(m):
        @pl.when(m < steps)
        def _():
            compute(m)

        @pl.when(m == steps - 1)
        def _():
            give_sums()

        @pl.when(m == steps)
        def _():
            mixer_back()

        @pl.when(jnp.logical_and(m >= steps, m < chunks - 1))
        def _():
            b = (m - steps) * 2 * CHUNK
            weight_grads(
                m % slots, act_a[:, span_of(b, CHUNK, CHUNK)], act_a[:, span_of(b + CHUNK, CHUNK, CHUNK)]
            )

        @pl.when(m == steps + 1)
        def _():
            gd[(steps + 1) % slots] = og[...]
            share_back()

        @pl.when(m == chunks - 1)
        def _():
            weight_grads(m % slots, zv[:, :CHUNK], zv[:, CHUNK:])

        @pl.when(m >= 3 * LAG)
        def _():
            finish(m - 3 * LAG)

        @pl.when(jnp.logical_and(m >= 2 * LAG, m < chunks + 2 * LAG))
        def _():
            send_z(m - 2 * LAG)

        @pl.when(jnp.logical_and(m >= LAG, m < chunks + LAG))
        def _():
            send_y(m - LAG)

        @pl.when(m < chunks)
        def _():
            send_x(m)

        @pl.when(m == chunks - 1)
        def _():
            finish_back()

        @pl.when(m + AHEAD < steps)
        def _():
            first_hop(m + AHEAD)

        @pl.when(m + RELAY < steps)
        def _():
            second_hop(m + RELAY)

        @pl.when(m + 1 < steps)
        def _():
            load(m + 1)

    finals_left(chunks - 1)
    landed(take.at[1], sem_in.at[1])
    landed(sg, sem_in.at[0])
    landed(take.at[0], sem_pair.at[4])

    @pl.when(me > 0)
    def _():
        landed(ks, sem_kh.at[0])

    for p in range(len(ag_peers)):
        landed(all_in.at[:, 0, 0], mg_send.at[p])
        landed(all_gu.at[:, :, 0, 0], ag_send.at[p])

        @pl.when(in_half)
        def _():
            landed(all_out.at[0], mg_osend.at[p])
            landed(all_down.at[:, pl.ds(0, gp)], ag_dsend.at[p])

    for d in range(1, nz):
        for e in range(1, ny):
            landed(all_in.at[:, 0, 0], mg_relay.at[d - 1, e - 1])
            landed(all_gu.at[:, :, 0, 0], ag_relay.at[d - 1, e - 1])
    for o in range(n // 2):
        zo, yo = out_owner(o)

        @pl.when(jnp.logical_and(zo != z, yo == y))
        def _():
            for e in range(1, ny):
                landed(all_out.at[0], mg_orelay.at[o, e - 1])

    for k in range(2):
        zo = (n // 2 * c) // ny + k

        @pl.when(zo != z)
        def _():
            for e in range(1, ny):
                landed(all_down.at[:, pl.ds(0, gp)], ag_drelay.at[zo % 2, e - 1])

    for p, (d, e) in enumerate(reps):
        landed(gu_full.at[0, 0], fr_g.at[p])
        landed(in_full.at[0, 0], fr_i.at[p])

        @pl.when(in_half if e == 0 else jnp.logical_not(in_half))
        def _():
            landed(down_full.at[0], fr_d.at[p])
            landed(out_full.at[0], fr_o.at[p])


def block_call(sizes, *operands):
    nx, nz, ny, seqs, span, width, hidden = sizes
    n = nz * ny
    rows = seqs * span
    dn = width // n
    dnx = dn // nx
    half = hidden // 2
    chan = width // 2
    steps = half // CHUNK
    own_rows = hidden // n
    gp = min(BLOCK, own_rows & -own_rows)
    pieces = CHUNK // gp
    lanes = width // nx
    s = 2 * LAG
    tseq = TILE // span
    reps = 2 * nx - 1
    hops = nz + ny - 2
    dma = lambda *dims: pltpu.SemaphoreType.DMA(dims)
    bf = lambda *dims: pltpu.VMEM(dims, BF16)
    fl = lambda *dims: pltpu.VMEM(dims, F32)
    anywhere = pl.BlockSpec(memory_space=pl.ANY)
    shape = jax.ShapeDtypeStruct
    specs = [anywhere] * 10
    specs[3] = pl.BlockSpec(memory_space=pltpu.VMEM)
    return pl.pallas_call(
        functools.partial(block_kernel, sizes),
        out_shape=[
            shape((rows, width), BF16),
            shape((rows, width), BF16),
            shape((nx, 2, 2, dnx, half), BF16),
            shape((nx, own_rows, lanes), BF16),
            shape((nx, 2, 6, dnx, CHUNK), BF16),
            shape((nx, dn, lanes), BF16),
            shape((8, width), F32),
            shape((steps, 2, nz, ny, dn, CHUNK), BF16),
            shape((steps, CHUNK, width), BF16),
            shape((6, nz, ny, dn, CHUNK), BF16),
            shape((n // 2, dn, width), BF16),
            shape((3, 2 * rows, chan), F32),
            shape((rows, width), F32),
            shape((rows, width), BF16),
        ],
        in_specs=specs,
        out_specs=[anywhere] * 14,
        scratch_shapes=[
            bf(2 * rows, width),
            bf(2 * rows, width),
            bf(width, 2 * rows),
            bf(2, nz, ny, dn, CHUNK),
            bf(CHUNK, width),
            fl(2 * rows, width),
            fl(2 * rows, width),
            bf(6, nz, ny, dn, CHUNK),
            bf(chan, width),
            bf(2 * rows, chan),
            bf(2, rows, width),
            bf(nx, CHUNK, lanes),
            fl(tseq, span + EDGE, CHUNK),
            fl(tseq, span + EDGE, CHUNK),
            bf(2, seqs, EDGE, width),
            fl(2 * seqs, EDGE, chan),
            fl(2 * seqs, EDGE, chan),
            fl(2 * seqs, EDGE, chan),
            fl(2 * seqs, EDGE, chan),
            fl(seqs * EDGE, width),
            fl(n, 8, dn),
            fl(8, width),
            fl(8, chan),
            fl(8, width),
            bf(s, 2, nx, nz, ny, dnx, CHUNK),
            bf(s, nx, CHUNK, lanes),
            bf(s, nx - 1, 2, nz, ny, dnx, CHUNK),
            bf(s, nx - 1, CHUNK, lanes),
            bf(s, ny, 2, nz, dnx, CHUNK),
            bf(s, CHUNK, lanes),
            bf(s, ny - 1, 2, nz, dnx, CHUNK),
            bf(s, ny - 1, CHUNK, lanes),
            bf(s, nz, 2, dnx, CHUNK),
            bf(s, CHUNK, lanes),
            bf(s, nz - 1, 2, dnx, CHUNK),
            bf(s, nz - 1, CHUNK, lanes),
            bf(2, dnx, CHUNK),
            bf(CHUNK, lanes),
            dma(2),
            dma(2 + n // 2),
            dma(2, steps * pieces),
            dma(12),
            dma(3),
            dma(4),
            dma(2),
            dma(8),
            dma(steps, nz - 1),
            dma(steps, ny - 1),
            dma(steps, pieces),
            dma(steps, pieces),
            dma(hops),
            dma(nz - 1, ny - 1),
            dma(hops),
            dma(2, ny - 1),
            dma(2),
            dma(nz - 1),
            dma(ny - 1),
            dma(n // 2),
            dma(n // 2),
            dma(hops),
            dma(nz - 1, ny - 1),
            dma(hops),
            dma(n // 2, ny - 1),
            dma(s, nx - 1),
            dma(s, nx - 1),
            dma(s, ny - 1),
            dma(s, ny - 1, pieces),
            dma(s, nz - 1),
            dma(s, nz - 1, pieces),
            dma(s, nx - 1),
            dma(s, nx - 1),
            dma(s, ny - 1),
            dma(s, pieces),
            dma(s, nz - 1),
            dma(s, pieces),
            dma(1 + pieces),
            dma(reps),
            dma(reps, pieces),
            dma(reps),
            dma(reps),
            dma(reps),
            dma(reps),
        ],
        compiler_params=pltpu.CompilerParams(
            collective_id=0, has_side_effects=True, vmem_limit_bytes=63 << 20
        ),
        name="gated_block",
    )(*operands)[:7]


def live_mask(lengths, deal, span):
    slots = jnp.arange(deal.shape[1], dtype=jnp.int32)
    picked = deal[0][:, None] == slots[None, :]
    source_len = jnp.sum(jnp.where(picked, lengths[0][:, None], 0), axis=0)
    position = lax.axis_index(GROUP) * span + jnp.arange(span, dtype=jnp.int32)
    return (position[None, :] < source_len[:, None]).astype(F32).reshape(-1, 1)


def body(
    tokens,
    cotangent,
    lengths,
    deal,
    norm_gain,
    in_weight,
    conv_weight,
    out_weight,
    ffn_gain,
    gate_weight,
    up_weight,
    down_weight,
):
    seqs, span, width = tokens.shape
    hidden = gate_weight.shape[1]
    nx, nz, ny = (lax.axis_size(axis) for axis in ("x", "z", "y"))
    dn = width // (nz * ny)
    small = jnp.stack([norm_gain, ffn_gain, *(conv_weight[:, k] for k in range(3))]).astype(F32)
    small = jnp.pad(small, ((0, 3), (0, 0)))
    block_out, block_grad, gu, down, mixer_in, mixer_out, sums = block_call(
        (nx, nz, ny, seqs, span, width, hidden),
        tokens.reshape(-1, width),
        tokens,
        cotangent.reshape(-1, width),
        live_mask(lengths, deal, span),
        small,
        in_weight,
        out_weight,
        gate_weight,
        up_weight,
        down_weight,
    )
    sums = lax.psum(sums, ("x", "core", "z", "y"))
    sums = lax.dynamic_slice_in_dim(sums, lax.axis_index(GROUP) * dn, dn, axis=1)
    gate_grad = gu[:, :, 0].transpose(0, 2, 1, 3).reshape(dn, hidden).astype(F32)
    up_grad = gu[:, :, 1].transpose(0, 2, 1, 3).reshape(dn, hidden).astype(F32)
    mixer_in = mixer_in.reshape(nx, 2, 3, 2, dn // nx, CHUNK)
    in_grad = mixer_in.transpose(0, 4, 2, 1, 3, 5).reshape(dn, 3 * width).astype(F32)
    out_grad = mixer_out.transpose(1, 0, 2).reshape(dn, width).astype(F32)
    down_grad = down.transpose(1, 0, 2).reshape(-1, width).astype(F32)
    return (
        block_out.reshape(tokens.shape),
        block_grad.reshape(tokens.shape),
        sums[0],
        in_grad,
        sums[2:5].T,
        out_grad,
        sums[1],
        gate_grad,
        up_grad,
        down_grad,
    )


def solution(mesh):
    rep, fsdp = mesh.shape["rep"], mesh.shape["fsdp"]
    grid = (rep // 2, 2, 4, fsdp // 4)
    split = Mesh(mesh.devices.reshape(grid), ("x", "core", "z", "y"))
    copies = ("x", "core")
    rows = P(copies, GROUP, None)
    lists = P(copies, None)
    vector = P(GROUP)
    matrix = P(GROUP, None)
    return jax.shard_map(
        body,
        mesh=split,
        in_specs=(
            rows,
            rows,
            lists,
            lists,
            vector,
            matrix,
            matrix,
            matrix,
            vector,
            matrix,
            matrix,
            matrix,
        ),
        out_specs=(rows, rows, vector, matrix, matrix, matrix, vector, matrix, matrix, matrix),
        check_vma=False,
    )
```

time: 1520 us -> 510 us (0.34)
  waiting for transfers between devices: 1130 us -> 0 us
  Pallas kernels: 0 us -> 443 us
  matrix products: 212 us -> 0 us
  other arithmetic: 49.1 us -> 3.34 us
  blocking collectives: 79.7 us -> 40.2 us
    reduce_scatter x5 -> x0, waiting for transfers between devices: 638 us -> none  [reduced(): lax.psum_scatter(values.astype(BF16), 'fsdp', scatter_dimension=0, tiled=...]
    pallas_call x0 -> x1, Pallas kernels: none -> 443 us  [block_call(): pl.pallas_call(functools.partial(block_kernel, sizes), out_shape=[shape((...]
    all_gather x5 -> x0, waiting for transfers between devices: 440 us -> none  [gather(): return lax.all_gather(values, 'fsdp', axis=0, tiled=True)]
    dot_general x15 -> x0, matrix products: 212 us -> none  [the longest x5 79.8 us: over_cols(): lax.dot_general(left_side, right_side, (((1,), (1,)), ((), ())), preferre...]
    all_gather x3 -> x0, blocking collectives: 53.8 us -> none  [gather(): return lax.all_gather(values, 'fsdp', axis=0, tiled=True)]
    psum x1 -> x0, waiting for transfers between devices: 45.5 us -> none  [reduced(): return lax.psum(share, 'rep').astype(F32)]
    psum x1, blocking collectives: 6.54 us -> 40.2 us  [body(): sums = lax.psum(sums, ('x', 'core', 'z', 'y'))]
    convert_element_type x16 -> x4, other arithmetic: 22.3 us -> 1.67 us  [the longest x1 1 us: body(): out_grad = mixer_out.transpose(1, 0, 2).reshape(dn, width).astype(F32)]
  transfers between devices with their start and end apart: 14 -> 0, of which waited for: 12 -> 0; matrix products, arithmetic and copies ran while one was open for 12% -> 0% of each run, Pallas kernels for 0% -> 0%
where the time goes in v3:
time: 510 us; the launch traced here: 509 us
  Pallas kernels  443 us (87%)
  blocking collectives  40.2 us (8%)
  local copies, waits for them, and re-layouts  21.5 us (4%)
    pallas_call x1, Pallas kernels, block_call(): pl.pallas_call(functools.partial(block_kernel, sizes), out_shape=[shape((...  443 us
    psum x1, blocking collectives, body(): sums = lax.psum(sums, ('x', 'core', 'z', 'y'))  40.2 us

profile of v3, /device:TPU:0, one launch (start us, length us, event | category | flops | bytes accessed | tf_op | source)
XLA Modules:
  0.0 509.0 jit_solution(10993209067274227622)
XLA Ops:
  0.7 0.8 select_reduce_fusion
  1.4 0.8 slice_bitcast_fusion.3
  2.2 0.7 stack.11
  2.9 0.6 pad_convert_fusion.small_in
  3.5 0.1 compare_convert_fusion
  3.6 1.3 reshape.102.live_in
  4.8 443.2 %gated_block.1 = (bf16[1024,1024]{1,0:T(8,128)(2,1)}, bf16[1024,1024]{1,0:T(8,128)(2,1)}, bf16[2,2,2,64,2304]{4,3,2,1,0:T(8,128)(2,1)}, bf16[2,576,512]{2,1,0:T(...) custom-call(bf16[1024,1024]{1,0:T(8,128)(2,1)} %bitcast.49, ...), custom_call_target="tpu_custom_call" | custom-call | tf_op jit(solution)/shard_map/gated_block/pallas_call | solution.py:951
  448.1 0.0 copy-start.4
  448.1 40.2 %psum.7 = f32[8,1024]{1,0:T(8,128)S(1)} all-reduce(f32[8,1024]{1,0:T(8,128)} %get-tuple-element.19), channel_id=1, replica_groups=mesh['x'=2,'core'=2,'z'=4,'y'=2] {'x','core','z','y'}, use_global_device_ids=true, to_apply=%region_1.2 | all-reduce | flops 8192 | bytes 65536 | tf_op jit(solution)/shard_map/psum | solution.py:1103
  488.3 0.5 slice_bitcast_fusion.1
  488.8 0.6 slice_bitcast_fusion
  489.4 1.0 convert_bitcast_fusion.4
  490.4 0.2 copy.32
  490.6 1.0 copy.36
  491.6 0.0 copy-done.4
  491.6 0.2 convert_bitcast_fusion.3
  491.8 1.2 copy.31
  493.0 0.0 copy-start.3
  493.0 2.4 reshape.94
  495.4 0.0 copy-done.3
  495.4 0.3 convert_bitcast_fusion.2
  495.8 0.0 copy-start
  495.8 1.7 copy.37
  497.4 0.9 copy-done
  498.3 0.4 convert_bitcast_fusion
  498.7 1.8 copy.34
  500.5 1.6 copy.39
  502.1 1.8 copy.33
  503.9 1.6 copy.38
  505.5 0.9 copy-done.2
  506.4 1.3 copy.42
  507.7 1.3 copy.43
  (5 shorter events, 0.0 us)
Async XLA Ops:
  448.1 43.5 %copy-start.4 = (bf16[2,2,6,64,256]{4,3,2,1,0:T(8,128)(2,1)S(1)}, bf16[2,2,6,64,256]{4,3,2,1,0:T(8,128)(2,1)}, u32[]{:S(2)}) copy-start(bf16[2,2,6,64,256]{4,3,2,1,0:T(8,128)(2,1)} %get-tuple-element.20) | copy-start | bytes 2359300
  493.0 2.4 copy-start.3
  495.8 2.5 copy-start
  503.9 2.4 copy-start.2
  505.5 2.2 copy-start.1

commit v4 on v3

--- a/solution.py
+++ b/solution.py
@@ -17,9 +17,9 @@
 BLOCK = 128
 TILE = 256
 EDGE = 8
-LAG = 1
 AHEAD = 4
 RELAY = 2
+HOLD = 4
 
 
 def dot(left, right):
@@ -43,14 +43,15 @@
     tok_in, edge_in, cot_in, live_in, small_in, in_in, out_in, gate_in, up_in, down_in,
     y_out, dx_out, gu_full, down_full, in_full, out_full, small_out,
     all_gu, all_down, all_in, all_out, spill_p, spill_h, spill_t,
+    h1g, h1d, hyg, hyd, h2g, h2d, hzg, hzd,
     act_a, act_b, tr, wgu, wd, outv, dnv, acts, wout, zv, take, og,
-    ub, vb, hal, uh, kh, ks, chd, hf, smallv, vec, conv_acc, sg,
-    ggu, gd, rxg, rxd, s1g, s1d, ryg, ryd, s2g, s2d, rzg, rzd, fing, find,
+    ub, vb, hal, uh, kh, ks, chd, hf, smallv, vec, conv_acc, sg, sg_all, sg_mine, sg_parts,
+    ggu, gd, rxg, rxd, s1g, s1d, y1g, y1d, yrg, yrd, z2g, z2d, zrg, zrd, fing, find,
     sem_in, sem_load, sem_own, sem_pair, sem_small, sem_edge, sem_kh, sem_spill,
-    ag_z, ag_y, ag_dz, ag_dy, ag_send, ag_relay, ag_dsend, ag_drelay,
+    ag_far, ag_z, ag_y, ag_dz, ag_dy, ag_send, ag_relay, ag_dsend, ag_drelay,
     mg_own, mg_z, mg_y, mg_oz, mg_oy, mg_send, mg_relay, mg_osend, mg_orelay,
-    rx_g, rx_d, ry_g, ry_d, rz_g, rz_d, sx_g, sx_d, sy_g, sy_d, sz_g, sz_d,
-    sem_fin, fs_g, fs_d, fr_g, fr_i, fr_d, fr_o,
+    rx_g, rx_d, sx_g, sx_d, st1, ry_g, ry_d, sy_g, sy_d, ld1, st2, rz_g, rz_d, sz_g, sz_d, ld2, st3,
+    fs_g, fs_i, fs_d, fs_o, fr_g, fr_i, fr_d, fr_o, sem_sum,
 ):
     nx, nz, ny, seqs, span, width, hidden = sizes
     n = nz * ny
@@ -66,7 +67,7 @@
     gp = min(BLOCK, own_rows & -own_rows)
     pieces = CHUNK // gp
     lanes = width // nx
-    slots = 2 * LAG
+    slots = 2
     tiles = rows // TILE
     tseq = TILE // span
     x, c = lax.axis_index("x"), lax.axis_index("core")
@@ -135,43 +136,93 @@
     def toward(ax, d):
         return at(z=zp(d)) if ax == 0 else at(y=yp(d))
 
-    for b in range(6):
+    def mixer_first_hop(b):
         here = in_in.at[:, span_of((b // 2) * width + c * chan + (b % 2) * CHUNK, CHUNK, CHUNK)]
         there = all_in.at[b, z, y]
         local(here, there, mg_own.at[0]).start()
+        hops(here, there, mg_send, lambda d: mg_z.at[b, d - 1], lambda d: mg_y.at[b, d - 1])
+
+    def out_first_hop():
+        @pl.when(in_half)
+        def _():
+            o = me - c * (n // 2)
+            local(out_in, all_out.at[o], mg_own.at[1]).start()
+            hops(out_in, all_out.at[o], mg_osend, lambda d: mg_oz.at[o], lambda d: mg_oy.at[o])
+
+    def off(zs):
+        return (zs - z) * (zs - z)
+
+    inner = jnp.logical_and(z > 0, z < nz - 1)
+    end = jnp.where(z == 1, 0, nz - 1)
+    end_slot = jnp.where(z == 1, 0, nz - 2)
+
+    def hops(here, there, send, recv_z, recv_y):
         for p, (ax, d) in enumerate(ag_peers):
-            remote(here, there, mg_send.at[p], (mg_z, mg_y)[ax].at[d - 1], toward(ax, d)).start()
-
-    @pl.when(in_half)
-    def _():
-        o = me - c * (n // 2)
-        local(out_in, all_out.at[o], mg_own.at[1]).start()
-        for p, (ax, d) in enumerate(ag_peers):
-            remote(out_in, all_out.at[o], mg_osend.at[p], (mg_oz, mg_oy)[ax].at[o], toward(ax, d)).start()
+            if ax == 1:
+                remote(here, there, send.at[p], recv_y(d), toward(ax, d)).start()
+            elif d in (1, nz - 1):
+
+                @pl.when(off(zp(d)) < (nz - 1) ** 2)
+                def _():
+                    remote(here, there, send.at[p], recv_z(d), toward(ax, d)).start()
+            else:
+                remote(here, there, send.at[p], recv_z(d), toward(ax, d)).start()
 
     def out_owner(o):
         j = c * (n // 2) + o
         return j // ny, j % ny
 
-    def mixer_second_hop():
+    def along_y(block, send, recv):
+        for e in range(1, ny):
+            remote(block, block, send.at[e - 1], recv(e), at(y=yp(e))).start()
+
+    def along(block, d, near, arrived, far_send, far_recv, y_send, y_recv):
+        if d in (1, nz - 1):
+            this = off(lax.rem(z - d + nz, nz)) == (nz - 1) ** 2
+
+            @pl.when(jnp.logical_not(this) if near else this)
+            def _():
+                landed(block, arrived)
+                along_y(block, y_send, y_recv)
+        elif near:
+            landed(block, arrived)
+
+            @pl.when(inner)
+            def _():
+                remote(block, block, far_send, far_recv, at(z=end)).start()
+
+            along_y(block, y_send, y_recv)
+
+    def mixer_hop(b, near):
         for d in range(1, nz):
-            zs = lax.rem(z - d + nz, nz)
-            block = all_in.at[:, zs, y]
-            landed(block, mg_z.at[d - 1])
-            for e in range(1, ny):
-                remote(block, block, mg_relay.at[d - 1, e - 1], mg_y.at[e - 1], at(y=yp(e))).start()
+            block = all_in.at[b, lax.rem(z - d + nz, nz), y]
+            along(
+                block, d, near, mg_z.at[b, d - 1], ag_far.at[0], mg_z.at[b, end_slot], mg_relay.at[d - 1], lambda e: mg_y.at[b, e - 1]
+            )
+
+    def owned(block, zo, near, arrived, far_send, y_send, y_recv):
+        @pl.when(off(zo) < (nz - 1) ** 2 if near else off(zo) == (nz - 1) ** 2)
+        def _():
+            landed(block, arrived)
+
+            @pl.when(jnp.logical_and(inner, off(zo) == 4))
+            def _():
+                remote(block, block, far_send, arrived, at(z=end)).start()
+
+            along_y(block, y_send, y_recv)
+
+    def out_hop(near):
         for o in range(n // 2):
             zo, yo = out_owner(o)
 
             @pl.when(jnp.logical_and(zo != z, yo == y))
             def _():
-                landed(all_out.at[o], mg_oz.at[o])
-                for e in range(1, ny):
-                    remote(all_out.at[o], all_out.at[o], mg_orelay.at[o, e - 1], mg_oy.at[o], at(y=yp(e))).start()
+                owned(all_out.at[o], zo, near, mg_oz.at[o], ag_far.at[1], mg_orelay.at[o], lambda e: mg_oy.at[o])
 
     def mixer_arrived():
         for e in range(1, ny):
-            landed(all_in.at[:, :, lax.rem(y - e + ny, ny)], mg_y.at[e - 1])
+            for b in range(6):
+                landed(all_in.at[b, :, lax.rem(y - e + ny, ny)], mg_y.at[b, e - 1])
         for o in range(n // 2):
             _, yo = out_owner(o)
 
@@ -225,8 +276,7 @@
                 here = src.at[:, pl.ds(column(b[k]), BLOCK)]
                 there = all_gu.at[m, w, z, y, :, pl.ds(k * BLOCK, BLOCK)]
                 local(here, there, sem_own.at[0, m]).start()
-                for p, (ax, d) in enumerate(ag_peers):
-                    remote(here, there, ag_send.at[p], (ag_z, ag_y)[ax].at[m, d - 1], toward(ax, d)).start()
+                hops(here, there, ag_send, lambda d: ag_z.at[m, d - 1], lambda d: ag_y.at[m, d - 1])
         for q in range(pieces):
             zo, yo, row = owner(m, q)
 
@@ -235,25 +285,21 @@
                 here = down_in.at[pl.ds(row, gp)]
                 there = all_down.at[m, pl.ds(q * gp, gp)]
                 local(here, there, sem_own.at[1, m * pieces + q]).start()
-                for p, (ax, d) in enumerate(ag_peers):
-                    remote(here, there, ag_dsend.at[p], (ag_dz, ag_dy)[ax].at[m, q], toward(ax, d)).start()
-
-    def second_hop(m):
+                hops(here, there, ag_dsend, lambda d: ag_dz.at[m, q], lambda d: ag_dy.at[m, q])
+
+    def next_hop(m, near):
         for d in range(1, nz):
-            zs = lax.rem(z - d + nz, nz)
-            block = all_gu.at[m, :, zs, y]
-            landed(block, ag_z.at[m, d - 1])
-            for e in range(1, ny):
-                remote(block, block, ag_relay.at[d - 1, e - 1], ag_y.at[m, e - 1], at(y=yp(e))).start()
+            block = all_gu.at[m, :, lax.rem(z - d + nz, nz), y]
+            along(
+                block, d, near, ag_z.at[m, d - 1], ag_far.at[2], ag_z.at[m, end_slot], ag_relay.at[d - 1], lambda e: ag_y.at[m, e - 1]
+            )
         for q in range(pieces):
             zo, yo, _ = owner(m, q)
 
             @pl.when(jnp.logical_and(zo != z, yo == y))
             def _():
                 block = all_down.at[m, pl.ds(q * gp, gp)]
-                landed(block, ag_dz.at[m, q])
-                for e in range(1, ny):
-                    remote(block, block, ag_drelay.at[zo % 2, e - 1], ag_dy.at[m, q], at(y=yp(e))).start()
+                owned(block, zo, near, ag_dz.at[m, q], ag_far.at[3], ag_drelay.at[zo % 2], lambda e: ag_dy.at[m, q])
 
     def load(m):
         landed(all_gu.at[m, :, 0, 0], sem_own.at[0, m])
@@ -271,12 +317,29 @@
             def _():
                 landed(block, ag_dy.at[m, q])
 
-        a = local(all_gu.at[m], wgu, sem_load.at[0])
-        b = local(all_down.at[m], wd, sem_load.at[1])
-        a.start()
-        b.start()
-        a.wait()
-        b.wait()
+        local(all_gu.at[m], wgu, sem_load.at[0]).start()
+        local(all_down.at[m], wd, sem_load.at[1]).start()
+
+    def loaded_weights():
+        landed(wgu, sem_load.at[0])
+        landed(wd, sem_load.at[1])
+
+    def pass_on(m):
+        @pl.when(m < steps)
+        def _():
+            next_hop(m, True)
+
+    def pass_on_far(m):
+        @pl.when(m < steps)
+        def _():
+            next_hop(m, False)
+
+        @pl.when(m + AHEAD - RELAY < steps)
+        def _():
+            first_hop(m + AHEAD - RELAY)
+
+    for b in range(3):
+        mixer_first_hop(b)
 
     local(cot_in, take.at[1], sem_in.at[1]).wait()
 
@@ -308,9 +371,19 @@
     def _():
         hal[...] = jnp.zeros_like(hal)
 
-    mixer_second_hop()
-    first_hop(0)
-    first_hop(1)
+    for b in range(6):
+        mixer_hop(b, True)
+        if b > 0:
+            mixer_hop(b - 1, False)
+        if b < 3:
+            mixer_first_hop(b + 3)
+        elif b == 3:
+            out_first_hop()
+        else:
+            first_hop(b - 4)
+    mixer_hop(5, False)
+    out_hop(True)
+    out_hop(False)
     local(tok_in, act_a.at[mine], sem_in.at[0]).wait()
     landed(act_a.at[mine], sem_pair.at[0])
     landed(act_a.at[other], sem_pair.at[1])
@@ -382,13 +455,19 @@
         def _():
             outv[rs, :] = act_a[rs, :].astype(F32) + mixed
 
+        @pl.when(lax.rem(t, tiles) == 1)
+        def _():
+            pass_on(t // tiles)
+
+        @pl.when(lax.rem(t, tiles) == tiles - 1)
+        def _():
+            pass_on_far(t // tiles)
+
         @pl.when(t == tiles - 1)
         def _():
             landed(act_a.at[other], sem_spill.at[6])
             remote(tr.at[:, pl.ds(0, width)], take.at[0], sem_pair.at[4], sem_pair.at[5], at(c=1 - c)).start()
 
-    first_hop(2)
-    second_hop(0)
     for slot in range(2):
         for i in range(3):
             spilled(slot, i, pl.ds(0, TILE)).wait()
@@ -404,8 +483,6 @@
     remote(act_a.at[mine], act_a.at[mine], sem_pair.at[6], sem_pair.at[7], at(c=1 - c)).start()
     local(outv.at[mine], spill_h, sem_spill.at[7]).start()
     landed(take.at[0], sem_pair.at[4])
-    first_hop(3)
-    second_hop(1)
 
     @pl.loop(0, tiles)
     def _(t):
@@ -427,6 +504,7 @@
 
     local(outv.at[mine], spill_h, sem_spill.at[7]).wait()
     load(0)
+    loaded_weights()
 
     big = 512
     zb = big // (ny * dn)
@@ -455,7 +533,16 @@
             for w, value in enumerate((q, gg, gv)):
                 acts[2 * w + r // 2, zi] = value.reshape(zb, ny, dn, CHUNK)
             outv[rs, :] += dot(q, wd[...])
+
+            @pl.when(r == 1)
+            def _():
+                pass_on(m + RELAY)
+
             dnv[rs, :] += dot_nt(gg, gate) + dot_nt(gv, up)
+
+        @pl.when(m + 1 < steps)
+        def _():
+            load(m + 1)
 
         weight_grads(slot, hid(1), hid(2))
         for h in range(nx):
@@ -484,7 +571,7 @@
             def _():
                 remote(gd.at[slot, xo], rxd.at[slot, d - 1], sx_d.at[slot, d - 1], rx_d.at[slot, d - 1], at(x=xo)).start()
 
-    def send_y(m):
+    def sum_x(m):
         slot = m % slots
         for d in range(1, nx):
             landed(rxg.at[slot, d - 1], rx_g.at[slot, d - 1])
@@ -497,11 +584,9 @@
                     total = ggu[slot, w, x, zi, yi].astype(F32)
                     for d in range(1, nx):
                         total += rxg[slot, d - 1, w, zi, yi].astype(F32)
-                    s1g[slot, yi, w, zi] = total.astype(BF16)
-
-        for d in range(1, ny):
-            yo = yp(d)
-            remote(s1g.at[slot, yo], ryg.at[slot, d - 1], sy_g.at[slot, d - 1], ry_g.at[slot, d - 1], at(y=yo)).start()
+                    s1g[yi, w, zi] = total.astype(BF16)
+
+        local(s1g, h1g.at[m], st1.at[0]).start()
 
         @pl.when(m < chunks - 1)
         def _():
@@ -511,7 +596,20 @@
             total = gd[slot, x].astype(F32)
             for d in range(1, nx):
                 total += rxd[slot, d - 1].astype(F32)
-            s1d[slot] = total.astype(BF16)
+            s1d[...] = total.astype(BF16)
+            copy = local(s1d, h1d.at[m], st1.at[1])
+            copy.start()
+            copy.wait()
+
+        landed(s1g, st1.at[0])
+
+    def send_y(m, _):
+        for d in range(1, ny):
+            yo = yp(d)
+            remote(h1g.at[m, yo], hyg.at[m, d - 1], sy_g.at[m], ry_g.at[m], at(y=yo)).start()
+
+        @pl.when(m < chunks - 1)
+        def _():
             for q in range(pieces):
                 _, yo, _ = grad_owner(m, q)
                 part = pl.ds(q * gp, gp)
@@ -519,24 +617,59 @@
                 @pl.when(yo != y)
                 def _():
                     d = lax.rem(yo - y + ny, ny)
-                    remote(
-                        s1d.at[slot, part], ryd.at[slot, d - 1, part], sy_d.at[slot, q], ry_d.at[slot, d - 1, q], at(y=yo)
-                    ).start()
-
-    def send_z(m):
-        slot = m % slots
-        for d in range(1, ny):
-            landed(ryg.at[slot, d - 1], ry_g.at[slot, d - 1])
-            landed(ryg.at[slot, d - 1], sy_g.at[slot, d - 1])
+                    remote(h1d.at[m, part], hyd.at[m, d - 1, part], sy_d.at[m, q], ry_d.at[m, q], at(y=yo)).start()
+
+    def y_copies(m, i):
+        copies = [local(h1g.at[m, y], y1g.at[i], ld1.at[i, 0]), local(hyg.at[m], yrg.at[i], ld1.at[i, 1])]
+        late = [local(h1d.at[m], y1d.at[i], ld1.at[i, 2]), local(hyd.at[m], yrd.at[i], ld1.at[i, 3])]
+        return copies, late
+
+    def fetch_y(m, i):
+        landed(hyg.at[m], ry_g.at[m])
+        copies, late = y_copies(m, i)
+        for copy in copies:
+            copy.start()
+
+        @pl.when(m < chunks - 1)
+        def _():
+            for q in range(pieces):
+                _, yo, _ = grad_owner(m, q)
+
+                @pl.when(yo == y)
+                def _():
+                    landed(hyd.at[m, :, pl.ds(q * gp, gp)], ry_d.at[m, q])
+
+            for copy in late:
+                copy.start()
+
+    def send_z(m, i):
+        copies, late = y_copies(m, i)
+        for copy in copies:
+            copy.wait()
         for zi in range(nz):
             for w in range(2):
-                total = s1g[slot, y, w, zi].astype(F32)
+                total = y1g[i, w, zi].astype(F32)
                 for d in range(1, ny):
-                    total += ryg[slot, d - 1, w, zi].astype(F32)
-                s2g[slot, zi, w] = total.astype(BF16)
+                    total += yrg[i, d - 1, w, zi].astype(F32)
+                s1g[0, w, zi] = total.astype(BF16)
+        stores = [local(s1g.at[0], h2g.at[m], st2.at[0]), local(s1d, h2d.at[m], st2.at[1])]
+        stores[0].start()
+
+        @pl.when(m < chunks - 1)
+        def _():
+            for copy in late:
+                copy.wait()
+            total = y1d[i].astype(F32)
+            for d in range(1, ny):
+                total += yrd[i, d - 1].astype(F32)
+            s1d[...] = total.astype(BF16)
+            stores[1].start()
+            stores[1].wait()
+
+        stores[0].wait()
         for d in range(1, nz):
             zo = zp(d)
-            remote(s2g.at[slot, zo], rzg.at[slot, d - 1], sz_g.at[slot, d - 1], rz_g.at[slot, d - 1], at(z=zo)).start()
+            remote(h2g.at[m, :, zo], hzg.at[m, d - 1], sz_g.at[m], rz_g.at[m], at(z=zo)).start()
 
         @pl.when(m < chunks - 1)
         def _():
@@ -544,110 +677,143 @@
                 zo, yo, _ = grad_owner(m, q)
                 part = pl.ds(q * gp, gp)
 
-                @pl.when(yo != y)
+                @pl.when(jnp.logical_and(yo == y, zo != z))
                 def _():
-                    landed(s1d.at[slot, part], sy_d.at[slot, q])
-
-                @pl.when(yo == y)
+                    d = lax.rem(zo - z + nz, nz)
+                    remote(h2d.at[m, part], hzd.at[m, d - 1, part], sz_d.at[m, q], rz_d.at[m, q], at(z=zo)).start()
+
+    def z_copies(m, i):
+        copies = [local(h2g.at[m, :, z], z2g.at[i], ld2.at[i, 0]), local(hzg.at[m], zrg.at[i], ld2.at[i, 1])]
+        late = [local(h2d.at[m], z2d.at[i], ld2.at[i, 2]), local(hzd.at[m], zrd.at[i], ld2.at[i, 3])]
+        return copies, late
+
+    def fetch_z(m, i):
+        landed(hzg.at[m], rz_g.at[m])
+        copies, late = z_copies(m, i)
+        for copy in copies:
+            copy.start()
+
+        @pl.when(m < chunks - 1)
+        def _():
+            for q in range(pieces):
+                zo, yo, _ = grad_owner(m, q)
+
+                @pl.when(jnp.logical_and(yo == y, zo == z))
                 def _():
-                    total = s1d[slot, part].astype(F32)
-                    for d in range(1, ny):
-                        landed(ryd.at[slot, d - 1, part], ry_d.at[slot, d - 1, q])
-                        total += ryd[slot, d - 1, part].astype(F32)
-                    s2d[slot, part] = total.astype(BF16)
-
-                    @pl.when(zo != z)
-                    def _():
-                        d = lax.rem(zo - z + nz, nz)
-                        remote(
-                            s2d.at[slot, part], rzd.at[slot, d - 1, part], sz_d.at[slot, q], rz_d.at[slot, d - 1, q], at(z=zo)
-                        ).start()
+                    landed(hzd.at[m, :, pl.ds(q * gp, gp)], rz_d.at[m, q])
+
+            for copy in late:
+                copy.start()
 
     def rep(p):
         d, e = reps[p]
         return at(x=xp(d), c=lax.rem(c + e, 2))
 
-    def finals_left(m):
-        landed(fing, sem_fin.at[0])
+    def spread(there, ssem, rsem):
         for p in range(len(reps)):
-            landed(fing, fs_g.at[p])
-
-        @pl.when(m < chunks - 1)
-        def _():
-            for q in range(pieces):
-                zo, yo, _ = grad_owner(m, q)
-                part = pl.ds(q * gp, gp)
-
-                @pl.when(jnp.logical_and(yo == y, zo == z))
-                def _():
-                    landed(find.at[part], sem_fin.at[1 + q])
-                    for p in range(len(reps)):
-                        landed(find.at[part], fs_d.at[p, q])
-
-    def finish(m):
-        slot = m % slots
-
-        @pl.when(m > 0)
-        def _():
-            finals_left(m - 1)
-
-        for d in range(1, nz):
-            landed(rzg.at[slot, d - 1], rz_g.at[slot, d - 1])
-            landed(rzg.at[slot, d - 1], sz_g.at[slot, d - 1])
+            remote(there, there, ssem.at[p], rsem.at[p], rep(p)).start()
+
+    def finish(m, i):
+        copies, late = z_copies(m, i)
+        for copy in copies:
+            copy.wait()
         for w in range(2):
-            total = s2g[slot, z, w].astype(F32)
+            total = z2g[i, w].astype(F32)
             for d in range(1, nz):
-                total += rzg[slot, d - 1, w].astype(F32)
+                total += zrg[i, d - 1, w].astype(F32)
             fing[w] = total.astype(BF16)
 
         @pl.when(m < steps)
         def _():
             b = blocks(m)
             for k in range(2):
-                here = fing.at[:, :, pl.ds(k * BLOCK, BLOCK)]
                 there = gu_full.at[x, c, :, :, span_of(b[k] * BLOCK, BLOCK, BLOCK)]
-                local(here, there, sem_fin.at[0]).start()
-                for p in range(len(reps)):
-                    remote(here, there, fs_g.at[p], fr_g.at[p], rep(p)).start()
+                copy = local(fing.at[:, :, pl.ds(k * BLOCK, BLOCK)], there, st3.at[0])
+                copy.start()
+                copy.wait()
+                spread(there, fs_g, fr_g)
 
         @pl.when(m >= steps)
         def _():
             there = in_full.at[x, c, pl.ds(2 * (m - steps), 2)]
-            local(fing, there, sem_fin.at[0]).start()
-            for p in range(len(reps)):
-                remote(fing, there, fs_g.at[p], fr_i.at[p], rep(p)).start()
+            copy = local(fing, there, st3.at[0])
+            copy.start()
+            copy.wait()
+            spread(there, fs_i, fr_i)
 
         @pl.when(m < chunks - 1)
         def _():
+            for copy in late:
+                copy.wait()
             for q in range(pieces):
                 zo, yo, row = grad_owner(m, q)
                 part = pl.ds(q * gp, gp)
 
-                @pl.when(jnp.logical_and(yo == y, zo != z))
-                def _():
-                    landed(s2d.at[slot, part], sz_d.at[slot, q])
-
                 @pl.when(jnp.logical_and(yo == y, zo == z))
                 def _():
-                    total = s2d[slot, part].astype(F32)
+                    total = z2d[i, part].astype(F32)
                     for d in range(1, nz):
-                        landed(rzd.at[slot, d - 1, part], rz_d.at[slot, d - 1, q])
-                        total += rzd[slot, d - 1, part].astype(F32)
-                    find[part] = total.astype(BF16)
+                        total += zrd[i, d - 1, part].astype(F32)
+                    find[...] = total.astype(BF16)
 
                     @pl.when(m < steps)
                     def _():
                         there = down_full.at[x, pl.ds(row, gp)]
-                        local(find.at[part], there, sem_fin.at[1 + q]).start()
-                        for p in range(len(reps)):
-                            remote(find.at[part], there, fs_d.at[p, q], fr_d.at[p], rep(p)).start()
+                        copy = local(find, there, st3.at[1])
+                        copy.start()
+                        copy.wait()
+                        spread(there, fs_d, fr_d)
 
                     @pl.when(m >= steps)
                     def _():
                         there = out_full.at[x, pl.ds(row, gp)]
-                        local(find.at[part], there, sem_fin.at[1 + q]).start()
-                        for p in range(len(reps)):
-                            remote(find.at[part], there, fs_d.at[p, q], fr_o.at[p], rep(p)).start()
+                        copy = local(find, there, st3.at[1])
+                        copy.start()
+                        copy.wait()
+                        spread(there, fs_o, fr_o)
+
+    def gone(m):
+        return jnp.clip(jnp.minimum(m, 2 * (m - HOLD)), 0, chunks)
+
+    def two(m, do):
+        for i in range(2):
+            k = gone(m - 1) + i
+
+            @pl.when(k < gone(m))
+            def _():
+                do(k, i)
+
+    def own_rep():
+        return x * 2 + c
+
+    def sum_reps():
+        local(sg, sg_all.at[own_rep()], sem_sum.at[0]).start()
+        for p in range(len(reps)):
+            remote(sg, sg_all.at[own_rep()], sem_sum.at[1], sem_sum.at[2], rep(p)).start()
+
+    def sum_group():
+        landed(sg, sem_sum.at[0])
+        landed(sg_all.at[pl.ds(0, len(reps))], sem_sum.at[1])
+        landed(sg_all.at[pl.ds(0, len(reps))], sem_sum.at[2])
+        total = sg_all[0]
+        for p in range(1, 2 * nx):
+            total += sg_all[p]
+        for j in range(n):
+            sg_mine[j] = total[:, j * dn : (j + 1) * dn]
+        local(sg_mine.at[me], sg_parts.at[me], sem_sum.at[3]).start()
+        for d in range(1, n):
+            j = lax.rem(me + d, n)
+            remote(sg_mine.at[j], sg_parts.at[me], sem_sum.at[4], sem_sum.at[5], member(j)).start()
+
+    def sum_last():
+        landed(sg_mine.at[0], sem_sum.at[3])
+        landed(sg_parts.at[pl.ds(0, n - 1)], sem_sum.at[4])
+        landed(sg_parts.at[pl.ds(0, n - 1)], sem_sum.at[5])
+        total = sg_parts[0]
+        for j in range(1, n):
+            total += sg_parts[j]
+        smallv[0] = total
+        local(smallv.at[0], small_out, sem_in.at[0]).start()
 
     def give_sums():
         for i, src in enumerate((dnv, outv)):
@@ -812,9 +978,9 @@
 
         local(take.at[1], dx_out, sem_in.at[1]).start()
         sg[2:5, span_of(c * chan, chan, chan)] = conv_acc[0:3, :]
-        local(sg, small_out, sem_in.at[0]).start()
-
-    @pl.loop(0, chunks + 3 * LAG)
+        sum_reps()
+
+    @pl.loop(0, chunks + 3)
     def _(m):
         @pl.when(m < steps)
         def _():
@@ -838,61 +1004,104 @@
         @pl.when(m == steps + 1)
         def _():
             gd[(steps + 1) % slots] = og[...]
+
+        @pl.when(m == chunks - 1)
+        def _():
+            weight_grads(m % slots, zv[:, :CHUNK], zv[:, CHUNK:])
+
+        @pl.when(jnp.logical_and(m >= 1, m < chunks + 1))
+        def _():
+            sum_x(m - 1)
+
+        @pl.when(m < chunks)
+        def _():
+            send_x(m)
+
+        two(m - 1, fetch_y)
+        two(m - 2, fetch_z)
+        pass_on_far(m + RELAY)
+        two(m, send_y)
+        two(m - 1, send_z)
+        two(m - 2, finish)
+
+        @pl.when(m == steps + 1)
+        def _():
             share_back()
 
         @pl.when(m == chunks - 1)
         def _():
-            weight_grads(m % slots, zv[:, :CHUNK], zv[:, CHUNK:])
-
-        @pl.when(m >= 3 * LAG)
-        def _():
-            finish(m - 3 * LAG)
-
-        @pl.when(jnp.logical_and(m >= 2 * LAG, m < chunks + 2 * LAG))
-        def _():
-            send_z(m - 2 * LAG)
-
-        @pl.when(jnp.logical_and(m >= LAG, m < chunks + LAG))
-        def _():
-            send_y(m - LAG)
-
-        @pl.when(m < chunks)
-        def _():
-            send_x(m)
-
-        @pl.when(m == chunks - 1)
-        def _():
             finish_back()
 
-        @pl.when(m + AHEAD < steps)
-        def _():
-            first_hop(m + AHEAD)
-
-        @pl.when(m + RELAY < steps)
-        def _():
-            second_hop(m + RELAY)
+        @pl.when(m == chunks)
+        def _():
+            sum_group()
+
+        @pl.when(m == chunks + 1)
+        def _():
+            sum_last()
 
         @pl.when(m + 1 < steps)
         def _():
-            load(m + 1)
-
-    finals_left(chunks - 1)
+            loaded_weights()
+
     landed(take.at[1], sem_in.at[1])
-    landed(sg, sem_in.at[0])
+    landed(smallv.at[0], sem_in.at[0])
+
+    @pl.loop(0, chunks)
+    def _(m):
+        landed(hyg.at[m], sy_g.at[m])
+        landed(hzg.at[m], sz_g.at[m])
+
+        @pl.when(m < chunks - 1)
+        def _():
+            for q in range(pieces):
+                zo, yo, _ = grad_owner(m, q)
+                part = pl.ds(q * gp, gp)
+
+                @pl.when(yo != y)
+                def _():
+                    landed(h1d.at[m, part], sy_d.at[m, q])
+
+                @pl.when(jnp.logical_and(yo == y, zo != z))
+                def _():
+                    landed(h2d.at[m, part], sz_d.at[m, q])
+
+    for p in range(len(reps)):
+        landed(gu_full.at[0, 0], fs_g.at[p])
+        landed(in_full.at[0, 0], fs_i.at[p])
+
+        @pl.when(in_half)
+        def _():
+            landed(down_full.at[0], fs_d.at[p])
+            landed(out_full.at[0], fs_o.at[p])
     landed(take.at[0], sem_pair.at[4])
 
     @pl.when(me > 0)
     def _():
         landed(ks, sem_kh.at[0])
 
-    for p in range(len(ag_peers)):
-        landed(all_in.at[:, 0, 0], mg_send.at[p])
-        landed(all_gu.at[:, :, 0, 0], ag_send.at[p])
-
-        @pl.when(in_half)
+    for p, (ax, d) in enumerate(ag_peers):
+        direct = ax == 1 or off(zp(d)) < (nz - 1) ** 2
+
+        @pl.when(direct)
+        def _():
+            landed(all_in.at[:, 0, 0], mg_send.at[p])
+            landed(all_gu.at[:, :, 0, 0], ag_send.at[p])
+
+        @pl.when(jnp.logical_and(direct, in_half))
         def _():
             landed(all_out.at[0], mg_osend.at[p])
             landed(all_down.at[:, pl.ds(0, gp)], ag_dsend.at[p])
+
+    @pl.when(inner)
+    def _():
+        landed(all_in.at[:, 0, 0], ag_far.at[0])
+        landed(all_gu.at[:, :, 0, 0], ag_far.at[2])
+
+    @pl.when(z == jnp.where(c == 0, 2, 1))
+    def _():
+        landed(all_out.at[0], ag_far.at[1])
+        landed(all_down.at[:, pl.ds(0, gp)], ag_far.at[3])
 
     for d in range(1, nz):
         for e in range(1, ny):
@@ -937,7 +1146,7 @@
     gp = min(BLOCK, own_rows & -own_rows)
     pieces = CHUNK // gp
     lanes = width // nx
-    s = 2 * LAG
+    chunks = steps + 3
     tseq = TILE // span
     reps = 2 * nx - 1
     hops = nz + ny - 2
@@ -957,7 +1166,7 @@
             shape((nx, own_rows, lanes), BF16),
             shape((nx, 2, 6, dnx, CHUNK), BF16),
             shape((nx, dn, lanes), BF16),
-            shape((8, width), F32),
+            shape((8, dn), F32),
             shape((steps, 2, nz, ny, dn, CHUNK), BF16),
             shape((steps, CHUNK, width), BF16),
             shape((6, nz, ny, dn, CHUNK), BF16),
@@ -965,9 +1174,17 @@
             shape((3, 2 * rows, chan), F32),
             shape((rows, width), F32),
             shape((rows, width), BF16),
+            shape((chunks, ny, 2, nz, dnx, CHUNK), BF16),
+            shape((chunks, CHUNK, lanes), BF16),
+            shape((chunks, ny - 1, 2, nz, dnx, CHUNK), BF16),
+            shape((chunks, ny - 1, CHUNK, lanes), BF16),
+            shape((chunks, 2, nz, dnx, CHUNK), BF16),
+            shape((chunks, CHUNK, lanes), BF16),
+            shape((chunks, nz - 1, 2, dnx, CHUNK), BF16),
+            shape((chunks, nz - 1, CHUNK, lanes), BF16),
         ],
         in_specs=specs,
-        out_specs=[anywhere] * 14,
+        out_specs=[anywhere] * 22,
         scratch_shapes=[
             bf(2 * rows, width),
             bf(2 * rows, width),
@@ -993,20 +1210,25 @@
             fl(8, width),
             fl(8, chan),
             fl(8, width),
-            bf(s, 2, nx, nz, ny, dnx, CHUNK),
-            bf(s, nx, CHUNK, lanes),
-            bf(s, nx - 1, 2, nz, ny, dnx, CHUNK),
-            bf(s, nx - 1, CHUNK, lanes),
-            bf(s, ny, 2, nz, dnx, CHUNK),
-            bf(s, CHUNK, lanes),
-            bf(s, ny - 1, 2, nz, dnx, CHUNK),
-            bf(s, ny - 1, CHUNK, lanes),
-            bf(s, nz, 2, dnx, CHUNK),
-            bf(s, CHUNK, lanes),
-            bf(s, nz - 1, 2, dnx, CHUNK),
-            bf(s, nz - 1, CHUNK, lanes),
+            fl(2 * nx, 8, width),
+            fl(n, 8, dn),
+            fl(n, 8, dn),
+            bf(2, 2, nx, nz, ny, dnx, CHUNK),
+            bf(2, nx, CHUNK, lanes),
+            bf(2, nx - 1, 2, nz, ny, dnx, CHUNK),
+            bf(2, nx - 1, CHUNK, lanes),
+            bf(ny, 2, nz, dnx, CHUNK),
+            bf(CHUNK, lanes),
+            bf(2, 2, nz, dnx, CHUNK),
+            bf(2, CHUNK, lanes),
+            bf(2, ny - 1, 2, nz, dnx, CHUNK),
+            bf(2, ny - 1, CHUNK, lanes),
+            bf(2, 2, dnx, CHUNK),
+            bf(2, CHUNK, lanes),
+            bf(2, nz - 1, 2, dnx, CHUNK),
+            bf(2, nz - 1, CHUNK, lanes),
             bf(2, dnx, CHUNK),
-            bf(CHUNK, lanes),
+            bf(gp, lanes),
             dma(2),
             dma(2 + n // 2),
             dma(2, steps * pieces),
@@ -1015,6 +1237,7 @@
             dma(4),
             dma(2),
             dma(8),
+            dma(4),
             dma(steps, nz - 1),
             dma(steps, ny - 1),
             dma(steps, pieces),
@@ -1024,33 +1247,40 @@
             dma(hops),
             dma(2, ny - 1),
             dma(2),
-            dma(nz - 1),
-            dma(ny - 1),
+            dma(6, nz - 1),
+            dma(6, ny - 1),
             dma(n // 2),
             dma(n // 2),
             dma(hops),
             dma(nz - 1, ny - 1),
             dma(hops),
             dma(n // 2, ny - 1),
-            dma(s, nx - 1),
-            dma(s, nx - 1),
-            dma(s, ny - 1),
-            dma(s, ny - 1, pieces),
-            dma(s, nz - 1),
-            dma(s, nz - 1, pieces),
-            dma(s, nx - 1),
-            dma(s, nx - 1),
-            dma(s, ny - 1),
-            dma(s, pieces),
-            dma(s, nz - 1),
-            dma(s, pieces),
-            dma(1 + pieces),
-            dma(reps),
-            dma(reps, pieces),
+            dma(2, nx - 1),
+            dma(2, nx - 1),
+            dma(2, nx - 1),
+            dma(2, nx - 1),
+            dma(2),
+            dma(chunks),
+            dma(chunks, pieces),
+            dma(chunks),
+            dma(chunks, pieces),
+            dma(2, 4),
+            dma(2),
+            dma(chunks),
+            dma(chunks, pieces),
+            dma(chunks),
+            dma(chunks, pieces),
+            dma(2, 4),
+            dma(2),
             dma(reps),
             dma(reps),
             dma(reps),
             dma(reps),
+            dma(reps),
+            dma(reps),
+            dma(reps),
+            dma(reps),
+            dma(6),
         ],
         compiler_params=pltpu.CompilerParams(
             collective_id=0, has_side_effects=True, vmem_limit_bytes=63 << 20
@@ -1100,8 +1330,6 @@
         up_weight,
         down_weight,
     )
-    sums = lax.psum(sums, ("x", "core", "z", "y"))
-    sums = lax.dynamic_slice_in_dim(sums, lax.axis_index(GROUP) * dn, dn, axis=1)
     gate_grad = gu[:, :, 0].transpose(0, 2, 1, 3).reshape(dn, hidden).astype(F32)
     up_grad = gu[:, :, 1].transpose(0, 2, 1, 3).reshape(dn, hidden).astype(F32)
     mixer_in = mixer_in.reshape(nx, 2, 3, 2, dn // nx, CHUNK)

time: 510 us -> 454 us (0.89)
  blocking collectives: 40.2 us -> 0 us
  Pallas kernels: 443 us -> 426 us
    psum x1 -> x0, blocking collectives: 40.2 us -> none  [body(): sums = lax.psum(sums, ('x', 'core', 'z', 'y'))]
    pallas_call x1, Pallas kernels: 443 us -> 426 us  [block_call(): pl.pallas_call(functools.partial(block_kernel, sizes), out_shape=[shape((...]
where the time goes in v4:
time: 454 us; the launch traced here: 453 us
  Pallas kernels  426 us (94%)
  local copies, waits for them, and re-layouts  22.9 us (5%)
    pallas_call x1, Pallas kernels, block_call(): pl.pallas_call(functools.partial(block_kernel, sizes), out_shape=[shape((...  426 us

profile of v4, /device:TPU:0, one launch (start us, length us, event | category | flops | bytes accessed | tf_op | source)
XLA Modules:
  0.0 453.1 jit_solution(4727817286943379273)
XLA Ops:
  0.7 0.8 select_reduce_fusion
  1.4 0.8 slice_bitcast_fusion.3
  2.2 0.7 stack.11
  2.9 0.6 pad_convert_fusion.small_in
  3.5 0.1 compare_convert_fusion
  3.6 1.3 reshape.102.live_in
  4.8 426.1 %gated_block.1 = (bf16[1024,1024]{1,0:T(8,128)(2,1)}, bf16[1024,1024]{1,0:T(8,128)(2,1)}, bf16[2,2,2,64,2304]{4,3,2,1,0:T(8,128)(2,1)}, bf16[2,576,512]{2,1,0:T(...) custom-call(bf16[1024,1024]{1,0:T(8,128)(2,1)} %bitcast.49, ...), custom_call_target="tpu_custom_call" | custom-call | tf_op jit(solution)/shard_map/gated_block/pallas_call | solution.py:1160
  430.9 0.0 copy-start.4
  430.9 1.3 slice_bitcast_fusion.1
  432.2 1.3 slice_bitcast_fusion
  433.5 1.0 convert_bitcast_fusion.4
  434.5 0.2 copy.32
  434.7 1.0 copy.36
  435.7 0.0 copy-done.4
  435.7 0.2 convert_bitcast_fusion.3
  435.9 1.2 copy.31
  437.1 0.0 copy-start.3
  437.1 2.4 reshape.94
  439.5 0.0 copy-done.3
  439.5 0.3 convert_bitcast_fusion.2
  439.8 0.0 copy-start
  439.8 1.7 copy.37
  441.5 0.9 copy-done
  442.4 0.4 convert_bitcast_fusion
  442.8 1.8 copy.34
  444.6 1.6 copy.39
  446.2 1.8 copy.33
  448.0 0.0 copy-start.2
  448.0 1.6 copy.38
  449.6 0.9 copy-done.2
  450.4 1.3 copy.42
  451.8 1.3 copy.43
  (3 shorter events, 0.0 us)
Async XLA Ops:
  430.9 4.8 %copy-start.4 = (bf16[2,2,6,64,256]{4,3,2,1,0:T(8,128)(2,1)S(1)}, bf16[2,2,6,64,256]{4,3,2,1,0:T(8,128)(2,1)}, u32[]{:S(2)}) copy-start(bf16[2,2,6,64,256]{4,3,2,1,0:T(8,128)(2,1)} %get-tuple-element.20) | copy-start | bytes 2359300
  437.1 2.4 copy-start.3
  439.8 2.5 copy-start
  448.0 2.4 copy-start.2
  449.6 2.2 copy-start.1

commit v5 on v4

--- a/solution.py
+++ b/solution.py
@@ -19,7 +19,8 @@
 EDGE = 8
 AHEAD = 4
 RELAY = 2
-HOLD = 4
+HOLD = 5
+SHARED = 2
 
 
 def dot(left, right):
@@ -43,14 +44,14 @@
     tok_in, edge_in, cot_in, live_in, small_in, in_in, out_in, gate_in, up_in, down_in,
     y_out, dx_out, gu_full, down_full, in_full, out_full, small_out,
     all_gu, all_down, all_in, all_out, spill_p, spill_h, spill_t,
-    h1g, h1d, hyg, hyd, h2g, h2d, hzg, hzd,
-    act_a, act_b, tr, wgu, wd, outv, dnv, acts, wout, zv, take, og,
+    h0g, h0d, h1g, h1d, hyg, hyd, h2g, h2d, hzg, hzd,
+    act_a, act_b, tr, wgu, wd, outv, dnv, acts, wout, zv, take,
     ub, vb, hal, uh, kh, ks, chd, hf, smallv, vec, conv_acc, sg, sg_all, sg_mine, sg_parts,
-    ggu, gd, rxg, rxd, s1g, s1d, y1g, y1d, yrg, yrd, z2g, z2d, zrg, zrd, fing, find,
-    sem_in, sem_load, sem_own, sem_pair, sem_small, sem_edge, sem_kh, sem_spill,
-    ag_far, ag_z, ag_y, ag_dz, ag_dy, ag_send, ag_relay, ag_dsend, ag_drelay,
+    ggu, gd, vag, vad, s1g, s1d, og, y1g, y1d, yrg, yrd, z2g, z2d, zrg, zrd, fing, find,
+    sem_in, sem_load, sem_own, sem_pair, sem_half, sem_n2, sem_sums, sem_dm, sem_small, sem_edge, sem_kh, sem_spill,
+    ag_cross, ag_x, mg_cross, mg_x, ag_far, ag_z, ag_y, ag_dz, ag_dy, ag_send, ag_relay, ag_dsend, ag_drelay,
     mg_own, mg_z, mg_y, mg_oz, mg_oy, mg_send, mg_relay, mg_osend, mg_orelay,
-    rx_g, rx_d, sx_g, sx_d, st1, ry_g, ry_d, sy_g, sy_d, ld1, st2, rz_g, rz_d, sz_g, sz_d, ld2, st3,
+    ra_g, ra_d, sa_g, sa_d, ld0, st1, ry_g, ry_d, sy_g, sy_d, ld1, st2, rz_g, rz_d, sz_g, sz_d, ld2, st3,
     fs_g, fs_i, fs_d, fs_o, fr_g, fr_i, fr_d, fr_o, sem_sum,
 ):
     nx, nz, ny, seqs, span, width, hidden = sizes
@@ -67,7 +68,7 @@
     gp = min(BLOCK, own_rows & -own_rows)
     pieces = CHUNK // gp
     lanes = width // nx
-    slots = 2
+    slots = 3
     tiles = rows // TILE
     tseq = TILE // span
     x, c = lax.axis_index("x"), lax.axis_index("core")
@@ -123,9 +124,8 @@
     @pl.when(me < n - 1)
     def _():
         for e in range(2):
-            src = edge_in.at[:, pl.ds(span - EDGE, EDGE)]
             dev = member(lax.rem(me + 1, n), c=lax.rem(c + e, 2))
-            remote(src, hal.at[c], sem_edge.at[e], sem_edge.at[2 + c], dev).start()
+            remote(edge_in, hal.at[c], sem_edge.at[e], sem_edge.at[2 + c], dev).start()
 
     local(tok_in, act_a.at[mine], sem_in.at[0]).start()
     local(cot_in, take.at[1], sem_in.at[1]).start()
@@ -140,7 +140,7 @@
         here = in_in.at[:, span_of((b // 2) * width + c * chan + (b % 2) * CHUNK, CHUNK, CHUNK)]
         there = all_in.at[b, z, y]
         local(here, there, mg_own.at[0]).start()
-        hops(here, there, mg_send, lambda d: mg_z.at[b, d - 1], lambda d: mg_y.at[b, d - 1])
+        hops(here, there, mg_send, lambda d: mg_z.at[b, d - 1], lambda d: mg_y.at[b, d - 1], b % 2)
 
     def out_first_hop():
         @pl.when(in_half)
@@ -156,10 +156,16 @@
     end = jnp.where(z == 1, 0, nz - 1)
     end_slot = jnp.where(z == 1, 0, nz - 2)
 
-    def hops(here, there, send, recv_z, recv_y):
+    plane = x % 2
+    partner = x + 1 - 2 * plane
+
+    def hops(here, there, send, recv_z, recv_y, only=None):
         for p, (ax, d) in enumerate(ag_peers):
             if ax == 1:
-                remote(here, there, send.at[p], recv_y(d), toward(ax, d)).start()
+
+                @pl.when(True if only is None else plane == only)
+                def _():
+                    remote(here, there, send.at[p], recv_y(d), toward(ax, d)).start()
             elif d in (1, nz - 1):
 
                 @pl.when(off(zp(d)) < (nz - 1) ** 2)
@@ -176,14 +182,17 @@
         for e in range(1, ny):
             remote(block, block, send.at[e - 1], recv(e), at(y=yp(e))).start()
 
-    def along(block, d, near, arrived, far_send, far_recv, y_send, y_recv):
+    def along(block, part, wanted, d, near, arrived, far_send, far_recv, y_send, y_recv):
         if d in (1, nz - 1):
             this = off(lax.rem(z - d + nz, nz)) == (nz - 1) ** 2
 
             @pl.when(jnp.logical_not(this) if near else this)
             def _():
                 landed(block, arrived)
-                along_y(block, y_send, y_recv)
+
+                @pl.when(wanted)
+                def _():
+                    along_y(part, y_send, y_recv)
         elif near:
             landed(block, arrived)
 
@@ -191,13 +200,23 @@
             def _():
                 remote(block, block, far_send, far_recv, at(z=end)).start()
 
-            along_y(block, y_send, y_recv)
+            @pl.when(wanted)
+            def _():
+                along_y(part, y_send, y_recv)
+
+    def mixer_cross(b):
+        @pl.when(plane == b % 2)
+        def _():
+            for e in range(1, ny):
+                block = all_in.at[b, :, lax.rem(y - e + ny, ny)]
+                landed(block, mg_y.at[b, e - 1])
+                remote(block, block, mg_cross.at[e - 1], mg_x.at[b, e - 1], at(x=partner)).start()
 
     def mixer_hop(b, near):
         for d in range(1, nz):
             block = all_in.at[b, lax.rem(z - d + nz, nz), y]
             along(
-                block, d, near, mg_z.at[b, d - 1], ag_far.at[0], mg_z.at[b, end_slot], mg_relay.at[d - 1], lambda e: mg_y.at[b, e - 1]
+                block, block, plane == b % 2, d, near, mg_z.at[b, d - 1], ag_far.at[0], mg_z.at[b, end_slot], mg_relay.at[d - 1], lambda e: mg_y.at[b, e - 1]
             )
 
     def owned(block, zo, near, arrived, far_send, y_send, y_recv):
@@ -222,7 +241,10 @@
     def mixer_arrived():
         for e in range(1, ny):
             for b in range(6):
-                landed(all_in.at[b, :, lax.rem(y - e + ny, ny)], mg_y.at[b, e - 1])
+
+                @pl.when(plane != b % 2)
+                def _():
+                    landed(all_in.at[b, :, lax.rem(y - e + ny, ny)], mg_x.at[b, e - 1])
         for o in range(n // 2):
             _, yo = out_owner(o)
 
@@ -269,14 +291,14 @@
             pl.multiple_of(jnp.where(late, mixed - j * dn, row), gp),
         )
 
-    def first_hop(m):
+    def first_hop(m, shared=False):
         b = blocks(m)
         for k in range(2):
             for w, src in enumerate((gate_in, up_in)):
                 here = src.at[:, pl.ds(column(b[k]), BLOCK)]
                 there = all_gu.at[m, w, z, y, :, pl.ds(k * BLOCK, BLOCK)]
                 local(here, there, sem_own.at[0, m]).start()
-                hops(here, there, ag_send, lambda d: ag_z.at[m, d - 1], lambda d: ag_y.at[m, d - 1])
+                hops(here, there, ag_send, lambda d: ag_z.at[m, d - 1], lambda d: ag_y.at[m, d - 1], k if shared else None)
         for q in range(pieces):
             zo, yo, row = owner(m, q)
 
@@ -287,11 +309,22 @@
                 local(here, there, sem_own.at[1, m * pieces + q]).start()
                 hops(here, there, ag_dsend, lambda d: ag_dz.at[m, q], lambda d: ag_dy.at[m, q])
 
-    def next_hop(m, near):
+    def half_of(m, ys, side):
+        return all_gu.at[m, :, :, ys, :, span_of(side * BLOCK, BLOCK, BLOCK)]
+
+    def cross(m):
+        for e in range(1, ny):
+            block = half_of(m, lax.rem(y - e + ny, ny), plane)
+            landed(block, ag_y.at[m, e - 1])
+            remote(block, block, ag_cross.at[e - 1], ag_x.at[m, e - 1], at(x=partner)).start()
+
+    def next_hop(m, near, shared=False):
         for d in range(1, nz):
-            block = all_gu.at[m, :, lax.rem(z - d + nz, nz), y]
+            zs = lax.rem(z - d + nz, nz)
+            block = all_gu.at[m, :, zs, y]
+            part = all_gu.at[m, :, zs, y, :, span_of(plane * BLOCK, BLOCK, BLOCK)] if shared else block
             along(
-                block, d, near, ag_z.at[m, d - 1], ag_far.at[2], ag_z.at[m, end_slot], ag_relay.at[d - 1], lambda e: ag_y.at[m, e - 1]
+                block, part, True, d, near, ag_z.at[m, d - 1], ag_far.at[2], ag_z.at[m, end_slot], ag_relay.at[d - 1], lambda e: ag_y.at[m, e - 1]
             )
         for q in range(pieces):
             zo, yo, _ = owner(m, q)
@@ -301,10 +334,16 @@
                 block = all_down.at[m, pl.ds(q * gp, gp)]
                 owned(block, zo, near, ag_dz.at[m, q], ag_far.at[3], ag_drelay.at[zo % 2], lambda e: ag_dy.at[m, q])
 
+    def arrived_shared(m):
+        for e in range(1, ny):
+            landed(half_of(m, lax.rem(y - e + ny, ny), 1 - plane), ag_x.at[m, e - 1])
+
+    def arrived(m):
+        for e in range(1, ny):
+            landed(all_gu.at[m, :, :, lax.rem(y - e + ny, ny)], ag_y.at[m, e - 1])
+
     def load(m):
         landed(all_gu.at[m, :, 0, 0], sem_own.at[0, m])
-        for e in range(1, ny):
-            landed(all_gu.at[m, :, :, lax.rem(y - e + ny, ny)], ag_y.at[m, e - 1])
         for q in range(pieces):
             zo, yo, _ = owner(m, q)
             block = all_down.at[m, pl.ds(q * gp, gp)]
@@ -371,19 +410,20 @@
     def _():
         hal[...] = jnp.zeros_like(hal)
 
-    for b in range(6):
-        mixer_hop(b, True)
-        if b > 0:
+    for b in range(8):
+        if b < 6:
+            mixer_hop(b, True)
+        if 0 < b < 7:
             mixer_hop(b - 1, False)
         if b < 3:
             mixer_first_hop(b + 3)
         elif b == 3:
             out_first_hop()
-        else:
-            first_hop(b - 4)
-    mixer_hop(5, False)
-    out_hop(True)
-    out_hop(False)
+        elif b > 5:
+            out_hop(b == 6)
+            first_hop(b - 6, True)
+        if b > 1:
+            mixer_cross(b - 2)
     local(tok_in, act_a.at[mine], sem_in.at[0]).wait()
     landed(act_a.at[mine], sem_pair.at[0])
     landed(act_a.at[other], sem_pair.at[1])
@@ -401,13 +441,17 @@
         return (tokens * row_scale(tokens) * vec[0:1, :]).astype(BF16)
 
     for cc in range(2):
-        edge = normed(hal[cc].astype(F32).reshape(seqs * EDGE, width))
-        for h in range(2):
-            product = dot(edge, win(h)) * dot(edge, win(4 + h))
-            uh[cc * seqs : (cc + 1) * seqs, :, h * CHUNK : (h + 1) * CHUNK] = product.reshape(seqs, EDGE, CHUNK)
+        for k in range(2):
+            edge = normed(hal[cc, k].astype(F32))
+            for h in range(2):
+                hl = slice(h * CHUNK, (h + 1) * CHUNK)
+                uh[k, cc * seqs : (cc + 1) * seqs, hl] = dot(edge, win(h)) * dot(edge, win(4 + h))
 
     def convolve(product, first, h):
-        ub[:, :EDGE, :] = uh[pl.ds(first, tseq), :, h * CHUNK : (h + 1) * CHUNK]
+        for i in range(tseq):
+            for k in range(2):
+                row = EDGE - 2 + k
+                ub[i, row : row + 1, :] = uh[k, pl.ds(first + i, 1), h * CHUNK : (h + 1) * CHUNK]
         ub[:, EDGE:, :] = product.reshape(tseq, span, CHUNK)
         lag_two = ub[:, EDGE - 2 : EDGE - 2 + span, :]
         lag_one = ub[:, EDGE - 1 : EDGE - 1 + span, :]
@@ -440,69 +484,81 @@
             hl = pl.ds(h * CHUNK, CHUNK)
             for i in range(3):
                 dnv[span_of((t % 2) * 3 * TILE + i * TILE, TILE, TILE), hl] = parts[i]
-            chd[pl.ds(first, tseq), :, hl] = parts[1].reshape(tseq, span, CHUNK)[:, :EDGE]
+            for i in range(tseq):
+                for k in range(2):
+                    chd[k, pl.ds(first + i, 1), hl] = parts[1][i * span + k : i * span + k + 1, :]
             conv = convolve(parts[0] * parts[2], first, h)[3].reshape(TILE, CHUNK)
             zv[rs, hl] = (parts[1] * conv).astype(BF16)
         for i in range(3):
             spilled(t, i, rs).start()
         mixed = dot(zv[rs, :], wout[...])
 
+        i = lax.rem(t, tiles)
+        half_rows = span_of(i * TILE, TILE, TILE)
+
+        @pl.when(t == 0)
+        def _():
+            landed(act_a.at[other], sem_spill.at[6])
+
         @pl.when(t < tiles)
         def _():
-            tr[span_of(t * TILE, TILE, TILE), pl.ds(0, width)] = mixed.astype(BF16)
+            tr[half_rows, other] = mixed.astype(BF16)
+            remote(
+                tr.at[half_rows, other], take.at[0, half_rows], sem_half.at[0, i], sem_half.at[1, i], at(c=1 - c)
+            ).start()
+            outv[rs, :] = jnp.zeros((TILE, width), F32)
 
         @pl.when(t >= tiles)
         def _():
-            outv[rs, :] = act_a[rs, :].astype(F32) + mixed
+            landed(take.at[0, half_rows], sem_half.at[1, i])
+            middle = act_a[rs, :].astype(F32) + mixed + take[0, half_rows, :].astype(F32)
+            outv[rs, :] = middle
+            n2 = (middle * row_scale(middle) * vec[1:2, :]).astype(BF16)
+            act_a[rs, :] = n2
+            remote(act_a.at[rs], act_a.at[rs], sem_n2.at[0, i], sem_n2.at[1, i], at(c=1 - c)).start()
+            tr[:, rs] = n2.T
 
         @pl.when(lax.rem(t, tiles) == 1)
         def _():
-            pass_on(t // tiles)
+            next_hop(t // tiles, True, True)
+
+        @pl.when(t == tiles + 1)
+        def _():
+            cross(0)
 
         @pl.when(lax.rem(t, tiles) == tiles - 1)
         def _():
-            pass_on_far(t // tiles)
-
-        @pl.when(t == tiles - 1)
-        def _():
-            landed(act_a.at[other], sem_spill.at[6])
-            remote(tr.at[:, pl.ds(0, width)], take.at[0], sem_pair.at[4], sem_pair.at[5], at(c=1 - c)).start()
+            next_hop(t // tiles, False, True)
+            first_hop(t // tiles + 2)
+
 
     for slot in range(2):
         for i in range(3):
             spilled(slot, i, pl.ds(0, TILE)).wait()
-    landed(take.at[0], sem_pair.at[5])
+    local(outv.at[mine], spill_h, sem_spill.at[7]).start()
+    cross(1)
+
+    @pl.loop(0, tiles)
+    def _(t):
+        half_rows = span_of(t * TILE, TILE, TILE)
+        rs = span_of(c * rows + t * TILE, TILE, TILE)
+        ro = span_of((1 - c) * rows + t * TILE, TILE, TILE)
+        dnv[ro, :] = jnp.zeros((TILE, width), F32)
+        dnv[rs, :] = jnp.zeros((TILE, width), F32)
+        landed(tr.at[half_rows, other], sem_half.at[0, t])
 
     @pl.loop(0, tiles)
     def _(t):
         rs = span_of(c * rows + t * TILE, TILE, TILE)
-        middle = outv[rs, :] + take[0, span_of(t * TILE, TILE, TILE), :].astype(F32)
-        outv[rs, :] = middle
-        act_a[rs, :] = (middle * row_scale(middle) * vec[1:2, :]).astype(BF16)
-
-    remote(act_a.at[mine], act_a.at[mine], sem_pair.at[6], sem_pair.at[7], at(c=1 - c)).start()
-    local(outv.at[mine], spill_h, sem_spill.at[7]).start()
-    landed(take.at[0], sem_pair.at[4])
-
-    @pl.loop(0, tiles)
-    def _(t):
         ro = span_of((1 - c) * rows + t * TILE, TILE, TILE)
-        rs = span_of(c * rows + t * TILE, TILE, TILE)
-        outv[ro, :] = jnp.zeros((TILE, width), F32)
-        dnv[ro, :] = jnp.zeros((TILE, width), F32)
-        dnv[rs, :] = jnp.zeros((TILE, width), F32)
-
-    landed(act_a.at[other], sem_pair.at[7])
-    landed(act_a.at[mine], sem_pair.at[6])
+        landed(act_a.at[rs], sem_n2.at[0, t])
+        landed(act_a.at[ro], sem_n2.at[1, t])
+        tr[:, ro] = act_a[ro, :].T
+
     landed(act_b.at[other], sem_pair.at[3])
     landed(act_b.at[mine], sem_pair.at[2])
-
-    @pl.loop(0, 2 * tiles)
-    def _(t):
-        rs = span_of(t * TILE, TILE, TILE)
-        tr[:, rs] = act_a[rs, :].T
-
     local(outv.at[mine], spill_h, sem_spill.at[7]).wait()
+    arrived_shared(0)
     load(0)
     loaded_weights()
 
@@ -540,6 +596,14 @@
 
             dnv[rs, :] += dot_nt(gg, gate) + dot_nt(gv, up)
 
+        @pl.when(m == 0)
+        def _():
+            arrived_shared(1)
+
+        @pl.when(jnp.logical_and(m >= 1, m + 1 < steps))
+        def _():
+            arrived(m + 1)
+
         @pl.when(m + 1 < steps)
         def _():
             load(m + 1)
@@ -561,21 +625,32 @@
                         j = t * group + k
                         ggu[slot, w, h, j // ny, j % ny] = full[k, h]
 
+    def has_rows(m):
+        return m < chunks - 1
+
     def send_x(m):
         slot = m % slots
         for d in range(1, nx):
             xo = xp(d)
-            remote(ggu.at[slot, :, xo], rxg.at[slot, d - 1], sx_g.at[slot, d - 1], rx_g.at[slot, d - 1], at(x=xo)).start()
-
-            @pl.when(m < chunks - 1)
-            def _():
-                remote(gd.at[slot, xo], rxd.at[slot, d - 1], sx_d.at[slot, d - 1], rx_d.at[slot, d - 1], at(x=xo)).start()
+            remote(ggu.at[slot, :, xo], h0g.at[m, d - 1], sa_g.at[slot], ra_g.at[m], at(x=xo)).start()
+
+            @pl.when(has_rows(m))
+            def _():
+                remote(gd.at[slot, xo], h0d.at[m, d - 1], sa_d.at[slot], ra_d.at[m], at(x=xo)).start()
+
+    def fetch_x(m):
+        landed(h0g.at[m], ra_g.at[m])
+        local(h0g.at[m], vag, ld0.at[0]).start()
+
+        @pl.when(has_rows(m))
+        def _():
+            landed(h0d.at[m], ra_d.at[m])
+            local(h0d.at[m], vad, ld0.at[1]).start()
 
     def sum_x(m):
         slot = m % slots
-        for d in range(1, nx):
-            landed(rxg.at[slot, d - 1], rx_g.at[slot, d - 1])
-            landed(rxg.at[slot, d - 1], sx_g.at[slot, d - 1])
+        landed(h0g.at[m], sa_g.at[slot])
+        landed(vag, ld0.at[0])
 
         @pl.loop(0, nz)
         def _(zi):
@@ -583,19 +658,18 @@
                 for w in range(2):
                     total = ggu[slot, w, x, zi, yi].astype(F32)
                     for d in range(1, nx):
-                        total += rxg[slot, d - 1, w, zi, yi].astype(F32)
+                        total += vag[d - 1, w, zi, yi].astype(F32)
                     s1g[yi, w, zi] = total.astype(BF16)
 
         local(s1g, h1g.at[m], st1.at[0]).start()
 
-        @pl.when(m < chunks - 1)
-        def _():
-            for d in range(1, nx):
-                landed(rxd.at[slot, d - 1], rx_d.at[slot, d - 1])
-                landed(rxd.at[slot, d - 1], sx_d.at[slot, d - 1])
+        @pl.when(has_rows(m))
+        def _():
+            landed(h0d.at[m], sa_d.at[slot])
+            landed(vad, ld0.at[1])
             total = gd[slot, x].astype(F32)
             for d in range(1, nx):
-                total += rxd[slot, d - 1].astype(F32)
+                total += vad[d - 1].astype(F32)
             s1d[...] = total.astype(BF16)
             copy = local(s1d, h1d.at[m], st1.at[1])
             copy.start()
@@ -608,7 +682,7 @@
             yo = yp(d)
             remote(h1g.at[m, yo], hyg.at[m, d - 1], sy_g.at[m], ry_g.at[m], at(y=yo)).start()
 
-        @pl.when(m < chunks - 1)
+        @pl.when(has_rows(m))
         def _():
             for q in range(pieces):
                 _, yo, _ = grad_owner(m, q)
@@ -709,9 +783,39 @@
         d, e = reps[p]
         return at(x=xp(d), c=lax.rem(c + e, 2))
 
+    direct_reps = [p for p, (d, e) in enumerate(reps) if d == 0 or e == 0]
+
     def spread(there, ssem, rsem):
-        for p in range(len(reps)):
+        for p in direct_reps:
             remote(there, there, ssem.at[p], rsem.at[p], rep(p)).start()
+
+    def own_gu(xs, cs):
+        return gu_full.at[:, pl.ds(pl.multiple_of(xs * dnx, dnx), dnx), span_of(cs * half, half, BLOCK)]
+
+    def own_in(xs, k):
+        return in_full.at[
+            pl.ds(pl.multiple_of(xs * dnx, dnx), dnx), span_of(k * width + c * chan, chan, chan)
+        ]
+
+    in_size = in_full.at[pl.ds(0, dnx), pl.ds(0, 3 * chan)]
+
+    def own_lanes(ref, xs):
+        return ref.at[:, span_of(xs * lanes, lanes, BLOCK)]
+
+    def hand_over(mixer):
+        for d in range(1, nx):
+            p, q = reps.index((d, 0)), reps.index((d, 1))
+            xs = lax.rem(x - d + nx, nx)
+            sems = (fs_i, fr_i) if mixer else (fs_g, fr_g)
+            landed(in_size if mixer else own_gu(xs, c), sems[1].at[p])
+            for part in [own_in(xs, k) for k in range(3)] if mixer else [own_gu(xs, c)]:
+                remote(part, part, sems[0].at[q], sems[1].at[q], at(c=1 - c)).start()
+
+            @pl.when(in_half)
+            def _():
+                part = own_lanes(out_full if mixer else down_full, xs)
+                landed(part, (fr_o if mixer else fr_d).at[p])
+                remote(part, part, (fs_o if mixer else fs_d).at[q], (fr_o if mixer else fr_d).at[q], at(c=1 - c)).start()
 
     def finish(m, i):
         copies, late = z_copies(m, i)
@@ -727,7 +831,9 @@
         def _():
             b = blocks(m)
             for k in range(2):
-                there = gu_full.at[x, c, :, :, span_of(b[k] * BLOCK, BLOCK, BLOCK)]
+                there = gu_full.at[
+                    :, pl.ds(pl.multiple_of(x * dnx, dnx), dnx), span_of(c * half + b[k] * BLOCK, BLOCK, BLOCK)
+                ]
                 copy = local(fing.at[:, :, pl.ds(k * BLOCK, BLOCK)], there, st3.at[0])
                 copy.start()
                 copy.wait()
@@ -735,11 +841,15 @@
 
         @pl.when(m >= steps)
         def _():
-            there = in_full.at[x, c, pl.ds(2 * (m - steps), 2)]
-            copy = local(fing, there, st3.at[0])
-            copy.start()
-            copy.wait()
-            spread(there, fs_i, fr_i)
+            for w in range(2):
+                there = in_full.at[
+                    pl.ds(pl.multiple_of(x * dnx, dnx), dnx),
+                    span_of((m - steps) * width + c * chan + w * CHUNK, CHUNK, CHUNK),
+                ]
+                copy = local(fing.at[w], there, st3.at[0])
+                copy.start()
+                copy.wait()
+                spread(there, fs_i, fr_i)
 
         @pl.when(m < chunks - 1)
         def _():
@@ -758,7 +868,7 @@
 
                     @pl.when(m < steps)
                     def _():
-                        there = down_full.at[x, pl.ds(row, gp)]
+                        there = down_full.at[pl.ds(row, gp), span_of(x * lanes, lanes, BLOCK)]
                         copy = local(find, there, st3.at[1])
                         copy.start()
                         copy.wait()
@@ -766,14 +876,14 @@
 
                     @pl.when(m >= steps)
                     def _():
-                        there = out_full.at[x, pl.ds(row, gp)]
+                        there = out_full.at[pl.ds(row, gp), span_of(x * lanes, lanes, BLOCK)]
                         copy = local(find, there, st3.at[1])
                         copy.start()
                         copy.wait()
                         spread(there, fs_o, fr_o)
 
     def gone(m):
-        return jnp.clip(jnp.minimum(m, 2 * (m - HOLD)), 0, chunks)
+        return jnp.clip(jnp.minimum(m - 1, 2 * (m - HOLD)), 0, chunks)
 
     def two(m, do):
         for i in range(2):
@@ -816,15 +926,17 @@
         local(smallv.at[0], small_out, sem_in.at[0]).start()
 
     def give_sums():
-        for i, src in enumerate((dnv, outv)):
-            side = pl.ds((1 - i) * width, width)
-
-            @pl.loop(0, tiles)
-            def _(t):
-                ro = span_of((1 - c) * rows + t * TILE, TILE, TILE)
-                tr[span_of(t * TILE, TILE, TILE), side] = src[ro, :].astype(BF16)
-
-            remote(tr.at[:, side], take.at[1 - i], sem_pair.at[8 + 2 * i], sem_pair.at[9 + 2 * i], at(c=1 - c)).start()
+        @pl.loop(0, tiles)
+        def _(t):
+            rl = span_of(t * TILE, TILE, TILE)
+            ro = span_of((1 - c) * rows + t * TILE, TILE, TILE)
+            for i, src in enumerate((outv, dnv)):
+                side = pl.ds(i * width, width)
+                tr[rl, side] = src[ro, :].astype(BF16)
+                remote(
+                    tr.at[rl, side], take.at[i, rl], sem_sums.at[i, t], sem_sums.at[2 + i, t], at(c=1 - c)
+                ).start()
+
         local(spill_h, outv.at[other], sem_spill.at[7]).start()
         local(tok_in, act_a.at[mine], sem_in.at[0]).start()
         local(spill_t, act_a.at[other], sem_spill.at[6]).start()
@@ -838,9 +950,6 @@
         mixer_load()
         conv_acc[...] = jnp.zeros_like(conv_acc)
         sg[...] = jnp.zeros_like(sg)
-        for i in range(2):
-            landed(take.at[1 - i], sem_pair.at[9 + 2 * i])
-            landed(take.at[1 - i], sem_pair.at[8 + 2 * i])
         local(spill_h, outv.at[other], sem_spill.at[7]).wait()
         for i in range(3):
             loaded(0, i).start()
@@ -850,6 +959,9 @@
             rl = span_of(t * TILE, TILE, TILE)
             rs = span_of(c * rows + t * TILE, TILE, TILE)
             ro = span_of((1 - c) * rows + t * TILE, TILE, TILE)
+            for i in range(2):
+                landed(take.at[i, rl], sem_sums.at[2 + i, t])
+                landed(take.at[i, rl], sem_sums.at[i, t])
             total = outv[rs, :] + take[0, rl, :].astype(F32)
             tr[rl, pl.ds(0, width)] = (total * live_in[rl, :]).astype(BF16)
             dn2 = dnv[rs, :] + take[1, rl, :].astype(F32)
@@ -862,10 +974,10 @@
             back = act_b[rs, :].astype(F32) + back
             dnv[rs, :] = back
             act_b[rs, :] = back.astype(BF16)
+            remote(act_b.at[rs], act_b.at[rs], sem_dm.at[0, t], sem_dm.at[1, t], at(c=1 - c)).start()
 
         out = local(tr.at[:, pl.ds(0, width)], y_out, sem_in.at[1])
         out.start()
-        remote(act_b.at[mine], act_b.at[mine], sem_pair.at[2], sem_pair.at[3], at(c=1 - c)).start()
         local(tok_in, act_a.at[mine], sem_in.at[0]).wait()
         local(spill_t, act_a.at[other], sem_spill.at[6]).wait()
         out.wait()
@@ -875,17 +987,22 @@
             rs = span_of(t * TILE, TILE, TILE)
             tr[:, rs] = normed(act_a[rs, :].astype(F32)).T
 
-        landed(act_b.at[mine], sem_pair.at[2])
-        landed(act_b.at[other], sem_pair.at[3])
+        @pl.loop(0, tiles)
+        def _(t):
+            landed(act_b.at[span_of(c * rows + t * TILE, TILE, TILE)], sem_dm.at[0, t])
+            landed(act_b.at[span_of((1 - c) * rows + t * TILE, TILE, TILE)], sem_dm.at[1, t])
 
         for cc in range(2):
 
             @pl.loop(0, seqs)
             def _(s):
-                hf[span_of(s * EDGE, EDGE, EDGE), :] = act_b[span_of(cc * rows + s * span, EDGE, span), :].astype(F32)
-
-            head = dot_nt(hf[...].astype(BF16), wout[...]).reshape(seqs, EDGE, chan)
-            ks[cc * seqs : (cc + 1) * seqs] = head * chd[cc * seqs : (cc + 1) * seqs]
+                head = act_b[span_of(cc * rows + s * span, EDGE, span), :].astype(F32)
+                for k in range(2):
+                    hf[k, pl.ds(s, 1), :] = head[k : k + 1, :]
+
+            for k in range(2):
+                own = slice(cc * seqs, (cc + 1) * seqs)
+                ks[k, own, :] = dot_nt(hf[k].astype(BF16), wout[...]) * chd[k, own, :]
 
         @pl.when(me > 0)
         def _():
@@ -931,7 +1048,9 @@
                 for k in range(3):
                     conv_acc[k : k + 1, hl] += jnp.sum((dk * lags[k]).reshape(TILE, CHUNK), axis=0, keepdims=True)
                 vb[:, :span, :] = dk
-                vb[:, span:, :] = kh[pl.ds(first, tseq), :, hl]
+                for i in range(tseq):
+                    for k in range(2):
+                        vb[i, span + k : span + k + 1, :] = kh[k, pl.ds(first + i, 1), hl]
                 du = tap(2, h) * dk + tap(1, h) * vb[:, 1 : 1 + span, :] + tap(0, h) * vb[:, 2 : 2 + span, :]
                 act_a[rs, hl] = (du * x_value).astype(BF16).reshape(TILE, CHUNK)
                 act_a[rs, pl.ds(chan + h * CHUNK, CHUNK)] = (dz * conv).astype(BF16).reshape(TILE, CHUNK)
@@ -980,7 +1099,7 @@
         sg[2:5, span_of(c * chan, chan, chan)] = conv_acc[0:3, :]
         sum_reps()
 
-    @pl.loop(0, chunks + 3)
+    @pl.loop(0, chunks + 4)
     def _(m):
         @pl.when(m < steps)
         def _():
@@ -1009,17 +1128,22 @@
         def _():
             weight_grads(m % slots, zv[:, :CHUNK], zv[:, CHUNK:])
 
-        @pl.when(jnp.logical_and(m >= 1, m < chunks + 1))
-        def _():
-            sum_x(m - 1)
-
         @pl.when(m < chunks)
         def _():
             send_x(m)
+
+        @pl.when(jnp.logical_and(m >= 2, m < chunks + 2))
+        def _():
+            fetch_x(m - 2)
 
         two(m - 1, fetch_y)
         two(m - 2, fetch_z)
         pass_on_far(m + RELAY)
+
+        @pl.when(jnp.logical_and(m >= 2, m < chunks + 2))
+        def _():
+            sum_x(m - 2)
+
         two(m, send_y)
         two(m - 1, send_z)
         two(m - 2, finish)
@@ -1039,6 +1163,7 @@
         @pl.when(m == chunks + 1)
         def _():
             sum_last()
+            hand_over(False)
 
         @pl.when(m + 1 < steps)
         def _():
@@ -1066,14 +1191,15 @@
                 def _():
                     landed(h2d.at[m, part], sz_d.at[m, q])
 
+    hand_over(True)
     for p in range(len(reps)):
-        landed(gu_full.at[0, 0], fs_g.at[p])
-        landed(in_full.at[0, 0], fs_i.at[p])
+        landed(own_gu(0, 0), fs_g.at[p])
+        landed(in_size, fs_i.at[p])
 
         @pl.when(in_half)
         def _():
-            landed(down_full.at[0], fs_d.at[p])
-            landed(out_full.at[0], fs_o.at[p])
+            landed(own_lanes(down_full, 0), fs_d.at[p])
+            landed(own_lanes(out_full, 0), fs_o.at[p])
     landed(take.at[0], sem_pair.at[4])
 
     @pl.when(me > 0)
@@ -1085,8 +1211,8 @@
 
         @pl.when(direct)
         def _():
-            landed(all_in.at[:, 0, 0], mg_send.at[p])
-            landed(all_gu.at[:, :, 0, 0], ag_send.at[p])
+            landed(all_in.at[pl.ds(0, 3) if ax else pl.ds(0, 6), 0, 0], mg_send.at[p])
+            landed(all_gu.at[pl.ds(0, steps - ax), :, 0, 0], ag_send.at[p])
 
         @pl.when(jnp.logical_and(direct, in_half))
         def _():
@@ -1105,8 +1231,11 @@
 
     for d in range(1, nz):
         for e in range(1, ny):
-            landed(all_in.at[:, 0, 0], mg_relay.at[d - 1, e - 1])
-            landed(all_gu.at[:, :, 0, 0], ag_relay.at[d - 1, e - 1])
+            landed(all_in.at[pl.ds(0, 3), 0, 0], mg_relay.at[d - 1, e - 1])
+            landed(all_gu.at[pl.ds(0, steps - 1), :, 0, 0], ag_relay.at[d - 1, e - 1])
+    for e in range(1, ny):
+        landed(all_in.at[pl.ds(0, 3), :, 0], mg_cross.at[e - 1])
+        landed(all_gu.at[0, :, :, 0], ag_cross.at[e - 1])
     for o in range(n // 2):
         zo, yo = out_owner(o)
 
@@ -1124,13 +1253,14 @@
                 landed(all_down.at[:, pl.ds(0, gp)], ag_drelay.at[zo % 2, e - 1])
 
     for p, (d, e) in enumerate(reps):
-        landed(gu_full.at[0, 0], fr_g.at[p])
-        landed(in_full.at[0, 0], fr_i.at[p])
-
-        @pl.when(in_half if e == 0 else jnp.logical_not(in_half))
-        def _():
-            landed(down_full.at[0], fr_d.at[p])
-            landed(out_full.at[0], fr_o.at[p])
+        if d == 0 or e == 1:
+            landed(own_gu(0, 0), fr_g.at[p])
+            landed(in_size, fr_i.at[p])
+
+            @pl.when(jnp.logical_not(in_half))
+            def _():
+                landed(own_lanes(down_full, 0), fr_d.at[p])
+                landed(own_lanes(out_full, 0), fr_o.at[p])
 
 
 def block_call(sizes, *operands):
@@ -1148,6 +1278,7 @@
     lanes = width // nx
     chunks = steps + 3
     tseq = TILE // span
+    tiles = rows // TILE
     reps = 2 * nx - 1
     hops = nz + ny - 2
     dma = lambda *dims: pltpu.SemaphoreType.DMA(dims)
@@ -1162,10 +1293,10 @@
         out_shape=[
             shape((rows, width), BF16),
             shape((rows, width), BF16),
-            shape((nx, 2, 2, dnx, half), BF16),
-            shape((nx, own_rows, lanes), BF16),
-            shape((nx, 2, 6, dnx, CHUNK), BF16),
-            shape((nx, dn, lanes), BF16),
+            shape((2, dn, hidden), BF16),
+            shape((own_rows, width), BF16),
+            shape((dn, 3 * width), BF16),
+            shape((dn, width), BF16),
             shape((8, dn), F32),
             shape((steps, 2, nz, ny, dn, CHUNK), BF16),
             shape((steps, CHUNK, width), BF16),
@@ -1174,6 +1305,8 @@
             shape((3, 2 * rows, chan), F32),
             shape((rows, width), F32),
             shape((rows, width), BF16),
+            shape((chunks, nx - 1, 2, nz, ny, dnx, CHUNK), BF16),
+            shape((chunks, nx - 1, CHUNK, lanes), BF16),
             shape((chunks, ny, 2, nz, dnx, CHUNK), BF16),
             shape((chunks, CHUNK, lanes), BF16),
             shape((chunks, ny - 1, 2, nz, dnx, CHUNK), BF16),
@@ -1184,7 +1317,7 @@
             shape((chunks, nz - 1, CHUNK, lanes), BF16),
         ],
         in_specs=specs,
-        out_specs=[anywhere] * 22,
+        out_specs=[anywhere] * 24,
         scratch_shapes=[
             bf(2 * rows, width),
             bf(2 * rows, width),
@@ -1197,15 +1330,14 @@
             bf(chan, width),
             bf(2 * rows, chan),
             bf(2, rows, width),
-            bf(nx, CHUNK, lanes),
             fl(tseq, span + EDGE, CHUNK),
             fl(tseq, span + EDGE, CHUNK),
-            bf(2, seqs, EDGE, width),
-            fl(2 * seqs, EDGE, chan),
-            fl(2 * seqs, EDGE, chan),
-            fl(2 * seqs, EDGE, chan),
-            fl(2 * seqs, EDGE, chan),
-            fl(seqs * EDGE, width),
+            bf(2, 2, seqs, width),
+            fl(2, 2 * seqs, chan),
+            fl(2, 2 * seqs, chan),
+            fl(2, 2 * seqs, chan),
+            fl(2, 2 * seqs, chan),
+            fl(2, seqs, width),
             fl(n, 8, dn),
             fl(8, width),
             fl(8, chan),
@@ -1213,12 +1345,13 @@
             fl(2 * nx, 8, width),
             fl(n, 8, dn),
             fl(n, 8, dn),
-            bf(2, 2, nx, nz, ny, dnx, CHUNK),
-            bf(2, nx, CHUNK, lanes),
-            bf(2, nx - 1, 2, nz, ny, dnx, CHUNK),
-            bf(2, nx - 1, CHUNK, lanes),
+            bf(3, 2, nx, nz, ny, dnx, CHUNK),
+            bf(3, nx, CHUNK, lanes),
+            bf(nx - 1, 2, nz, ny, dnx, CHUNK),
+            bf(nx - 1, CHUNK, lanes),
             bf(ny, 2, nz, dnx, CHUNK),
             bf(CHUNK, lanes),
+            bf(nx, CHUNK, lanes),
             bf(2, 2, nz, dnx, CHUNK),
             bf(2, CHUNK, lanes),
             bf(2, ny - 1, 2, nz, dnx, CHUNK),
@@ -1232,11 +1365,19 @@
             dma(2),
             dma(2 + n // 2),
             dma(2, steps * pieces),
-            dma(12),
+            dma(6),
+            dma(2, tiles),
+            dma(2, tiles),
+            dma(4, tiles),
+            dma(2, tiles),
             dma(3),
             dma(4),
             dma(2),
             dma(8),
+            dma(ny - 1),
+            dma(SHARED, ny - 1),
+            dma(ny - 1),
+            dma(6, ny - 1),
             dma(4),
             dma(steps, nz - 1),
             dma(steps, ny - 1),
@@ -1255,10 +1396,11 @@
             dma(nz - 1, ny - 1),
             dma(hops),
             dma(n // 2, ny - 1),
-            dma(2, nx - 1),
-            dma(2, nx - 1),
-            dma(2, nx - 1),
-            dma(2, nx - 1),
+            dma(chunks),
+            dma(chunks),
+            dma(3),
+            dma(3),
+            dma(2),
             dma(2),
             dma(chunks),
             dma(chunks, pieces),
@@ -1320,7 +1462,7 @@
     block_out, block_grad, gu, down, mixer_in, mixer_out, sums = block_call(
         (nx, nz, ny, seqs, span, width, hidden),
         tokens.reshape(-1, width),
-        tokens,
+        tokens[:, span - 2 :].transpose(1, 0, 2),
         cotangent.reshape(-1, width),
         live_mask(lengths, deal, span),
         small,
@@ -1330,23 +1472,17 @@
         up_weight,
         down_weight,
     )
-    gate_grad = gu[:, :, 0].transpose(0, 2, 1, 3).reshape(dn, hidden).astype(F32)
-    up_grad = gu[:, :, 1].transpose(0, 2, 1, 3).reshape(dn, hidden).astype(F32)
-    mixer_in = mixer_in.reshape(nx, 2, 3, 2, dn // nx, CHUNK)
-    in_grad = mixer_in.transpose(0, 4, 2, 1, 3, 5).reshape(dn, 3 * width).astype(F32)
-    out_grad = mixer_out.transpose(1, 0, 2).reshape(dn, width).astype(F32)
-    down_grad = down.transpose(1, 0, 2).reshape(-1, width).astype(F32)
     return (
         block_out.reshape(tokens.shape),
         block_grad.reshape(tokens.shape),
         sums[0],
-        in_grad,
+        mixer_in.astype(F32),
         sums[2:5].T,
-        out_grad,
+        mixer_out.astype(F32),
         sums[1],
-        gate_grad,
-        up_grad,
-        down_grad,
+        gu[0].astype(F32),
+        gu[1].astype(F32),
+        down.astype(F32),
     )
 
 

time: 454 us -> 390 us (0.86)
  Pallas kernels: 426 us -> 367 us
  local copies, waits for them, and re-layouts: 22.9 us -> 10.7 us
  other arithmetic: 3.34 us -> 10.2 us
    pallas_call x1, Pallas kernels: 426 us -> 367 us  [block_call(): pl.pallas_call(functools.partial(block_kernel, sizes), out_shape=[shape((...]
    convert_element_type x6 -> x0, local copies, waits for them, and re-layouts: 9.11 us -> none  [the longest x2 3.62 us: body(): mixer_in.transpose(0, 4, 2, 1, 3, 5).reshape(dn, 3 * width).astype(F32)]
    convert_element_type x3 -> x4, other arithmetic: 1.59 us -> 8.8 us  [the longest x1 2.74 us: body(): gu[1].astype(F32)]
where the time goes in v5:
time: 390 us; the launch traced here: 389 us
  Pallas kernels  367 us (94%)
  local copies, waits for them, and re-layouts  10.7 us (3%)
  other arithmetic  10.2 us (3%)
    pallas_call x1, Pallas kernels, block_call(): pl.pallas_call(functools.partial(block_kernel, sizes), out_shape=[shape((...  367 us

profile of v5, /device:TPU:0, one launch (start us, length us, event | category | flops | bytes accessed | tf_op | source)
XLA Modules:
  0.0 388.8 jit_solution(13443561636011442409)
XLA Ops:
  0.7 0.8 select_reduce_fusion
  1.4 0.8 slice_bitcast_fusion.3
  2.2 0.7 stack.11
  2.9 0.6 pad_convert_fusion.small_in
  3.5 0.1 compare_convert_fusion
  3.6 1.0 slice.27
  4.6 0.6 copy.29
  5.2 1.3 reshape.78.live_in
  6.5 367.2 %gated_block.1 = (bf16[1024,1024]{1,0:T(8,128)(2,1)}, bf16[1024,1024]{1,0:T(8,128)(2,1)}, bf16[2,128,4608]{2,1,0:T(8,128)(2,1)}, bf16[576,1024]{1,0:T(8,128)(2,1...) custom-call(bf16[1024,1024]{1,0:T(8,128)(2,1)} %bitcast.29, ...), custom_call_target="tpu_custom_call" | custom-call | tf_op jit(solution)/shard_map/gated_block/pallas_call | solution.py:1291
  373.7 0.0 copy-start.3
  373.8 1.3 slice_bitcast_fusion.1
  375.1 1.3 slice_bitcast_fusion
  376.3 1.8 convert_element_type.40
  378.1 0.0 copy-start
  378.1 2.6 convert_element_type.39
  380.7 0.0 copy-done.3
  380.7 1.7 convert_element_type.45
  382.4 0.0 copy-done
  382.4 0.0 copy-start.2
  382.4 2.7 bitcast_convert_fusion
  385.1 0.0 copy-start.1
  385.1 0.0 copy-done.2
  385.1 1.3 copy.32
  386.5 1.0 copy-done.1
  387.5 1.3 copy.33
  (1 shorter events, 0.0 us)
Async XLA Ops:
  373.7 7.0 %copy-start.3 = (bf16[576,1024]{1,0:T(8,128)(2,1)S(1)}, bf16[576,1024]{1,0:T(8,128)(2,1)}, u32[]{:S(2)}) copy-start(bf16[576,1024]{1,0:T(8,128)(2,1)} %get-tuple-element.23) | copy-start | bytes 3538948
  378.1 4.3 %copy-start = (bf16[2,128,4608]{2,1,0:T(8,128)(2,1)S(1)}, bf16[2,128,4608]{2,1,0:T(8,128)(2,1)}, u32[]{:S(2)}) copy-start(bf16[2,128,4608]{2,1,0:T(8,128)(2,1)} %get-tuple-element.22) | copy-start | bytes 7077892
  382.4 2.7 copy-start.2
  385.1 2.3 copy-start.1

commit v6 on v5

--- a/solution.py
+++ b/solution.py
@@ -826,61 +826,81 @@
             for d in range(1, nz):
                 total += zrg[i, d - 1, w].astype(F32)
             fing[w] = total.astype(BF16)
+        part_rows = pl.ds(pl.multiple_of(x * dnx, dnx), dnx)
+        part_lanes = span_of(x * lanes, lanes, BLOCK)
+        b = blocks(jnp.minimum(m, steps - 1))
+
+        def gu_place(k):
+            return gu_full.at[:, part_rows, span_of(c * half + b[k] * BLOCK, BLOCK, BLOCK)]
+
+        def in_place(w):
+            start = jnp.maximum(m - steps, 0) * width + c * chan + w * CHUNK
+            return in_full.at[part_rows, span_of(start, CHUNK, CHUNK)]
+
+        def owned_rows(do):
+            @pl.when(m < chunks - 1)
+            def _():
+                for q in range(pieces):
+                    zo, yo, row = grad_owner(m, q)
+
+                    @pl.when(jnp.logical_and(yo == y, zo == z))
+                    def _():
+                        do(q, pl.ds(q * gp, gp), pl.ds(row, gp))
 
         @pl.when(m < steps)
         def _():
-            b = blocks(m)
             for k in range(2):
-                there = gu_full.at[
-                    :, pl.ds(pl.multiple_of(x * dnx, dnx), dnx), span_of(c * half + b[k] * BLOCK, BLOCK, BLOCK)
-                ]
-                copy = local(fing.at[:, :, pl.ds(k * BLOCK, BLOCK)], there, st3.at[0])
-                copy.start()
-                copy.wait()
-                spread(there, fs_g, fr_g)
+                local(fing.at[:, :, pl.ds(k * BLOCK, BLOCK)], gu_place(k), st3.at[0]).start()
 
         @pl.when(m >= steps)
         def _():
             for w in range(2):
-                there = in_full.at[
-                    pl.ds(pl.multiple_of(x * dnx, dnx), dnx),
-                    span_of((m - steps) * width + c * chan + w * CHUNK, CHUNK, CHUNK),
-                ]
-                copy = local(fing.at[w], there, st3.at[0])
-                copy.start()
-                copy.wait()
-                spread(there, fs_i, fr_i)
+                local(fing.at[w], in_place(w), st3.at[0]).start()
 
         @pl.when(m < chunks - 1)
         def _():
             for copy in late:
                 copy.wait()
-            for q in range(pieces):
-                zo, yo, row = grad_owner(m, q)
-                part = pl.ds(q * gp, gp)
-
-                @pl.when(jnp.logical_and(yo == y, zo == z))
-                def _():
-                    total = z2d[i, part].astype(F32)
-                    for d in range(1, nz):
-                        total += zrd[i, d - 1, part].astype(F32)
-                    find[...] = total.astype(BF16)
-
-                    @pl.when(m < steps)
-                    def _():
-                        there = down_full.at[pl.ds(row, gp), span_of(x * lanes, lanes, BLOCK)]
-                        copy = local(find, there, st3.at[1])
-                        copy.start()
-                        copy.wait()
-                        spread(there, fs_d, fr_d)
-
-                    @pl.when(m >= steps)
-                    def _():
-                        there = out_full.at[pl.ds(row, gp), span_of(x * lanes, lanes, BLOCK)]
-                        copy = local(find, there, st3.at[1])
-                        copy.start()
-                        copy.wait()
-                        spread(there, fs_o, fr_o)
+
+        def add_rows(q, part, rows_at):
+            total = z2d[i, part].astype(F32)
+            for d in range(1, nz):
+                total += zrd[i, d - 1, part].astype(F32)
+            find[part] = total.astype(BF16)
+
+            @pl.when(m < steps)
+            def _():
+                local(find.at[part], down_full.at[rows_at, part_lanes], st3.at[1 + q]).start()
+
+            @pl.when(m >= steps)
+            def _():
+                local(find.at[part], out_full.at[rows_at, part_lanes], st3.at[1 + q]).start()
+
+        def spread_rows(q, part, rows_at):
+            landed(find.at[part], st3.at[1 + q])
+
+            @pl.when(m < steps)
+            def _():
+                spread(down_full.at[rows_at, part_lanes], fs_d, fr_d)
+
+            @pl.when(m >= steps)
+            def _():
+                spread(out_full.at[rows_at, part_lanes], fs_o, fr_o)
+
+        owned_rows(add_rows)
+        landed(fing, st3.at[0])
+
+        @pl.when(m < steps)
+        def _():
+            for k in range(2):
+                spread(gu_place(k), fs_g, fr_g)
+
+        @pl.when(m >= steps)
+        def _():
+            for w in range(2):
+                spread(in_place(w), fs_i, fr_i)
+
+        owned_rows(spread_rows)
 
     def gone(m):
         return jnp.clip(jnp.minimum(m - 1, 2 * (m - HOLD)), 0, chunks)
@@ -1361,7 +1381,7 @@
             bf(2, nz - 1, 2, dnx, CHUNK),
             bf(2, nz - 1, CHUNK, lanes),
             bf(2, dnx, CHUNK),
-            bf(gp, lanes),
+            bf(CHUNK, lanes),
             dma(2),
             dma(2 + n // 2),
             dma(2, steps * pieces),
@@ -1413,7 +1433,7 @@
             dma(chunks),
             dma(chunks, pieces),
             dma(2, 4),
-            dma(2),
+            dma(1 + pieces),
             dma(reps),
             dma(reps),
             dma(reps),

time: 390 us -> 388 us (level)
  no operation moved by 1% of the time
where the time goes in v6:
time: 388 us; the launch traced here: 387 us
  Pallas kernels  366 us (94%)
  local copies, waits for them, and re-layouts  10.7 us (3%)
  other arithmetic  10.2 us (3%)
    pallas_call x1, Pallas kernels, block_call(): pl.pallas_call(functools.partial(block_kernel, sizes), out_shape=[shape((...  366 us

profile of v6, /device:TPU:0, one launch (start us, length us, event | category | flops | bytes accessed | tf_op | source)
XLA Modules:
  0.0 387.4 jit_solution(9569651537544387385)
XLA Ops:
  0.7 0.8 select_reduce_fusion
  1.4 0.8 slice_bitcast_fusion.3
  2.2 0.7 stack.11
  2.9 0.6 pad_convert_fusion.small_in
  3.5 0.1 compare_convert_fusion
  3.6 1.0 slice.27
  4.6 0.6 copy.29
  5.2 1.3 reshape.78.live_in
  6.5 365.9 %gated_block.1 = (bf16[1024,1024]{1,0:T(8,128)(2,1)}, bf16[1024,1024]{1,0:T(8,128)(2,1)}, bf16[2,128,4608]{2,1,0:T(8,128)(2,1)}, bf16[576,1024]{1,0:T(8,128)(2,1...) custom-call(bf16[1024,1024]{1,0:T(8,128)(2,1)} %bitcast.29, ...), custom_call_target="tpu_custom_call" | custom-call | tf_op jit(solution)/shard_map/gated_block/pallas_call | solution.py:1311
  372.4 0.0 copy-start.3
  372.4 1.3 slice_bitcast_fusion.1
  373.7 1.3 slice_bitcast_fusion
  375.0 1.8 convert_element_type.40
  376.8 0.0 copy-start
  376.8 2.6 convert_element_type.39
  379.3 0.0 copy-done.3
  379.3 1.7 convert_element_type.45
  381.0 0.0 copy-done
  381.0 0.0 copy-start.2
  381.0 2.7 bitcast_convert_fusion
  383.8 0.0 copy-start.1
  383.8 0.0 copy-done.2
  383.8 1.3 copy.32
  385.1 1.0 copy-done.1
  386.1 1.3 copy.33
  (1 shorter events, 0.0 us)
Async XLA Ops:
  372.4 7.0 %copy-start.3 = (bf16[576,1024]{1,0:T(8,128)(2,1)S(1)}, bf16[576,1024]{1,0:T(8,128)(2,1)}, u32[]{:S(2)}) copy-start(bf16[576,1024]{1,0:T(8,128)(2,1)} %get-tuple-element.23) | copy-start | bytes 3538948
  376.8 4.3 %copy-start = (bf16[2,128,4608]{2,1,0:T(8,128)(2,1)S(1)}, bf16[2,128,4608]{2,1,0:T(8,128)(2,1)}, u32[]{:S(2)}) copy-start(bf16[2,128,4608]{2,1,0:T(8,128)(2,1)} %get-tuple-element.22) | copy-start | bytes 7077892
  381.0 2.7 copy-start.2
  383.8 2.3 copy-start.1

commit v7 on v6

--- a/solution.py
+++ b/solution.py
@@ -613,11 +613,12 @@
             gd[slot, h] = dot_tn(hid(0), act_b[:, pl.ds(h * lanes, lanes)]).astype(BF16)
 
     def weight_grads(slot, first, second):
-        group = n // 4
-
-        @pl.loop(0, 4)
+        group = n // 2
+        depth = width // 2
+
+        @pl.loop(0, 2)
         def _(t):
-            a = tr[span_of(t * TILE, TILE, TILE), :]
+            a = tr[span_of(t * depth, depth, depth), :]
             for w, src in enumerate((first, second)):
                 full = dot(a, src).astype(BF16).reshape(group, nx, dnx, CHUNK)
                 for h in range(nx):

time: 388 us -> 387 us (level)
  no operation moved by 1% of the time
where the time goes in v7:
time: 387 us; the launch traced here: 386 us
  Pallas kernels  365 us (94%)
  local copies, waits for them, and re-layouts  10.7 us (3%)
  other arithmetic  10.2 us (3%)
    pallas_call x1, Pallas kernels, block_call(): pl.pallas_call(functools.partial(block_kernel, sizes), out_shape=[shape((...  365 us

profile of v7, /device:TPU:0, one launch (start us, length us, event | category | flops | bytes accessed | tf_op | source)
XLA Modules:
  0.0 386.4 jit_solution(1084918027506560244)
XLA Ops:
  0.7 0.8 select_reduce_fusion
  1.4 0.8 slice_bitcast_fusion.3
  2.2 0.7 stack.11
  2.9 0.6 pad_convert_fusion.small_in
  3.5 0.1 compare_convert_fusion
  3.6 1.0 slice.27
  4.6 0.6 copy.29
  5.2 1.3 reshape.78.live_in
  6.5 364.9 %gated_block.1 = (bf16[1024,1024]{1,0:T(8,128)(2,1)}, bf16[1024,1024]{1,0:T(8,128)(2,1)}, bf16[2,128,4608]{2,1,0:T(8,128)(2,1)}, bf16[576,1024]{1,0:T(8,128)(2,1...) custom-call(bf16[1024,1024]{1,0:T(8,128)(2,1)} %bitcast.29, ...), custom_call_target="tpu_custom_call" | custom-call | tf_op jit(solution)/shard_map/gated_block/pallas_call | solution.py:1312
  371.4 0.0 copy-start.3
  371.4 1.3 slice_bitcast_fusion.1
  372.7 1.3 slice_bitcast_fusion
  374.0 1.8 convert_element_type.40
  375.8 0.0 copy-start
  375.8 2.6 convert_element_type.39
  378.3 0.0 copy-done.3
  378.3 1.7 convert_element_type.45
  380.0 0.0 copy-done
  380.0 0.0 copy-start.2
  380.0 2.7 bitcast_convert_fusion
  382.8 0.0 copy-start.1
  382.8 0.0 copy-done.2
  382.8 1.3 copy.32
  384.1 1.0 copy-done.1
  385.1 1.3 copy.33
  (1 shorter events, 0.0 us)
Async XLA Ops:
  371.4 7.0 %copy-start.3 = (bf16[576,1024]{1,0:T(8,128)(2,1)S(1)}, bf16[576,1024]{1,0:T(8,128)(2,1)}, u32[]{:S(2)}) copy-start(bf16[576,1024]{1,0:T(8,128)(2,1)} %get-tuple-element.23) | copy-start | bytes 3538948
  375.8 4.3 %copy-start = (bf16[2,128,4608]{2,1,0:T(8,128)(2,1)S(1)}, bf16[2,128,4608]{2,1,0:T(8,128)(2,1)}, u32[]{:S(2)}) copy-start(bf16[2,128,4608]{2,1,0:T(8,128)(2,1)} %get-tuple-element.22) | copy-start | bytes 7077892
  380.0 2.7 copy-start.2
  382.8 2.3 copy-start.1
